TPU v7x, 32 devices: a whole 2x2x4 slice. The times are simulated.
32 devices in a mesh: tm: 2 (over x), space: 16 (over z, y, core).
Axes of the slice: x: 2, y: 2, z: 4, core: 2. Of those that a mesh axis runs over, the one named last changes fastest.
Arguments:
- increment: float32 [4, 5, 48, 128, 128], P('tm', None, None, 'space'), may hold values from -6 to 6
- multiplier: float32 [4, 5, 48, 128, 128], P('tm', None, None, 'space'), may hold values from -20 to 20
- sensor_multiplier: float32 [4, 2048], P('tm'), may hold values from -6 to 6
- misfit: float32 [4, 5, 48, 128, 128], P('tm', None, None, 'space'), may hold values from -20 to 20
- innovation: float32 [4, 2048], P('tm'), may hold values from -6 to 6
- model_error: float32 [5, 48], replicated, may hold values from 0.2 to 1
- sensor_error: float32 [4, 2048], P('tm'), may hold values from 0.3 to 1.5
- trajectory: bfloat16 [4, 2, 2, 48, 128, 128], P('tm', None, None, None, 'space'), may hold values from 0 to 1
- land_sea: int32 [128, 128], P('space'), may hold values 0 or 1
- sensor_cells: int32 [4, 2048], P('tm'), may hold values from 0 to 1572863
Outputs:
- increment_next: float32 [4, 5, 48, 128, 128], P('tm', None, None, 'space')
- multiplier_next: float32 [4, 5, 48, 128, 128], P('tm', None, None, 'space')
- sensor_next: float32 [4, 2048], P('tm')
Inputs may be any that keep to these rules, and one draw needn't show every extreme that they name: `sensor_cells`: the flat index ((f * 48 + l) * 128 + x) * 128 + y of the observed cell at field f (0 temperature, 1 salinity), level l, column x, row y; an index may repeat.
All inputs are finite; a program needn't handle non-finite values. No bound on the sum of `land_sea` on one device may be relied on, other than what follows from the above.
Results may differ from a plain program's by a relative error of at most 0.0017.
Values may be sent and summed in bfloat16 or wider, within the bound.
No kernel may reach another device: no remote copies, remote signals or barrier semaphores. Data moves between devices by JAX's collectives and lax.ppermute only.
A program may use at most 64 MiB of HBM per device.

v0:
```python
import jax
import jax.numpy as jnp
from jax import lax
from jax.sharding import PartitionSpec as P

thermal_lin = 0.2
thermal_quad = 0.02
haline_lin = 0.8
cabbeling = 0.01
gravity = 1.0
time_stride = 0.3
mixing = 0.15
coriolis = 0.5
relaxation = 0.5
epsilon = 1e-06


def extended(shard, sides, width):
    for axis, dim in sides:
        peers, length = (lax.axis_size(axis), shard.shape[dim])
        up = [(i, (i + 1) % peers) for i in range(peers)]
        down = [(j, i) for i, j in up]
        last = lax.slice_in_dim(shard, length - width, length, axis=dim)
        first = lax.slice_in_dim(shard, 0, width, axis=dim)
        before = lax.ppermute(last, axis, up)
        after = lax.ppermute(first, axis, down)
        shard = jnp.concatenate([before, shard, after], axis=dim)
    return shard


def shifted(shard, axis, by):
    peers = lax.axis_size(axis)
    pairs = [(i, i + by) for i in range(peers) if 0 <= i + by < peers]
    return lax.ppermute(shard, axis, pairs)


def column_pad(values):
    return jnp.pad(values, ((0, 0), (0, 0), (1, 1)))


def tendency(padded, history, landmask):
    temper = 30.0 * history[0] - 10.0
    saline = 8.0 * history[1] - 5.0
    dens_temper = -thermal_lin - thermal_quad * temper + cabbeling * saline
    dens_saline = haline_lin + cabbeling * temper
    density = dens_temper * padded[0] + dens_saline * padded[1]
    pressure = padded[4] + gravity * density
    latitude = padded.shape[3]
    rotation = (
        coriolis
        * (jnp.arange(latitude, dtype=jnp.float32) - 0.5 * (latitude - 1))
        / (0.5 * latitude)
    )

    def middle(f):
        return f[:, 1:-1]

    def zonal_slope(f):
        return 0.5 * (f[:, 2:] - f[:, :-2])

    def meridional_slope(f):
        g = column_pad(middle(f))
        return 0.5 * (g[..., 2:] - g[..., :-2])

    def laplacian(f):
        g = column_pad(middle(f))
        return f[:, 2:] + f[:, :-2] + g[..., 2:] + g[..., :-2] - 4.0 * middle(f)

    heat_next = middle(padded[0]) + mixing * laplacian(padded[0])
    salt_next = middle(padded[1]) + mixing * laplacian(padded[1])
    east_next = middle(padded[2]) + time_stride * (
        rotation * middle(padded[3]) - zonal_slope(pressure)
    )
    north_next = middle(padded[3]) + time_stride * (
        -rotation * middle(padded[2]) - meridional_slope(pressure)
    )
    surface_next = (
        middle(padded[4])
        - time_stride * (zonal_slope(padded[2]) + meridional_slope(padded[3]))
        + mixing * laplacian(padded[4])
    )
    return jnp.stack([heat_next, salt_next, east_next, north_next, surface_next]) * landmask


def tangent_substep(fields, history, landmask):
    padded = extended(fields, (("space", 2),), 1)
    return tendency(padded, history, landmask)


def adjoint_substep(upstream, history, landmask):
    blank = jnp.zeros(
        upstream.shape[:2] + (upstream.shape[2] + 2,) + upstream.shape[3:], jnp.float32
    )
    _, pull = jax.vjp(lambda v: tendency(v, history, landmask), blank)
    spread = pull(upstream)[0]
    rims = jnp.concatenate([spread[:, :, :1], spread[:, :, -1:]], axis=2)
    beyond = extended(rims.astype(jnp.bfloat16), (("space", 2),), 1).astype(rims.dtype)
    inner = spread[:, :, 1:-1]
    inner = inner.at[:, :, 0].add(beyond[:, :, 0])
    inner = inner.at[:, :, -1].add(beyond[:, :, 3])
    return inner


def on_device(
    increment,
    multiplier,
    sensor_multiplier,
    misfit,
    innovation,
    model_error,
    sensor_error,
    trajectory,
    land_sea,
    sensor_cells,
):
    subcount = increment.shape[0]
    substeps = trajectory.shape[1]
    levels = increment.shape[2]
    width = increment.shape[3]
    latitude = increment.shape[4]
    landmask = land_sea.astype(jnp.float32)
    forward = []
    history = extended(trajectory, (("space", 4),), 1).astype(jnp.float32)
    for k in range(subcount):
        fields = increment[k]
        for j in range(substeps):
            fields = tangent_substep(fields, history[k, j], landmask)
        forward.append(fields)
    damping = model_error[:, :, None, None]
    partial_value = multiplier[0] + relaxation * (
        misfit[0] - damping * multiplier[0] - increment[0]
    )
    received = shifted(partial_value, "tm", -1)
    incoming = shifted(forward[-1].astype(jnp.bfloat16), "tm", 1).astype(jnp.float32)
    previous = jnp.stack([incoming] + forward[:-1])
    model_residual = misfit - damping[None] * multiplier - (increment - previous)
    multiplier_next = multiplier + relaxation * model_residual
    columns = width * lax.axis_size("space")
    plane = columns * latitude
    offset = lax.axis_index("space") * width
    field_level = sensor_cells // plane
    remainder = sensor_cells % plane
    column_index = remainder // latitude
    row_index = remainder % latitude
    owned = (column_index >= offset) & (column_index < offset + width)
    local_index = jnp.where(
        owned, (field_level * width + (column_index - offset)) * latitude + row_index, 0
    )
    flattened = increment[:, :2].reshape(subcount, 2 * levels * width * latitude)
    local_values = jnp.where(owned, jnp.take_along_axis(flattened, local_index, axis=1), 0.0)
    observed = lax.psum(local_values, "space")
    sensor_residual = innovation - sensor_error * sensor_multiplier - observed
    sensor_next = sensor_multiplier + relaxation * sensor_residual
    misfit_local = jnp.sum(model_residual * model_residual) + jnp.sum(
        jnp.where(owned, sensor_residual * sensor_residual, 0.0)
    )
    misfit_square = lax.psum(misfit_local, ("tm", "space"))
    keeper = jnp.where(lax.axis_index("tm") < lax.axis_size("tm") - 1, 1.0, 0.0).astype(jnp.float32)
    carried = keeper * (received + relaxation * forward[-1])
    following = [multiplier_next[1]] + [carried]
    returned = []
    for k in range(subcount):
        upstream = following[k]
        for j in reversed(range(substeps)):
            upstream = adjoint_substep(upstream, history[k, j], landmask)
        returned.append(upstream)
    returned = jnp.stack(returned)
    subwindow_rows = jnp.arange(subcount, dtype=jnp.int32)[:, None]
    spread = (
        jnp.zeros_like(flattened)
        .at[subwindow_rows, local_index]
        .add(jnp.where(owned, sensor_next, 0.0))
    )
    spread = spread.reshape(subcount, 2, levels, width, latitude)
    sensor_part = jnp.concatenate(
        [spread, jnp.zeros((subcount, 3, levels, width, latitude), jnp.float32)], axis=1
    )
    gradient = multiplier_next - returned + sensor_part
    gradient_local = jnp.sum(gradient * gradient)
    gradient_square = lax.psum(gradient_local, ("tm", "space"))
    stride = misfit_square / (gradient_square + epsilon)
    return (increment - stride * gradient, multiplier_next, sensor_next)


def solution(mesh):
    placed = (
        P("tm", None, None, "space", None),
        P("tm", None, None, "space", None),
        P("tm", None),
        P("tm", None, None, "space", None),
        P("tm", None),
        P(),
        P("tm", None),
        P("tm", None, None, None, "space", None),
        P("space", None),
        P("tm", None),
    )
    return jax.shard_map(
        on_device,
        mesh=mesh,
        in_specs=placed,
        out_specs=(
            P("tm", None, None, "space", None),
            P("tm", None, None, "space", None),
            P("tm", None),
        ),
        check_vma=False,
    )
```

profile of v0, /device:TPU:0, one launch (start us, length us, event | category | flops | bytes accessed | tf_op | source)
XLA Modules:
  0.0 274.8 jit_solution(7733373252977561746)
XLA Ops:
  0.6 1.9 copy.36
  5.0 5.0 %collective-permute-start.1 = (f32[5,48,1,128]{3,1,2,0:T(8,128)}, f32[5,48,1,128]{3,1,2,0:T(8,128)}, u32[]{:S(2)}, u32[]{:S(2)}) collective-permute-start(f32[5,48,1,128]{3,1,2,0:T(8,128)} %get-tuple-element.232), channel_id=1, source_target_pairs={{1,0},{2,1},{3,2},{4,3},{5,4},{6,5},{7,6},{8,7},{9,8},{10,9},{11,1... | collective-permute-start | bytes 368648 | tf_op jit(solution)/shard_map/ppermute | solution.py:26
  11.0 4.5 %collective-permute-start.3 = (bf16[2,2,2,48,1,128]{5,3,4,2,1,0:T(8,128)(2,1)S(1)}, bf16[2,2,2,48,1,128]{5,3,4,2,1,0:T(8,128)(2,1)}, u32[]{:S(2)}, u32[]{:S(2)}) collective-permute-start(bf16[2,2,2,48,1,128]{5,3,4,2,1,0:T(8,128)(2,1)S(1)} %get-tuple-element.238), channel_id=1, source_target_pairs={{1,0},{2,1},{3,2},{4,3},{5,4},{6,5},{7,6},{8,7},{9,8},{10,9},{11,1... | collective-permute-start | bytes 294920 | tf_op jit(solution)/shard_map/ppermute | solution.py:26
  16.4 34.9 %gather_fusion = f32[4096]{0:T(1024)S(1)} fusion(f32[2,98304]{1,0:T(2,128)S(1)} %bitcast.526, s32[4096]{0:T(1024)S(1)} %bitcast.527), kind=kCustom, calls=%fused_computation | custom fusion | bytes 65536 | tf_op jit(solution)/shard_map/jit(take_along_axis)/gather | solution.py:150
  51.4 58.2 %psum.21 = f32[2,2048]{1,0:T(2,128)S(1)} all-reduce(f32[2,2048]{1,0:T(2,128)S(1)} %fusion.203), channel_id=1, replica_groups=mesh['tm'=2,'space'=16] {'space'}, use_global_device_ids=true, to_apply=%region_1.2 | all-reduce | flops 4096 | bytes 32768 | tf_op jit(solution)/shard_map/psum | solution.py:151
  109.6 1.3 select_bitcast_fusion.1
  111.2 28.0 %scatter_custom_fusion = f32[196608]{0:T(1024)} fusion(s32[4096]{0:T(1024)S(1)} %bitcast.541, f32[4096]{0:T(1024)S(1)} %bitcast.540, f32[]{:T(128)} %constant.307.clone.1), kind=kCustom, calls=%fused_computation.80 | custom fusion | flops 4096 | bytes 786436
  146.0 4.4 %collective-permute-start.5 = (f32[5,48,1,128]{3,1,2,0:T(8,128)S(1)}, f32[5,48,1,128]{3,1,2,0:T(8,128)S(1)}, u32[]{:S(2)}, u32[]{:S(2)}) collective-permute-start(f32[5,48,1,128]{3,1,2,0:T(8,128)S(1)} %get-tuple-element.230), channel_id=1, source_target_pairs={{1,0},{2,1},{3,2},{4,3},{5,4},{6,5},{7,6},{8,7},{9,8},{10,9},{11,1... | collective-permute-start | bytes 368648 | tf_op jit(solution)/shard_map/ppermute | solution.py:26
  151.0 2.1 collective-permute-done.4
  154.1 3.7 %collective-permute-done.9 = f32[5,48,1,128]{3,1,2,0:T(8,128)S(1)} collective-permute-done((f32[5,48,1,128]{3,1,2,0:T(8,128)S(1)}, f32[5,48,1,128]{3,1,2,0:T(8,128)S(1)}, u32[]{:S(2)}, u32[]{:S(2)}) %collective-permute-start.9) | collective-permute-done | bytes 122912 | tf_op jit(solution)/shard_map/ppermute | solution.py:25
  159.3 4.0 %collective-permute-start.6 = (bf16[5,48,8,128]{3,1,2,0:T(8,128)(2,1)S(1)}, bf16[5,48,8,128]{3,1,2,0:T(8,128)(2,1)S(1)}, u32[]{:S(2)}, u32[]{:S(2)}) collective-permute-start(bf16[5,48,8,128]{3,1,2,0:T(8,128)(2,1)S(1)} %multiply_convert_fusion), channel_id=1, source_target_pairs={{0,16},{1,17},{2,18},{3,19},{4,20},{5,21},{6,22},{7,23},{8,24},{9,... | collective-permute-start | bytes 1474568 | tf_op jit(solution)/shard_map/ppermute | solution.py:34
  164.4 5.0 %collective-permute-done.6 = bf16[5,48,8,128]{3,1,2,0:T(8,128)(2,1)S(1)} collective-permute-done((bf16[5,48,8,128]{3,1,2,0:T(8,128)(2,1)S(1)}, bf16[5,48,8,128]{3,1,2,0:T(8,128)(2,1)S(1)}, u32[]{:S(2)}, u32[]{:S(2)}) %collective-permute-start.6) | collective-permute-done | bytes 491552 | tf_op jit(solution)/shard_map/ppermute | solution.py:34
  169.6 1.6 broadcast_multiply_fusion
  173.7 1.4 copy-done.4
  175.1 1.2 fusion.5
  176.3 1.3 collective-permute-start.15
  179.2 4.4 %collective-permute-start.12 = (bf16[5,48,1,128]{3,1,2,0:T(8,128)(2,1)S(1)}, bf16[5,48,1,128]{3,1,2,0:T(8,128)(2,1)S(1)}, u32[]{:S(2)}, u32[]{:S(2)}) collective-permute-start(bf16[5,48,1,128]{3,1,2,0:T(8,128)(2,1)S(1)} %get-tuple-element.242), channel_id=1, source_target_pairs={{1,0},{2,1},{3,2},{4,3},{5,4},{6,5},{7,6},{8,7},{9,8},{10,9},{11,1... | collective-permute-start | bytes 184328 | tf_op jit(solution)/shard_map/ppermute | solution.py:26
  183.6 1.2 multiply_reduce_fusion.1
  187.1 1.6 fusion.200
  188.7 1.6 fusion.199
  190.3 6.4 %collective-permute-done.15 = f32[5,48,8,128]{3,1,2,0:T(8,128)} collective-permute-done((f32[5,48,8,128]{3,1,2,0:T(8,128)}, f32[5,48,8,128]{3,1,2,0:T(8,128)}, u32[]{:S(2)}, u32[]{:S(2)}) %collective-permute-start.15) | collective-permute-done | bytes 983072 | tf_op jit(solution)/shard_map/ppermute | solution.py:34
  196.6 1.7 broadcast_multiply_fusion.3
  202.0 5.4 %collective-permute-start.17 = (bf16[5,48,1,128]{3,1,2,0:T(8,128)(2,1)S(1)}, bf16[5,48,1,128]{3,1,2,0:T(8,128)(2,1)S(1)}, u32[]{:S(2)}, u32[]{:S(2)}) collective-permute-start(bf16[5,48,1,128]{3,1,2,0:T(8,128)(2,1)S(1)} %get-tuple-element.246), channel_id=1, source_target_pairs={{1,0},{2,1},{3,2},{4,3},{5,4},{6,5},{7,6},{8,7},{9,8},{10,9},{11,1... | collective-permute-start | bytes 184328 | tf_op jit(solution)/shard_map/ppermute | solution.py:26
  208.0 4.4 %collective-permute-start.14 = (bf16[5,48,1,128]{3,1,2,0:T(8,128)(2,1)S(1)}, bf16[5,48,1,128]{3,1,2,0:T(8,128)(2,1)S(1)}, u32[]{:S(2)}, u32[]{:S(2)}) collective-permute-start(bf16[5,48,1,128]{3,1,2,0:T(8,128)(2,1)S(1)} %get-tuple-element.240), channel_id=1, source_target_pairs={{1,0},{2,1},{3,2},{4,3},{5,4},{6,5},{7,6},{8,7},{9,8},{10,9},{11,1... | collective-permute-start | bytes 184328 | tf_op jit(solution)/shard_map/ppermute | solution.py:26
  213.2 1.2 collective-permute-done.13
  216.3 4.6 %collective-permute-start.19 = (bf16[5,48,1,128]{3,1,0,2:T(8,128)(2,1)S(1)}, bf16[5,48,1,128]{3,1,0,2:T(8,128)(2,1)S(1)}, u32[]{:S(2)}, u32[]{:S(2)}) collective-permute-start(bf16[5,48,1,128]{3,1,0,2:T(8,128)(2,1)S(1)} %get-tuple-element.244), channel_id=1, source_target_pairs={{1,0},{2,1},{3,2},{4,3},{5,4},{6,5},{7,6},{8,7},{9,8},{10,9},{11,1... | collective-permute-start | bytes 184328 | tf_op jit(solution)/shard_map/ppermute | solution.py:26
  221.2 1.4 collective-permute-done.18
  222.7 1.3 copy.43
  224.0 4.4 %scatter-add.54 = f32[1,5,48,8,128]{4,3,2,1,0:T(8,128)} dynamic-update-slice(f32[1,5,48,8,128]{4,3,2,1,0:T(8,128)} %copy.43, f32[1,5,48,1,128]{4,3,2,1,0:T(1,128)S(1)} %bitcast.537, s32[]{:T(128)} %constant.322.clone.1, s32[]{:T(128)} %constant.322.clone.1, s32[]{:T(128)} %constant.322.clone.1, s32[]{:T(128)} %constant.327.clone.1, s32[]{:T(128)} %constant.322.clone.1) | dynamic-update-slice | bytes 245764 | tf_op jit(solution)/shard_map/scatter-add | solution.py:100
  228.4 2.6 multiply_reduce_fusion
  231.0 38.9 %all-reduce.221 = (f32[]{:T(128)}, f32[]{:T(128)}) all-reduce(f32[]{:T(128)S(6)} %add.910, f32[]{:T(128)} %multiply_reduce_fusion), channel_id=1, replica_groups=mesh['tm'=2,'space'=16] {'tm','space'}, use_global_device_ids=true, to_apply=%region_3.4 | all-reduce | flops 2 | bytes 16 | tf_op jit(solution)/shard_map/psum | solution.py:157
  271.1 3.6 %multiply_subtract_fusion = f32[2,5,48,8,128]{4,3,2,1,0:T(8,128)} fusion(f32[2,5,48,8,128]{4,3,2,1,0:T(8,128)} %param.26, f32[]{:T(128)S(6)} %div.69, f32[2,2,48,8,128]{4,3,2,1,0:T(8,128)} %bitcast.530, f32[2,5,48,8,128]{4,3,2,1,0:T(8,128)S(1)} %copy-done.1, f32[1,5,48,8,128]{4,3,2,1,0:T(8,128)} %scatter-add.54, f32[1,5,48,8,128]{4,3,2,1,0:T(8,128)S(1)} %copy.44), kind=kLoop, calls=%fused_computation.7 | loop fusion | flops 2457600 | bytes 8650756 | tf_op jit(solution)/shard_map/sub | solution.py:182
  (251 shorter events, 26.8 us)
Async XLA Ops:
  3.8 7.0 %copy-start.6 = (f32[5,48,8,128]{3,1,2,0:T(8,128)}, f32[5,48,8,128]{3,1,2,0:T(8,128)S(1)}, u32[]{:S(2)}) copy-start(f32[5,48,8,128]{3,1,2,0:T(8,128)S(1)} %get-tuple-element.132) | copy-start | bytes 2949124
  3.8 7.1 %copy-start.8 = (f32[5,48,8,128]{3,1,2,0:T(8,128)}, f32[5,48,8,128]{3,1,2,0:T(8,128)S(1)}, u32[]{:S(2)}) copy-start(f32[5,48,8,128]{3,1,2,0:T(8,128)S(1)} %get-tuple-element.131) | copy-start | bytes 2949124
  3.8 6.9 %copy-start.12 = (bf16[2,2,2,48,8,128]{5,4,3,2,1,0:T(8,128)(2,1)S(1)}, bf16[2,2,2,48,8,128]{5,4,3,2,1,0:T(8,128)(2,1)}, u32[]{:S(2)}) copy-start(bf16[2,2,2,48,8,128]{5,4,3,2,1,0:T(8,128)(2,1)} %param.33) | copy-start | bytes 2359300
  4.5 136.4 %collective-permute-start = (f32[5,48,1,128]{3,1,2,0:T(8,128)}, f32[5,48,1,128]{3,1,2,0:T(8,128)}, u32[]{:S(2)}, u32[]{:S(2)}) collective-permute-start(f32[5,48,1,128]{3,1,2,0:T(8,128)} %get-tuple-element.231), channel_id=1, source_target_pairs={{0,1},{1,2},{2,3},{3,4},{4,5},{5,6},{6,7},{7,8},{8,9},{9,10},{10,1... | collective-permute-start | bytes 368648 | tf_op jit(solution)/shard_map/ppermute | solution.py:25
  5.0 136.0 %collective-permute-start.1 = (f32[5,48,1,128]{3,1,2,0:T(8,128)}, f32[5,48,1,128]{3,1,2,0:T(8,128)}, u32[]{:S(2)}, u32[]{:S(2)}) collective-permute-start(f32[5,48,1,128]{3,1,2,0:T(8,128)} %get-tuple-element.232), channel_id=1, source_target_pairs={{1,0},{2,1},{3,2},{4,3},{5,4},{6,5},{7,6},{8,7},{9,8},{10,9},{11,1... | collective-permute-start | bytes 368648 | tf_op jit(solution)/shard_map/ppermute | solution.py:26
  10.7 131.4 %collective-permute-start.7 = (f32[5,48,1,128]{3,1,2,0:T(8,128)}, f32[5,48,1,128]{3,1,2,0:T(8,128)}, u32[]{:S(2)}, u32[]{:S(2)}) collective-permute-start(f32[5,48,1,128]{3,1,2,0:T(8,128)} %get-tuple-element.235), channel_id=1, source_target_pairs={{0,1},{1,2},{2,3},{3,4},{4,5},{5,6},{6,7},{7,8},{8,9},{9,10},{10,1... | collective-permute-start | bytes 368648 | tf_op jit(solution)/shard_map/ppermute | solution.py:25
  10.9 128.3 %collective-permute-start.2 = (bf16[2,2,2,48,1,128]{5,3,4,2,1,0:T(8,128)(2,1)S(1)}, bf16[2,2,2,48,1,128]{5,3,4,2,1,0:T(8,128)(2,1)S(1)}, u32[]{:S(2)}, u32[]{:S(2)}) collective-permute-start(bf16[2,2,2,48,1,128]{5,3,4,2,1,0:T(8,128)(2,1)S(1)} %get-tuple-element.237), channel_id=1, source_target_pairs={{0,1},{1,2},{2,3},{3,4},{4,5},{5,6},{6,7},{7,8},{8,9},{9,10},{10,1... | collective-permute-start | bytes 294920 | tf_op jit(solution)/shard_map/ppermute | solution.py:25
  11.0 128.9 %collective-permute-start.3 = (bf16[2,2,2,48,1,128]{5,3,4,2,1,0:T(8,128)(2,1)S(1)}, bf16[2,2,2,48,1,128]{5,3,4,2,1,0:T(8,128)(2,1)}, u32[]{:S(2)}, u32[]{:S(2)}) collective-permute-start(bf16[2,2,2,48,1,128]{5,3,4,2,1,0:T(8,128)(2,1)S(1)} %get-tuple-element.238), channel_id=1, source_target_pairs={{1,0},{2,1},{3,2},{4,3},{5,4},{6,5},{7,6},{8,7},{9,8},{10,9},{11,1... | collective-permute-start | bytes 294920 | tf_op jit(solution)/shard_map/ppermute | solution.py:26
  16.3 93.3 %copy-start.15 = (f32[2,2048]{1,0:T(2,128)S(1)}, f32[2,2048]{1,0:T(2,128)}, u32[]{:S(2)}) copy-start(f32[2,2048]{1,0:T(2,128)} %param.28) | copy-start | bytes 49156
  16.4 93.2 %copy-start.16 = (f32[2,2048]{1,0:T(2,128)S(1)}, f32[2,2048]{1,0:T(2,128)}, u32[]{:S(2)}) copy-start(f32[2,2048]{1,0:T(2,128)} %param.30) | copy-start | bytes 49156
  16.4 93.2 %copy-start.17 = (f32[2,2048]{1,0:T(2,128)S(1)}, f32[2,2048]{1,0:T(2,128)}, u32[]{:S(2)}) copy-start(f32[2,2048]{1,0:T(2,128)} %param.32) | copy-start | bytes 49156
  16.4 94.5 %copy-start.20 = (s32[2]{0:T(128)S(1)}, s32[2]{0:T(128)}, u32[]{:S(2)}) copy-start(s32[2]{0:T(128)} %constant.788) | copy-start | bytes 28
  16.4 94.6 %copy-start.21 = (s32[2]{0:T(128)S(1)}, s32[2]{0:T(128)}, u32[]{:S(2)}) copy-start(s32[2]{0:T(128)} %constant.791) | copy-start | bytes 28
  139.2 2.9 %collective-permute-start.8 = (f32[5,48,1,128]{3,1,2,0:T(8,128)}, f32[5,48,1,128]{3,1,2,0:T(8,128)S(1)}, u32[]{:S(2)}, u32[]{:S(2)}) collective-permute-start(f32[5,48,1,128]{3,1,2,0:T(8,128)} %get-tuple-element.236), channel_id=1, source_target_pairs={{1,0},{2,1},{3,2},{4,3},{5,4},{6,5},{7,6},{8,7},{9,8},{10,9},{11,1... | collective-permute-start | bytes 368648 | tf_op jit(solution)/shard_map/ppermute | solution.py:26
  145.9 7.2 %collective-permute-start.4 = (f32[5,48,1,128]{3,1,2,0:T(8,128)S(1)}, f32[5,48,1,128]{3,1,2,0:T(8,128)S(1)}, u32[]{:S(2)}, u32[]{:S(2)}) collective-permute-start(f32[5,48,1,128]{3,1,2,0:T(8,128)S(1)} %get-tuple-element.229), channel_id=1, source_target_pairs={{0,1},{1,2},{2,3},{3,4},{4,5},{5,6},{6,7},{7,8},{8,9},{9,10},{10,1... | collective-permute-start | bytes 368648 | tf_op jit(solution)/shard_map/ppermute | solution.py:25
  146.0 7.1 %collective-permute-start.5 = (f32[5,48,1,128]{3,1,2,0:T(8,128)S(1)}, f32[5,48,1,128]{3,1,2,0:T(8,128)S(1)}, u32[]{:S(2)}, u32[]{:S(2)}) collective-permute-start(f32[5,48,1,128]{3,1,2,0:T(8,128)S(1)} %get-tuple-element.230), channel_id=1, source_target_pairs={{1,0},{2,1},{3,2},{4,3},{5,4},{6,5},{7,6},{8,7},{9,8},{10,9},{11,1... | collective-permute-start | bytes 368648 | tf_op jit(solution)/shard_map/ppermute | solution.py:26
  150.4 3.7 %collective-permute-start.10 = (f32[5,48,1,128]{3,1,2,0:T(8,128)S(1)}, f32[5,48,1,128]{3,1,2,0:T(8,128)S(1)}, u32[]{:S(2)}, u32[]{:S(2)}) collective-permute-start(f32[5,48,1,128]{3,1,2,0:T(8,128)S(1)} %get-tuple-element.234), channel_id=1, source_target_pairs={{1,0},{2,1},{3,2},{4,3},{5,4},{6,5},{7,6},{8,7},{9,8},{10,9},{11,1... | collective-permute-start | bytes 368648 | tf_op jit(solution)/shard_map/ppermute | solution.py:26
  150.8 7.0 %collective-permute-start.9 = (f32[5,48,1,128]{3,1,2,0:T(8,128)S(1)}, f32[5,48,1,128]{3,1,2,0:T(8,128)S(1)}, u32[]{:S(2)}, u32[]{:S(2)}) collective-permute-start(f32[5,48,1,128]{3,1,2,0:T(8,128)S(1)} %get-tuple-element.233), channel_id=1, source_target_pairs={{0,1},{1,2},{2,3},{3,4},{4,5},{5,6},{6,7},{7,8},{8,9},{9,10},{10,1... | collective-permute-start | bytes 368648 | tf_op jit(solution)/shard_map/ppermute | solution.py:25
  159.3 10.1 %collective-permute-start.6 = (bf16[5,48,8,128]{3,1,2,0:T(8,128)(2,1)S(1)}, bf16[5,48,8,128]{3,1,2,0:T(8,128)(2,1)S(1)}, u32[]{:S(2)}, u32[]{:S(2)}) collective-permute-start(bf16[5,48,8,128]{3,1,2,0:T(8,128)(2,1)S(1)} %multiply_convert_fusion), channel_id=1, source_target_pairs={{0,16},{1,17},{2,18},{3,19},{4,20},{5,21},{6,22},{7,23},{8,24},{9,... | collective-permute-start | bytes 1474568 | tf_op jit(solution)/shard_map/ppermute | solution.py:34
  163.8 5.7 %copy-start.11 = (f32[2,5,48,8,128]{4,3,2,1,0:T(8,128)S(1)}, f32[2,5,48,8,128]{4,3,2,1,0:T(8,128)}, u32[]{:S(2)}) copy-start(f32[2,5,48,8,128]{4,3,2,1,0:T(8,128)} %param.29) | copy-start | bytes 5898244
  164.0 5.5 %copy-start.5 = (f32[2,5,48,8,128]{4,3,2,1,0:T(8,128)S(1)}, f32[2,5,48,8,128]{4,3,2,1,0:T(8,128)}, u32[]{:S(2)}) copy-start(f32[2,5,48,8,128]{4,3,2,1,0:T(8,128)} %param.27) | copy-start | bytes 5898244
  176.3 20.3 %collective-permute-start.15 = (f32[5,48,8,128]{3,1,2,0:T(8,128)}, f32[5,48,8,128]{3,1,2,0:T(8,128)}, u32[]{:S(2)}, u32[]{:S(2)}) collective-permute-start(f32[5,48,8,128]{3,1,2,0:T(8,128)} %fusion.5), channel_id=1, source_target_pairs={{16,0},{17,1},{18,2},{19,3},{20,4},{21,5},{22,6},{23,7},{24,8},{25... | collective-permute-start | bytes 2949128 | tf_op jit(solution)/shard_map/ppermute | solution.py:34
  179.1 6.7 %copy-start.10 = (f32[5,48,10,128]{3,1,2,0:T(8,128)}, f32[5,48,10,128]{3,1,2,0:T(8,128)S(1)}, u32[]{:S(2)}) copy-start(f32[5,48,10,128]{3,1,2,0:T(8,128)S(1)} %get-tuple-element.106) | copy-start | bytes 3686404
  179.1 8.0 %collective-permute-start.11 = (bf16[5,48,1,128]{3,1,2,0:T(8,128)(2,1)S(1)}, bf16[5,48,1,128]{3,1,2,0:T(8,128)(2,1)S(1)}, u32[]{:S(2)}, u32[]{:S(2)}) collective-permute-start(bf16[5,48,1,128]{3,1,2,0:T(8,128)(2,1)S(1)} %get-tuple-element.241), channel_id=1, source_target_pairs={{0,1},{1,2},{2,3},{3,4},{4,5},{5,6},{6,7},{7,8},{8,9},{9,10},{10,1... | collective-permute-start | bytes 184328 | tf_op jit(solution)/shard_map/ppermute | solution.py:25
  179.2 8.0 %collective-permute-start.12 = (bf16[5,48,1,128]{3,1,2,0:T(8,128)(2,1)S(1)}, bf16[5,48,1,128]{3,1,2,0:T(8,128)(2,1)S(1)}, u32[]{:S(2)}, u32[]{:S(2)}) collective-permute-start(bf16[5,48,1,128]{3,1,2,0:T(8,128)(2,1)S(1)} %get-tuple-element.242), channel_id=1, source_target_pairs={{1,0},{2,1},{3,2},{4,3},{5,4},{6,5},{7,6},{8,7},{9,8},{10,9},{11,1... | collective-permute-start | bytes 184328 | tf_op jit(solution)/shard_map/ppermute | solution.py:26
  202.0 10.5 %collective-permute-start.16 = (bf16[5,48,1,128]{3,1,2,0:T(8,128)(2,1)S(1)}, bf16[5,48,1,128]{3,1,2,0:T(8,128)(2,1)S(1)}, u32[]{:S(2)}, u32[]{:S(2)}) collective-permute-start(bf16[5,48,1,128]{3,1,2,0:T(8,128)(2,1)S(1)} %get-tuple-element.245), channel_id=1, source_target_pairs={{0,1},{1,2},{2,3},{3,4},{4,5},{5,6},{6,7},{7,8},{8,9},{9,10},{10,1... | collective-permute-start | bytes 184328 | tf_op jit(solution)/shard_map/ppermute | solution.py:25
  202.0 10.5 %collective-permute-start.17 = (bf16[5,48,1,128]{3,1,2,0:T(8,128)(2,1)S(1)}, bf16[5,48,1,128]{3,1,2,0:T(8,128)(2,1)S(1)}, u32[]{:S(2)}, u32[]{:S(2)}) collective-permute-start(bf16[5,48,1,128]{3,1,2,0:T(8,128)(2,1)S(1)} %get-tuple-element.246), channel_id=1, source_target_pairs={{1,0},{2,1},{3,2},{4,3},{5,4},{6,5},{7,6},{8,7},{9,8},{10,9},{11,1... | collective-permute-start | bytes 184328 | tf_op jit(solution)/shard_map/ppermute | solution.py:26
  208.0 6.4 %collective-permute-start.13 = (bf16[5,48,1,128]{3,1,2,0:T(8,128)(2,1)S(1)}, bf16[5,48,1,128]{3,1,2,0:T(8,128)(2,1)S(1)}, u32[]{:S(2)}, u32[]{:S(2)}) collective-permute-start(bf16[5,48,1,128]{3,1,2,0:T(8,128)(2,1)S(1)} %get-tuple-element.239), channel_id=1, source_target_pairs={{0,1},{1,2},{2,3},{3,4},{4,5},{5,6},{6,7},{7,8},{8,9},{9,10},{10,1... | collective-permute-start | bytes 184328 | tf_op jit(solution)/shard_map/ppermute | solution.py:25
  208.0 6.3 %collective-permute-start.14 = (bf16[5,48,1,128]{3,1,2,0:T(8,128)(2,1)S(1)}, bf16[5,48,1,128]{3,1,2,0:T(8,128)(2,1)S(1)}, u32[]{:S(2)}, u32[]{:S(2)}) collective-permute-start(bf16[5,48,1,128]{3,1,2,0:T(8,128)(2,1)S(1)} %get-tuple-element.240), channel_id=1, source_target_pairs={{1,0},{2,1},{3,2},{4,3},{5,4},{6,5},{7,6},{8,7},{9,8},{10,9},{11,1... | collective-permute-start | bytes 184328 | tf_op jit(solution)/shard_map/ppermute | solution.py:26
  216.0 6.7 %collective-permute-start.18 = (bf16[5,48,1,128]{3,1,0,2:T(8,128)(2,1)S(1)}, bf16[5,48,1,128]{3,1,0,2:T(8,128)(2,1)S(1)}, u32[]{:S(2)}, u32[]{:S(2)}) collective-permute-start(bf16[5,48,1,128]{3,1,0,2:T(8,128)(2,1)S(1)} %get-tuple-element.243), channel_id=1, source_target_pairs={{0,1},{1,2},{2,3},{3,4},{4,5},{5,6},{6,7},{7,8},{8,9},{9,10},{10,1... | collective-permute-start | bytes 184328 | tf_op jit(solution)/shard_map/ppermute | solution.py:25
  216.3 6.5 %collective-permute-start.19 = (bf16[5,48,1,128]{3,1,0,2:T(8,128)(2,1)S(1)}, bf16[5,48,1,128]{3,1,0,2:T(8,128)(2,1)S(1)}, u32[]{:S(2)}, u32[]{:S(2)}) collective-permute-start(bf16[5,48,1,128]{3,1,0,2:T(8,128)(2,1)S(1)} %get-tuple-element.244), channel_id=1, source_target_pairs={{1,0},{2,1},{3,2},{4,3},{5,4},{6,5},{7,6},{8,7},{9,8},{10,9},{11,1... | collective-permute-start | bytes 184328 | tf_op jit(solution)/shard_map/ppermute | solution.py:26
  222.7 5.7 %copy-start.1 = (f32[2,5,48,8,128]{4,3,2,1,0:T(8,128)S(1)}, f32[2,5,48,8,128]{4,3,2,1,0:T(8,128)}, u32[]{:S(2)}) copy-start(f32[2,5,48,8,128]{4,3,2,1,0:T(8,128)} %copy-done) | copy-start | bytes 5898244
  (11 other events, 32.3 us)
where the time goes:
time: 275 us
  blocking collectives  97.1 us (35%)
  other arithmetic  60 us (22%)
  local copies, waits for them, and re-layouts  52.4 us (19%)
  starting transfers between devices  39.7 us (14%)
  waiting for transfers between devices  20.6 us (7%)
  between operations  4.83 us (2%)
    psum x1, blocking collectives, on_device(): observed = lax.psum(local_values, 'space')  58.2 us
    psum x1, blocking collectives, on_device(): misfit_square = lax.psum(misfit_local, ('tm', 'space'))  38.9 us
    gather x3, local copies, waits for them, and re-layouts, on_device(): jnp.take_along_axis(flattened, local_index, axis=1)  34.9 us
    ppermute x9, starting transfers between devices, extended(): after = lax.ppermute(first, axis, down)  33.2 us
    unnamed x20, other arithmetic  31.9 us
    ppermute x2, waiting for transfers between devices, shifted(): return lax.ppermute(shard, axis, pairs)  11.4 us
    ppermute x9, waiting for transfers between devices, extended(): before = lax.ppermute(last, axis, up)  8.36 us
    unnamed x51, local copies, waits for them, and re-layouts  7.02 us
  transfers between devices with their start and end apart: 20, of which 7 were waited for; matrix products, arithmetic and copies ran while one was open for 28% of the time, Pallas kernels for 0%

commit v1 on v0

v1 whole, which is shorter than its diff:
```python
import jax
import jax.numpy as jnp
from jax import lax
from jax.experimental import pallas as pl
from jax.experimental.pallas import tpu as pltpu
from jax.sharding import PartitionSpec as P

thermal_lin = 0.2
thermal_quad = 0.02
haline_lin = 0.8
cabbeling = 0.01
gravity = 1.0
time_stride = 0.3
mixing = 0.15
coriolis = 0.5
relaxation = 0.5
epsilon = 1e-06

kt0 = -thermal_lin + 10.0 * thermal_quad - 5.0 * cabbeling
kt1 = -30.0 * thermal_quad
kt2 = 8.0 * cabbeling
ks0 = haline_lin - 10.0 * cabbeling
ks1 = 30.0 * cabbeling
half = 0.5 * time_stride

LB = 16
TE, SA, U, V, PR = range(5)
F32 = jnp.float32
BF16 = jnp.bfloat16

NEAR = {TE: 0, SA: 1, U: 2, V: 3, PR: 4}
FAR = {TE: 5, SA: 6, U: 7, PR: 8}
BACK = 9
QN, QF, H0, H1 = 9, 10, 11, 12
AHEAD = 13


def rows_of(ref, lead, col, width):
    return ref[lead + (pl.ds(col, LB, stride=width), slice(None))]


def dens(h0, h1):
    return kt0 + kt1 * h0 + kt2 * h1, ks0 + ks1 * h0


class Rows:
    def __init__(self, latitude):
        lane = lax.broadcasted_iota(jnp.int32, (LB, latitude), 1)
        self.n = latitude
        self.first = lane == 0
        self.last = lane == latitude - 1
        row = lane.astype(F32)
        self.rot = (time_stride * coriolis / (0.5 * latitude)) * (row - 0.5 * (latitude - 1))

    def up(self, f):
        return jnp.where(self.last, 0.0, pltpu.roll(f, self.n - 1, 1))

    def down(self, f):
        return jnp.where(self.first, 0.0, pltpu.roll(f, 1, 1))

    def diff(self, f):
        return self.up(f) - self.down(f)

    def both(self, f):
        return self.up(f) + self.down(f)


def pack_kernel(inc_ref, traj_ref, land_ref, up_ref, dn_ref, h_s):
    subs, width = inc_ref.shape[0], land_ref.shape[0]
    for k in range(subs):
        for j in range(2):
            for s in range(2):
                h_s[2 * j + s] = traj_ref[k, j, s].astype(F32)
        for out, near, far in ((up_ref, width - 1, width - 2), (dn_ref, 0, 1)):
            base = AHEAD * k
            for col, planes, q in ((near, NEAR, QN), (far, FAR, QF)):
                vals = {f: rows_of(inc_ref, (k, f), col, width) for f in planes}
                for f, p in planes.items():
                    out[base + p] = vals[f].astype(BF16)
                kt, ks = dens(rows_of(h_s, (0,), col, width), rows_of(h_s, (1,), col, width))
                out[base + q] = (vals[PR] + gravity * (kt * vals[TE] + ks * vals[SA])).astype(BF16)
            out[base + H0] = rows_of(h_s, (2,), near, width).astype(BF16)
            out[base + H1] = rows_of(h_s, (3,), near, width).astype(BF16)
    for out, near in ((up_ref, width - 1), (dn_ref, 0)):
        mask = land_ref[near : near + 1, :].astype(F32)
        out[AHEAD * subs] = jnp.broadcast_to(mask, (LB, mask.shape[1])).astype(BF16)


def partial_kernel(inc_ref, mult_ref, misfit_ref, damp_ref, edge_ref, inner_ref):
    fields, width = inc_ref.shape[1], edge_ref.shape[1] + inner_ref.shape[1]
    for f in range(fields):
        damp = damp_ref[f]
        for c in range(width):
            mult = rows_of(mult_ref, (0, f), c, width)
            base = rows_of(misfit_ref, (0, f), c, width) - damp * mult - rows_of(inc_ref, (0, f), c, width)
            value = (mult + relaxation * base).astype(BF16)
            if 2 <= c < width - 2:
                inner_ref[f, c - 2] = value
            else:
                edge_ref[f, c if c < 2 else c - width + 4] = value


def sensor_kernel(inc_ref, row_ref, lat_ref, mult_ref, innov_ref, err_ref, obs_ref, spread_ref, sum_ref, acc_s):
    subs, rows, latitude = inc_ref.shape[0], 2 * inc_ref.shape[2], inc_ref.shape[3]
    nobs = row_ref.shape[1]
    blk = 512 if nobs % 512 == 0 else nobs
    total = jnp.zeros((1, blk), F32)
    for k in range(subs):
        flat = jnp.concatenate([inc_ref[k, 0], inc_ref[k, 1]], axis=0)
        flat_t = flat.T
        hi = flat_t.astype(BF16)
        lo = (flat_t - hi.astype(F32)).astype(BF16)
        left = jnp.concatenate([hi, lo], axis=0)
        for b in range(nobs // blk):
            span = pl.ds(b * blk, blk)
            row = row_ref[k : k + 1, span]
            lat = lat_ref[k : k + 1, span]
            hot = jnp.where(lax.broadcasted_iota(jnp.int32, (rows, blk), 0) == row, 1.0, 0.0).astype(BF16)
            here = lax.broadcasted_iota(jnp.int32, (latitude, blk), 0) == lat
            both = jnp.dot(left, hot, preferred_element_type=F32)
            seen = jnp.sum(jnp.where(here, both[:latitude] + both[latitude:], 0.0), axis=0, keepdims=True)
            mult = mult_ref[k : k + 1, span]
            resid = innov_ref[k : k + 1, span] - err_ref[k : k + 1, span] * mult - seen
            nxt = mult + relaxation * resid
            total = total + jnp.where(row >= 0, resid * resid, 0.0)
            nhi = nxt.astype(BF16).astype(F32)
            nlo = nxt - nhi
            right = jnp.concatenate([jnp.where(here, nhi, 0.0), jnp.where(here, nlo, 0.0)], axis=0).astype(BF16)
            add = lax.dot_general(hot, right, (((1,), (1,)), ((), ())), preferred_element_type=F32)
            if b == 0:
                acc_s[...] = add
            else:
                acc_s[...] += add
            obs_ref[k : k + 1, span] = seen
        spread_ref[k] = acc_s[:, :latitude] + acc_s[:, latitude:]
    sum_ref[...] = total


def forward_kernel(
    keep_ref, inc_ref, traj_ref, land_ref, left_ref, right_ref, mult_ref, misfit_ref, damp_ref, edge_ref,
    fwd_ref, send_ref, mult_out, up_ref, dn_ref, sum_ref, x_s, y_s, q_s, h_s,
):
    subs, fields, width, latitude = inc_ref.shape[0], inc_ref.shape[1], land_ref.shape[0], land_ref.shape[1]
    lanes = Rows(latitude)
    keep = keep_ref[0, 0]

    def mask_at(c):
        if c < 0:
            return left_ref[AHEAD * subs].astype(F32)
        if c >= width:
            return right_ref[AHEAD * subs].astype(F32)
        return jnp.broadcast_to(land_ref[c : c + 1, :].astype(F32), (LB, latitude))

    @pl.when(pl.program_id(0) == 0)
    def _():
        sum_ref[...] = jnp.zeros_like(sum_ref)

    total = jnp.zeros((LB, latitude), F32)
    for k in reversed(range(subs)):
        base = AHEAD * k
        for j in range(2):
            for s in range(2):
                h_s[2 * j + s] = traj_ref[k, j, s].astype(F32)
        for c in range(width):
            for f in range(fields):
                x_s[f, c + 2] = rows_of(inc_ref, (k, f), c, width)
            kt, ks = dens(rows_of(h_s, (0,), c, width), rows_of(h_s, (1,), c, width))
            q_s[c + 2] = x_s[PR, c + 2] + gravity * (kt * x_s[TE, c + 2] + ks * x_s[SA, c + 2])
        for ref, near, far in ((left_ref, 1, 0), (right_ref, width + 2, width + 3)):
            for f, p in NEAR.items():
                x_s[f, near] = ref[base + p].astype(F32)
            for f, p in FAR.items():
                x_s[f, far] = ref[base + p].astype(F32)
            q_s[near] = ref[base + QN].astype(F32)
            q_s[far] = ref[base + QF].astype(F32)

        def substep(src, q, i, mask, with_v):
            te, sa, u, v, pr = (src[f, i] for f in range(5))
            lap = lambda f, x: src[f, i + 1] + src[f, i - 1] + lanes.both(x)
            centre = 1.0 - 4.0 * mixing
            heat = mask * (centre * te + mixing * lap(TE, te))
            salt = mask * (centre * sa + mixing * lap(SA, sa))
            east = mask * (u + lanes.rot * v - half * (q[i + 1] - q[i - 1]))
            north = mask * (v - lanes.rot * u - half * lanes.diff(q[i])) if with_v else None
            surf = mask * (
                centre * pr + mixing * lap(PR, pr) - half * (src[U, i + 1] - src[U, i - 1] + lanes.diff(v))
            )
            return heat, salt, east, north, surf

        for c in range(-1, width + 1):
            inside = 0 <= c < width
            new = substep(x_s, q_s, c + 2, mask_at(c), inside)
            for f in range(5):
                if new[f] is not None:
                    y_s[f, c + 2] = new[f]
            if inside:
                h0, h1 = rows_of(h_s, (2,), c, width), rows_of(h_s, (3,), c, width)
            else:
                ref = left_ref if c < 0 else right_ref
                h0, h1 = ref[base + H0].astype(F32), ref[base + H1].astype(F32)
            kt, ks = dens(h0, h1)
            y_s[5, c + 2] = new[PR] + gravity * (kt * new[TE] + ks * new[SA])
        for c in range(width):
            mask = mask_at(c)
            new = substep(y_s, y_s.at[5], c + 2, mask, True)
            for f in range(fields):
                if k == subs - 1:
                    fwd_ref[f, c] = new[f]
                    send_ref[f, c] = new[f].astype(BF16)
                    if c < 2 or c >= width - 2:
                        got = edge_ref[f, c if c < 2 else c - width + 4].astype(F32)
                        after = mask * (keep * (got + relaxation * new[f]))
                else:
                    mult = rows_of(mult_ref, (0, f), c, width)
                    resid = (
                        rows_of(misfit_ref, (0, f), c, width)
                        - damp_ref[f] * mult
                        - (rows_of(inc_ref, (k + 1, f), c, width) - new[f])
                    )
                    total = total + resid * resid
                    after = mult + relaxation * resid
                    mult_out[f, c] = after
                    after = mask * after
                where = BACK * k
                if c == width - 1:
                    up_ref[where + NEAR[f]] = after.astype(BF16)
                if c == width - 2 and f != V:
                    up_ref[where + FAR[f]] = after.astype(BF16)
                if c == 0:
                    dn_ref[where + NEAR[f]] = after.astype(BF16)
                if c == 1 and f != V:
                    dn_ref[where + FAR[f]] = after.astype(BF16)
    sum_ref[...] += total


def adjoint_kernel(
    keep_ref, inc_ref, traj_ref, land_ref, left_ref, right_ref, backl_ref, backr_ref, mult_ref, misfit_ref, damp_ref,
    fwd_ref, mnext_ref, edge_ref, inner_ref, prev_ref, spread_ref, sumf_ref, sums_ref,
    mult_out, grad_ref, tot_ref, x_s, y_s, h_s, acc_s,
):
    subs, fields, width, latitude = traj_ref.shape[0], mult_ref.shape[1], land_ref.shape[0], land_ref.shape[1]
    lanes = Rows(latitude)
    keep = keep_ref[0, 0]

    def mask_at(c):
        if c < 0:
            return left_ref[AHEAD * subs].astype(F32)
        if c >= width:
            return right_ref[AHEAD * subs].astype(F32)
        return jnp.broadcast_to(land_ref[c : c + 1, :].astype(F32), (LB, latitude))

    @pl.when(pl.program_id(0) == 0)
    def _():
        acc_s[...] = jnp.zeros_like(acc_s)

    misfit_total = jnp.zeros((LB, latitude), F32)
    grad_total = jnp.zeros((LB, latitude), F32)
    for k in range(subs):
        for j in range(2):
            for s in range(2):
                h_s[2 * j + s] = traj_ref[k, j, s].astype(F32)
        for c in range(width):
            mask = mask_at(c)
            for f in range(fields):
                if k == subs - 1:
                    got = inner_ref[f, c - 2] if 2 <= c < width - 2 else edge_ref[f, c if c < 2 else c - width + 4]
                    x_s[f, c + 2] = mask * (keep * (got.astype(F32) + relaxation * fwd_ref[f, c]))
                else:
                    x_s[f, c + 2] = mask * mnext_ref[f, c]
        for ref, near, far in ((backl_ref, 1, 0), (backr_ref, width + 2, width + 3)):
            for f, p in NEAR.items():
                x_s[f, near] = ref[BACK * k + p].astype(F32)
            for f, p in FAR.items():
                x_s[f, far] = ref[BACK * k + p].astype(F32)

        def back(src, i, h0, h1, with_v):
            te, sa, u, v, pr = (src[f, i] for f in range(5))
            kt, ks = dens(h0, h1)
            centre = 1.0 - 4.0 * mixing
            mix = lambda f, x: centre * x + mixing * (src[f, i + 1] + src[f, i - 1] + lanes.both(x))
            q = half * (src[U, i + 1] - src[U, i - 1] + lanes.diff(v))
            gq = gravity * q
            heat = mix(TE, te) + kt * gq
            salt = mix(SA, sa) + ks * gq
            east = u - lanes.rot * v + half * (src[PR, i + 1] - src[PR, i - 1])
            north = v + lanes.rot * u + half * lanes.diff(pr) if with_v else None
            surf = mix(PR, pr) + q
            return heat, salt, east, north, surf

        for c in range(-1, width + 1):
            inside = 0 <= c < width
            if inside:
                h0, h1 = rows_of(h_s, (2,), c, width), rows_of(h_s, (3,), c, width)
            else:
                ref = left_ref if c < 0 else right_ref
                h0, h1 = ref[AHEAD * k + H0].astype(F32), ref[AHEAD * k + H1].astype(F32)
            mask = mask_at(c)
            new = back(x_s, c + 2, h0, h1, inside)
            for f in range(5):
                if new[f] is not None:
                    y_s[f, c + 2] = mask * new[f]
        for c in range(width):
            new = back(y_s, c + 2, rows_of(h_s, (0,), c, width), rows_of(h_s, (1,), c, width), True)
            for f in range(fields):
                if k == 0:
                    mult = rows_of(mult_ref, (0, f), c, width)
                    resid = (
                        rows_of(misfit_ref, (0, f), c, width)
                        - damp_ref[f] * mult
                        - (rows_of(inc_ref, (0, f), c, width) - prev_ref[f, c].astype(F32))
                    )
                    misfit_total = misfit_total + resid * resid
                    value = mult + relaxation * resid
                else:
                    value = mnext_ref[f, c]
                mult_out[k, f, pl.ds(c, LB, stride=width), :] = value
                grad = value - new[f]
                if f < 2:
                    grad = grad + rows_of(spread_ref, (k, f), c, width)
                grad_total = grad_total + grad * grad
                grad_ref[k, f, pl.ds(c, LB, stride=width), :] = grad
    acc_s[0] += misfit_total
    acc_s[1] += grad_total

    @pl.when(pl.program_id(0) == pl.num_programs(0) - 1)
    def _():
        misfit_sum = jnp.sum(acc_s[0] + sumf_ref[...]) + jnp.sum(sums_ref[...])
        grad_sum = jnp.sum(acc_s[1])
        lane = lax.broadcasted_iota(jnp.int32, tot_ref.shape, 1)
        tot_ref[...] = jnp.where(lane == 0, misfit_sum, jnp.where(lane == 1, grad_sum, 0.0))


def step_kernel(recv_ref, inc_ref, grad_ref, out_ref):
    misfit_square = jnp.sum(recv_ref[:, 0:1])
    gradient_square = jnp.sum(recv_ref[:, 1:2])
    top = jnp.full((1, 128), misfit_square, F32)
    stride = top / (jnp.full((1, 128), gradient_square, F32) + epsilon)
    stride = stride[0, 0]
    out_ref[...] = inc_ref[...] - stride * grad_ref[...]


def shifted(shard, axis, by):
    peers = lax.axis_size(axis)
    pairs = [(i, i + by) for i in range(peers) if 0 <= i + by < peers]
    return lax.ppermute(shard, axis, pairs)


def around(shard, axis, by):
    peers = lax.axis_size(axis)
    return lax.ppermute(shard, axis, [(i, (i + by) % peers) for i in range(peers)])


def whole(shape):
    return pl.BlockSpec(shape, lambda i: (0,) * len(shape))


def on_device(
    increment, multiplier, sensor_multiplier, misfit, innovation,
    model_error, sensor_error, trajectory, land_sea, sensor_cells,
):
    subs, fields, levels, width, latitude = increment.shape
    nobs = sensor_cells.shape[1]
    teams, tiles = lax.axis_size("tm"), lax.axis_size("space")
    assert fields == 5 and trajectory.shape[1] == 2 and subs == 2 and levels % LB == 0 and width >= 4
    rows = levels * width
    steps = levels // LB
    block = LB * width
    inc = increment.reshape(subs, fields, rows, latitude)
    mult = multiplier.reshape(subs, fields, rows, latitude)
    mis = misfit.reshape(subs, fields, rows, latitude)
    traj = trajectory.reshape(subs, 2, 2, rows, latitude)
    damp = jnp.broadcast_to(model_error[:, :, None], (fields, levels, latitude))
    keep = jnp.where(lax.axis_index("tm") < teams - 1, 1.0, 0.0).astype(F32).reshape(1, 1)

    def call(kernel, name, ins, outs, scratch):
        return pl.pallas_call(
            kernel,
            name=name,
            grid=(steps,),
            in_specs=ins,
            out_specs=[o[0] for o in outs],
            out_shape=[o[1] for o in outs],
            scratch_shapes=scratch,
        )

    shape = jax.ShapeDtypeStruct
    smem = pl.BlockSpec((1, 1), lambda i: (0, 0), memory_space=pltpu.SMEM)
    state = lambda n, first=0: pl.BlockSpec((n, fields, block, latitude), lambda i: (first, 0, i, 0))
    saved = pl.BlockSpec((subs, 2, 2, block, latitude), lambda i: (0, 0, 0, i, 0))
    planes = lambda n: pl.BlockSpec((n, LB, latitude), lambda i: (0, i, 0))
    columns = lambda n: pl.BlockSpec((fields, n, LB, latitude), lambda i: (0, 0, i, 0))
    damping = pl.BlockSpec((fields, LB, latitude), lambda i: (0, i, 0))
    land = whole((width, latitude))
    scr = lambda *s: pltpu.VMEM(s, F32)

    ahead = subs * AHEAD + 1
    up, dn = call(
        pack_kernel, "pack",
        [state(subs), saved, land],
        [(planes(ahead), shape((ahead, levels, latitude), BF16))] * 2,
        [scr(4, block, latitude)],
    )(inc, traj, land_sea)
    left = around(up, "space", 1)
    right = around(dn, "space", -1)

    edge, inner = call(
        partial_kernel, "partial",
        [state(1), state(1), state(1), damping],
        [
            (columns(4), shape((fields, 4, levels, latitude), BF16)),
            (columns(width - 4), shape((fields, width - 4, levels, latitude), BF16)),
        ],
        [],
    )(inc, mult, mis, damp)
    edge_in = shifted(edge, "tm", -1)
    inner_in = shifted(inner, "tm", -1)

    plane = width * tiles * latitude
    offset = lax.axis_index("space") * width
    field_level = sensor_cells // plane
    remainder = sensor_cells % plane
    column = remainder // latitude - offset
    owned = (column >= 0) & (column < width)
    row_index = jnp.where(owned, field_level * width + column, -1)
    lat_index = remainder % latitude
    full = lambda *s: pl.BlockSpec(s, lambda i: (0,) * len(s))
    observed, spread, sensor_sum = pl.pallas_call(
        sensor_kernel,
        name="sensor",
        grid=(1,),
        in_specs=[full(subs, 2, rows, latitude)] + [full(subs, nobs)] * 5,
        out_specs=[full(subs, nobs), full(subs, 2 * rows, latitude), full(1, 512 if nobs % 512 == 0 else nobs)],
        out_shape=[
            shape((subs, nobs), F32),
            shape((subs, 2 * rows, latitude), F32),
            shape((1, 512 if nobs % 512 == 0 else nobs), F32),
        ],
        scratch_shapes=[scr(2 * rows, 2 * latitude)],
    )(inc, row_index, lat_index, sensor_multiplier, innovation, sensor_error)
    spread = spread.reshape(subs, 2, rows, latitude)

    fwd, send, mnext, back_up, back_dn, forward_sum = call(
        forward_kernel, "forward",
        [smem, state(subs), saved, land, planes(ahead), planes(ahead), state(1, 1), state(1, 1), damping, columns(4)],
        [
            (columns(width), shape((fields, width, levels, latitude), F32)),
            (columns(width), shape((fields, width, levels, latitude), BF16)),
            (columns(width), shape((fields, width, levels, latitude), F32)),
            (planes(subs * BACK), shape((subs * BACK, levels, latitude), BF16)),
            (planes(subs * BACK), shape((subs * BACK, levels, latitude), BF16)),
            (whole((LB, latitude)), shape((LB, latitude), F32)),
        ],
        [scr(5, width + 4, LB, latitude), scr(6, width + 4, LB, latitude), scr(width + 4, LB, latitude), scr(4, block, latitude)],
    )(keep, inc, traj, land_sea, left, right, mult, mis, damp, edge_in)
    back_left = around(back_up, "space", 1)
    back_right = around(back_dn, "space", -1)
    prev = shifted(send, "tm", 1)

    share = nobs // tiles
    pieces = observed.reshape(subs, tiles, share).transpose(1, 0, 2).reshape(tiles, -1, 128)
    pieces = jnp.sum(lax.all_to_all(pieces, "space", 0, 0), axis=0)

    mult_next, gradient, totals = call(
        adjoint_kernel, "adjoint",
        [
            smem, state(1), saved, land, planes(ahead), planes(ahead), planes(subs * BACK), planes(subs * BACK),
            state(1), state(1), damping, columns(width), columns(width), columns(4), columns(width - 4), columns(width),
            pl.BlockSpec((subs, 2, block, latitude), lambda i: (0, 0, i, 0)),
            whole((LB, latitude)), whole(sensor_sum.shape),
        ],
        [
            (state(subs), shape((subs, fields, rows, latitude), F32)),
            (state(subs), shape((subs, fields, rows, latitude), F32)),
            (whole((1, 128)), shape((1, 128), F32)),
        ],
        [scr(5, width + 4, LB, latitude), scr(5, width + 4, LB, latitude), scr(4, block, latitude), scr(2, LB, latitude)],
    )(
        keep, inc, traj, land_sea, left, right, back_left, back_right, mult, mis, damp,
        fwd, mnext, edge_in, inner_in, prev, spread, forward_sum, sensor_sum,
    )

    final = jnp.concatenate([totals, pieces], axis=0)
    final = jnp.broadcast_to(final[None], (teams * tiles,) + final.shape)
    final = lax.all_to_all(final, ("tm", "space"), 0, 0)

    increment_next = call(
        step_kernel, "step",
        [whole((teams * tiles, 128)), state(subs), state(subs)],
        [(state(subs), shape((subs, fields, rows, latitude), F32))],
        [],
    )(final[:, 0], inc, gradient)[0]

    mine = lax.dynamic_slice_in_dim(final, lax.axis_index("tm") * tiles, tiles, axis=0)[:, 1:]
    whole_obs = mine.reshape(tiles, subs, share).transpose(1, 0, 2).reshape(subs, nobs)
    sensor_next = sensor_multiplier + relaxation * (innovation - sensor_error * sensor_multiplier - whole_obs)
    return (increment_next.reshape(increment.shape), mult_next.reshape(multiplier.shape), sensor_next)


def solution(mesh):
    state = P("tm", None, None, "space", None)
    placed = (
        state,
        state,
        P("tm", None),
        state,
        P("tm", None),
        P(),
        P("tm", None),
        P("tm", None, None, None, "space", None),
        P("space", None),
        P("tm", None),
    )
    return jax.shard_map(
        on_device,
        mesh=mesh,
        in_specs=placed,
        out_specs=(state, state, P("tm", None)),
        check_vma=False,
    )
```

time: 275 us -> 82 us (0.30)
  blocking collectives: 97.1 us -> 9.94 us
  other arithmetic: 60 us -> 2.69 us
  local copies, waits for them, and re-layouts: 52.4 us -> 3.88 us
  Pallas kernels: 0 us -> 32.4 us
  starting transfers between devices: 39.7 us -> 16.7 us
  waiting for transfers between devices: 20.6 us -> 15 us
  between operations: 4.83 us -> 0.79 us
    psum x2 -> x0, blocking collectives: 97.1 us -> none  [the longest x1 58.2 us: on_device(): observed = lax.psum(local_values, 'space')]
    gather x3 -> x0, local copies, waits for them, and re-layouts: 34.9 us -> none  [on_device(): jnp.take_along_axis(flattened, local_index, axis=1)]
    pallas_call x0 -> x6, Pallas kernels: none -> 32.4 us  [the longest x1 7.66 us: on_device(): call(adjoint_kernel, 'adjoint', [smem, state(1), saved, land, planes(ahea...]
    unnamed x20 -> x0, other arithmetic: 31.9 us -> none
    ppermute x18 -> x4, starting transfers between devices: 34.5 us -> 9.96 us  [around(): lax.ppermute(shard, axis, [(i, (i + by) % peers) for i in range(peers)])]
    all_to_all x0 -> x1, blocking collectives: none -> 9.94 us  [on_device(): pieces = jnp.sum(lax.all_to_all(pieces, 'space', 0, 0), axis=0)]
    ppermute x18 -> x4, waiting for transfers between devices: 9.24 us -> 0.01 us  [around(): lax.ppermute(shard, axis, [(i, (i + by) % peers) for i in range(peers)])]
    all_to_all x0 -> x1, waiting for transfers between devices: none -> 7.41 us  [on_device(): final = lax.all_to_all(final, ('tm', 'space'), 0, 0)]
  transfers between devices with their start and end apart: 20 -> 8, of which waited for: 7 -> 2; matrix products, arithmetic and copies ran while one was open for 28% -> 3% of each run, Pallas kernels for 0% -> 20%
where the time goes in v1:
time: 82 us; the launch traced here: 81.4 us
  Pallas kernels  32.4 us (40%)
  starting transfers between devices  16.7 us (20%)
  waiting for transfers between devices  15 us (18%)
  blocking collectives  9.94 us (12%)
  local copies, waits for them, and re-layouts  3.88 us (5%)
  other arithmetic  2.69 us (3%)
    ppermute x4, starting transfers between devices, around(): lax.ppermute(shard, axis, [(i, (i + by) % peers) for i in range(peers)])  9.96 us
    all_to_all x1, blocking collectives, on_device(): pieces = jnp.sum(lax.all_to_all(pieces, 'space', 0, 0), axis=0)  9.94 us
    pallas_call x1, Pallas kernels, on_device(): call(adjoint_kernel, 'adjoint', [smem, state(1), saved, land, planes(ahea...  7.66 us
    ppermute x3, waiting for transfers between devices, shifted(): return lax.ppermute(shard, axis, pairs)  7.59 us
    all_to_all x1, waiting for transfers between devices, on_device(): final = lax.all_to_all(final, ('tm', 'space'), 0, 0)  7.41 us
    pallas_call x1, Pallas kernels, on_device(): pl.pallas_call(sensor_kernel, name='sensor', grid=(1,), in_specs=[full(su...  6.75 us
    pallas_call x1, Pallas kernels, on_device(): call(forward_kernel, 'forward', [smem, state(subs), saved, land, planes(a...  6.34 us
    pallas_call x1, Pallas kernels, on_device(): call(step_kernel, 'step', [whole((teams * tiles, 128)), state(subs), stat...  4.61 us
  transfers between devices with their start and end apart: 8, of which 2 were waited for; matrix products, arithmetic and copies ran while one was open for 3% of the time, Pallas kernels for 20%

profile of v1, /device:TPU:0, one launch (start us, length us, event | category | flops | bytes accessed | tf_op | source)
XLA Modules:
  0.0 81.4 jit_solution(4793091533668730416)
XLA Ops:
  0.6 3.5 %pack.1 = (bf16[27,48,128]{2,1,0:T(8,128)(2,1)}, bf16[27,48,128]{2,1,0:T(8,128)(2,1)}) custom-call(f32[2,5,384,128]{3,2,1,0:T(8,128)} %bitcast.24, bf16[2,2,2,384,128]{4,3,2,1,0:T(8,128)(2,1)} %bitcast.36, s32[8,128]{1,0:T(8,128)} %land_ref.5), custom_call_target="tpu_custom_call" | custom-call | tf_op jit(solution)/shard_map/pack/pallas_call | solution.py:397
  4.1 0.5 collective-permute-start
  4.6 5.0 %collective-permute-start.1 = (bf16[27,48,128]{2,1,0:T(8,128)(2,1)}, bf16[27,48,128]{2,1,0:T(8,128)(2,1)S(1)}, u32[]{:S(2)}, u32[]{:S(2)}) collective-permute-start(bf16[27,48,128]{2,1,0:T(8,128)(2,1)} %get-tuple-element.20), channel_id=1, source_target_pairs={{0,15},{1,0},{2,1},{3,2},{4,3},{5,4},{6,5},{7,6},{8,7},{9,8},{10,9... | collective-permute-start | bytes 995336 | tf_op jit(solution)/shard_map/ppermute | solution.py:350
  9.6 0.7 broadcast_in_dim.6.damp_ref
  10.4 3.5 %partial.1 = (bf16[5,4,48,128]{3,2,1,0:T(8,128)(2,1)}, bf16[5,4,48,128]{3,2,1,0:T(8,128)(2,1)}) custom-call(f32[2,5,384,128]{3,2,1,0:T(8,128)} %bitcast.25, f32[2,5,384,128]{3,2,1,0:T(8,128)} %bitcast.30, f32[2,5,384,128]{3,2,1,0:T(8,128)} %bitcast.33, f32[5,48,128]{2,1,0:T(8,128)} %broadcast_in_dim.6.damp_ref), custom_call_target="tpu_custom_call" | custom-call | tf_op jit(solution)/shard_map/partial/pallas_call | solution.py:406
  13.9 1.3 %collective-permute-start.2 = (bf16[5,4,48,128]{3,2,1,0:T(8,128)(2,1)}, bf16[5,4,48,128]{3,2,1,0:T(8,128)(2,1)S(1)}, u32[]{:S(2)}, u32[]{:S(2)}) collective-permute-start(bf16[5,4,48,128]{3,2,1,0:T(8,128)(2,1)} %get-tuple-element.21), channel_id=1, source_target_pairs={{16,0},{17,1},{18,2},{19,3},{20,4},{21,5},{22,6},{23,7},{24,8},{25... | collective-permute-start | bytes 737288 | tf_op jit(solution)/shard_map/ppermute | solution.py:345
  15.2 1.3 %collective-permute-start.5 = (bf16[5,4,48,128]{3,2,1,0:T(8,128)(2,1)}, bf16[5,4,48,128]{3,2,1,0:T(8,128)(2,1)S(1)}, u32[]{:S(2)}, u32[]{:S(2)}) collective-permute-start(bf16[5,4,48,128]{3,2,1,0:T(8,128)(2,1)} %get-tuple-element.26), channel_id=1, source_target_pairs={{16,0},{17,1},{18,2},{19,3},{20,4},{21,5},{22,6},{23,7},{24,8},{25... | collective-permute-start | bytes 737288 | tf_op jit(solution)/shard_map/ppermute | solution.py:345
  16.5 7.6 %collective-permute-done.2.edge_ref = bf16[5,4,48,128]{3,2,1,0:T(8,128)(2,1)S(1)} collective-permute-done((bf16[5,4,48,128]{3,2,1,0:T(8,128)(2,1)}, bf16[5,4,48,128]{3,2,1,0:T(8,128)(2,1)S(1)}, u32[]{:S(2)}, u32[]{:S(2)}) %collective-permute-start.2) | collective-permute-done | bytes 245792 | tf_op jit(solution)/shard_map/ppermute | solution.py:345
  24.1 0.0 collective-permute-done.left_ref
  24.1 0.0 collective-permute-done.1.right_ref
  24.1 0.7 copy-done.2
  24.8 0.1 copy-done
  24.9 0.1 copy-done.1
  25.0 6.3 %forward.1 = (f32[5,8,48,128]{3,2,1,0:T(8,128)}, bf16[5,8,48,128]{3,2,1,0:T(8,128)(2,1)}, f32[5,8,48,128]{3,2,1,0:T(8,128)}, bf16[18,48,128]{2,1,0:T(8,128)(2,1)...) custom-call(f32[1,1]{1,0:T(1,128)} %bitcast.keep_ref, f32[2,5,384,128]{3,2,1,0:T(8,128)} %bitcast.26, ...), custom_call_target="tpu_custom_call" | custom-call | tf_op jit(solution)/shard_map/forward/pallas_call | solution.py:442
  31.4 1.6 %collective-permute-start.6 = (bf16[5,8,48,128]{3,2,1,0:T(8,128)(2,1)}, bf16[5,8,48,128]{3,2,1,0:T(8,128)(2,1)S(1)}, u32[]{:S(2)}, u32[]{:S(2)}) collective-permute-start(bf16[5,8,48,128]{3,2,1,0:T(8,128)(2,1)} %get-tuple-element.27), channel_id=1, source_target_pairs={{0,16},{1,17},{2,18},{3,19},{4,20},{5,21},{6,22},{7,23},{8,24},{9,... | collective-permute-start | bytes 1474568 | tf_op jit(solution)/shard_map/ppermute | solution.py:345
  33.0 0.7 and_select_fusion
  33.6 4.4 %collective-permute-start.4 = (bf16[18,48,128]{2,1,0:T(8,128)(2,1)}, bf16[18,48,128]{2,1,0:T(8,128)(2,1)S(1)}, u32[]{:S(2)}, u32[]{:S(2)}) collective-permute-start(bf16[18,48,128]{2,1,0:T(8,128)(2,1)} %get-tuple-element.23), channel_id=1, source_target_pairs={{0,15},{1,0},{2,1},{3,2},{4,3},{5,4},{6,5},{7,6},{8,7},{9,8},{10,9... | collective-permute-start | bytes 663560 | tf_op jit(solution)/shard_map/ppermute | solution.py:350
  38.1 0.7 and_select_fusion.2.row_ref
  38.8 6.8 %sensor.1 = (f32[2,2048]{1,0:T(2,128)}, f32[2,768,128]{2,1,0:T(8,128)}, f32[1,512]{1,0:T(1,128)}) custom-call(f32[2,5,384,128]{3,2,1,0:T(8,128)} %bitcast.27, s32[2,2048]{1,0:T(2,128)} %and_select_fusion.2.row_ref, s32[2,2048]{1,0:T(2,128)} %get-tuple-element.35.lat_ref, f32[2,2048]{1,0:T(2,128)} %mult_ref.1, f32[2,2048]{1,0:T(2,128)} %innov_ref.1, ...), custom_call_target="tpu_custom_call" | custom-call | tf_op jit(solution)/shard_map/sensor/pallas_call | solution.py:427
  45.5 9.9 %all_to_all.10 = f32[16,2,128]{2,1,0:T(2,128)S(1)} all-to-all(f32[16,2,128]{2,1,0:T(2,128)} %bitcast.42), channel_id=1, replica_groups=mesh['tm'=2,'space'=16] {'space'}, dimensions={0} | all-to-all | bytes 32768 | tf_op jit(solution)/shard_map/all_to_all | solution.py:461
  55.6 0.7 copy-done.4
  56.2 0.1 copy-done.5
  56.3 0.1 copy-done.6
  56.4 0.1 copy-done.3
  56.5 7.7 %adjoint.1 = (f32[2,5,384,128]{3,2,1,0:T(8,128)}, f32[2,5,384,128]{3,2,1,0:T(8,128)}, f32[1,128]{1,0:T(1,128)}) custom-call(f32[1,1]{1,0:T(1,128)} %bitcast.keep_ref, f32[2,5,384,128]{3,2,1,0:T(8,128)} %bitcast.28, bf16[2,2,2,384,128]{4,3,2,1,0:T(8,128)(2,1)} %bitcast.38, s32[8,128]{1,0:T(8,128)} %land_ref.5, bf16[27,48,128]{2,1,0:T(8,128)(2,1)} %copy-done, ...), custom_call_target="tpu_custom_call" | custom-call | tf_op jit(solution)/shard_map/adjoint/pallas_call | solution.py:463
  64.2 0.7 pad_maximum_fusion
  64.8 0.6 broadcast_in_dim.7
  65.5 2.6 %all-to-all-start.1 = ((f32[32,3,128]{2,1,0:T(4,128)}), f32[32,3,128]{2,1,0:T(4,128)S(1)}, u32[]{:S(2)}, u32[]{:S(2)}) async-start(f32[32,3,128]{2,1,0:T(4,128)} %broadcast_in_dim.7), calls=%async_computation.1 | async-start | bytes 131072 | tf_op jit(solution)/shard_map/all_to_all | solution.py:484
  68.0 7.4 %all-to-all-done.1 = f32[32,3,128]{2,1,0:T(4,128)S(1)} async-done(((f32[32,3,128]{2,1,0:T(4,128)}), f32[32,3,128]{2,1,0:T(4,128)S(1)}, u32[]{:S(2)}, u32[]{:S(2)}) %all-to-all-start.1) | async-done | bytes 49184 | tf_op jit(solution)/shard_map/all_to_all | solution.py:484
  75.5 0.6 slice.8
  76.1 4.6 %step.1 = f32[2,5,384,128]{3,2,1,0:T(8,128)} custom-call(f32[32,128]{1,0:T(8,128)} %bitcast.41, f32[2,5,384,128]{3,2,1,0:T(8,128)} %bitcast.29, f32[2,5,384,128]{3,2,1,0:T(8,128)} %get-tuple-element.33.grad_ref), custom_call_target="tpu_custom_call" | custom-call | tf_op jit(solution)/shard_map/step/pallas_call | solution.py:486
  80.7 0.6 fusion.2
  (23 shorter events, 0.1 us)
Async XLA Ops:
  0.6 9.0 %copy-start.11 = (f32[5,48]{1,0:T(8,128)S(1)}, f32[5,48]{1,0:T(8,128)}, u32[]{:S(2)}) copy-start(f32[5,48]{1,0:T(8,128)} %param.15) | copy-start | bytes 2884
  4.1 20.0 %collective-permute-start = (bf16[27,48,128]{2,1,0:T(8,128)(2,1)}, bf16[27,48,128]{2,1,0:T(8,128)(2,1)S(1)}, u32[]{:S(2)}, u32[]{:S(2)}) collective-permute-start(bf16[27,48,128]{2,1,0:T(8,128)(2,1)} %get-tuple-element.19), channel_id=1, source_target_pairs={{0,1},{1,2},{2,3},{3,4},{4,5},{5,6},{6,7},{7,8},{8,9},{9,10},{10,1... | collective-permute-start | bytes 995336 | tf_op jit(solution)/shard_map/ppermute | solution.py:350
  4.6 19.5 %collective-permute-start.1 = (bf16[27,48,128]{2,1,0:T(8,128)(2,1)}, bf16[27,48,128]{2,1,0:T(8,128)(2,1)S(1)}, u32[]{:S(2)}, u32[]{:S(2)}) collective-permute-start(bf16[27,48,128]{2,1,0:T(8,128)(2,1)} %get-tuple-element.20), channel_id=1, source_target_pairs={{0,15},{1,0},{2,1},{3,2},{4,3},{5,4},{6,5},{7,6},{8,7},{9,8},{10,9... | collective-permute-start | bytes 995336 | tf_op jit(solution)/shard_map/ppermute | solution.py:350
  13.9 10.2 %collective-permute-start.2 = (bf16[5,4,48,128]{3,2,1,0:T(8,128)(2,1)}, bf16[5,4,48,128]{3,2,1,0:T(8,128)(2,1)S(1)}, u32[]{:S(2)}, u32[]{:S(2)}) collective-permute-start(bf16[5,4,48,128]{3,2,1,0:T(8,128)(2,1)} %get-tuple-element.21), channel_id=1, source_target_pairs={{16,0},{17,1},{18,2},{19,3},{20,4},{21,5},{22,6},{23,7},{24,8},{25... | collective-permute-start | bytes 737288 | tf_op jit(solution)/shard_map/ppermute | solution.py:345
  15.2 40.3 %collective-permute-start.5 = (bf16[5,4,48,128]{3,2,1,0:T(8,128)(2,1)}, bf16[5,4,48,128]{3,2,1,0:T(8,128)(2,1)S(1)}, u32[]{:S(2)}, u32[]{:S(2)}) collective-permute-start(bf16[5,4,48,128]{3,2,1,0:T(8,128)(2,1)} %get-tuple-element.26), channel_id=1, source_target_pairs={{16,0},{17,1},{18,2},{19,3},{20,4},{21,5},{22,6},{23,7},{24,8},{25... | collective-permute-start | bytes 737288 | tf_op jit(solution)/shard_map/ppermute | solution.py:345
  24.1 0.7 copy-start.2
  24.1 0.8 copy-start
  24.1 0.9 %copy-start.1 = (bf16[27,48,128]{2,1,0:T(8,128)(2,1)}, bf16[27,48,128]{2,1,0:T(8,128)(2,1)S(1)}, u32[]{:S(2)}) copy-start(bf16[27,48,128]{2,1,0:T(8,128)(2,1)S(1)} %collective-permute-done.1.right_ref) | copy-start | bytes 995332
  25.0 7.9 %copy-start.10 = (s32[2,2048]{1,0:T(2,128)S(1)}, s32[2,2048]{1,0:T(2,128)}, u32[]{:S(2)}) copy-start(s32[2,2048]{1,0:T(2,128)} %param.19) | copy-start | bytes 49156
  31.4 24.2 %collective-permute-start.6 = (bf16[5,8,48,128]{3,2,1,0:T(8,128)(2,1)}, bf16[5,8,48,128]{3,2,1,0:T(8,128)(2,1)S(1)}, u32[]{:S(2)}, u32[]{:S(2)}) collective-permute-start(bf16[5,8,48,128]{3,2,1,0:T(8,128)(2,1)} %get-tuple-element.27), channel_id=1, source_target_pairs={{0,16},{1,17},{2,18},{3,19},{4,20},{5,21},{6,22},{7,23},{8,24},{9,... | collective-permute-start | bytes 1474568 | tf_op jit(solution)/shard_map/ppermute | solution.py:345
  33.6 21.9 %collective-permute-start.3 = (bf16[18,48,128]{2,1,0:T(8,128)(2,1)}, bf16[18,48,128]{2,1,0:T(8,128)(2,1)S(1)}, u32[]{:S(2)}, u32[]{:S(2)}) collective-permute-start(bf16[18,48,128]{2,1,0:T(8,128)(2,1)} %get-tuple-element.22), channel_id=1, source_target_pairs={{0,1},{1,2},{2,3},{3,4},{4,5},{5,6},{6,7},{7,8},{8,9},{9,10},{10,1... | collective-permute-start | bytes 663560 | tf_op jit(solution)/shard_map/ppermute | solution.py:350
  33.6 21.9 %collective-permute-start.4 = (bf16[18,48,128]{2,1,0:T(8,128)(2,1)}, bf16[18,48,128]{2,1,0:T(8,128)(2,1)S(1)}, u32[]{:S(2)}, u32[]{:S(2)}) collective-permute-start(bf16[18,48,128]{2,1,0:T(8,128)(2,1)} %get-tuple-element.23), channel_id=1, source_target_pairs={{0,15},{1,0},{2,1},{3,2},{4,3},{5,4},{6,5},{7,6},{8,7},{9,8},{10,9... | collective-permute-start | bytes 663560 | tf_op jit(solution)/shard_map/ppermute | solution.py:350
  55.5 0.7 copy-start.4
  55.5 0.8 copy-start.5
  55.5 0.8 %copy-start.6 = (bf16[18,48,128]{2,1,0:T(8,128)(2,1)}, bf16[18,48,128]{2,1,0:T(8,128)(2,1)S(1)}, u32[]{:S(2)}) copy-start(bf16[18,48,128]{2,1,0:T(8,128)(2,1)S(1)} %collective-permute-done.4.backr_ref) | copy-start | bytes 663556
  55.6 0.9 %copy-start.3 = (bf16[5,8,48,128]{3,2,1,0:T(8,128)(2,1)}, bf16[5,8,48,128]{3,2,1,0:T(8,128)(2,1)S(1)}, u32[]{:S(2)}) copy-start(bf16[5,8,48,128]{3,2,1,0:T(8,128)(2,1)S(1)} %collective-permute-done.6.prev_ref) | copy-start | bytes 1474564
  65.5 10.0 %all-to-all-start.1 = ((f32[32,3,128]{2,1,0:T(4,128)}), f32[32,3,128]{2,1,0:T(4,128)S(1)}, u32[]{:S(2)}, u32[]{:S(2)}) async-start(f32[32,3,128]{2,1,0:T(4,128)} %broadcast_in_dim.7), calls=%async_computation.1 | async-start | bytes 131072 | tf_op jit(solution)/shard_map/all_to_all | solution.py:484
  76.1 4.6 %copy-start.7 = (f32[2,2048]{1,0:T(2,128)S(1)}, f32[2,2048]{1,0:T(2,128)}, u32[]{:S(2)}) copy-start(f32[2,2048]{1,0:T(2,128)} %mult_ref.1) | copy-start | bytes 49156
  76.1 4.6 %copy-start.8 = (f32[2,2048]{1,0:T(2,128)S(1)}, f32[2,2048]{1,0:T(2,128)}, u32[]{:S(2)}) copy-start(f32[2,2048]{1,0:T(2,128)} %innov_ref.1) | copy-start | bytes 49156
  76.1 4.6 %copy-start.9 = (f32[2,2048]{1,0:T(2,128)S(1)}, f32[2,2048]{1,0:T(2,128)}, u32[]{:S(2)}) copy-start(f32[2,2048]{1,0:T(2,128)} %err_ref.1) | copy-start | bytes 49156

commit v2 on v0

v2 whole, which is shorter than its diff:
```python
import jax
import jax.numpy as jnp
from jax import lax
from jax.experimental import pallas as pl
from jax.experimental.pallas import tpu as pltpu
from jax.sharding import PartitionSpec as P

thermal_lin = 0.2
thermal_quad = 0.02
haline_lin = 0.8
cabbeling = 0.01
gravity = 1.0
time_stride = 0.3
mixing = 0.15
coriolis = 0.5
relaxation = 0.5
epsilon = 1e-06

kt0 = -thermal_lin + 10.0 * thermal_quad - 5.0 * cabbeling
kt1 = -30.0 * thermal_quad
kt2 = 8.0 * cabbeling
ks0 = haline_lin - 10.0 * cabbeling
ks1 = 30.0 * cabbeling
half = 0.5 * time_stride

LB = 16
VMEM_LIMIT = 16 * 1024 * 1024
TE, SA, U, V, PR = range(5)
F32 = jnp.float32
BF16 = jnp.bfloat16

NEAR = {TE: 0, SA: 1, U: 2, V: 3, PR: 4}
FAR = {TE: 5, SA: 6, U: 7, PR: 8}
BACK = 9
QN, QF, H0, H1 = 9, 10, 11, 12
AHEAD = 13


def rows_of(ref, lead, block, col, width):
    return ref[lead + (pl.ds(block * (LB * width) + col, LB, stride=width), slice(None))]


def dens(h0, h1):
    return kt0 + kt1 * h0 + kt2 * h1, ks0 + ks1 * h0


class Rows:
    def __init__(self, latitude):
        lane = lax.broadcasted_iota(jnp.int32, (LB, latitude), 1)
        self.n = latitude
        self.first = lane == 0
        self.last = lane == latitude - 1
        row = lane.astype(F32)
        self.rot = (time_stride * coriolis / (0.5 * latitude)) * (row - 0.5 * (latitude - 1))

    def up(self, f):
        return jnp.where(self.last, 0.0, pltpu.roll(f, self.n - 1, 1))

    def down(self, f):
        return jnp.where(self.first, 0.0, pltpu.roll(f, 1, 1))

    def diff(self, f):
        return self.up(f) - self.down(f)

    def both(self, f):
        return self.up(f) + self.down(f)


def blocks_of(levels, body):
    lax.fori_loop(0, levels // LB, lambda b, carry: (body(b), carry)[1], 0)


def at(block):
    return pl.ds(pl.multiple_of(block * LB, LB), LB)


def native(block, width):
    size = LB * width
    return pl.ds(pl.multiple_of(block * size, size), size)


def load_kernel(
    error_ref, inc_hbm, traj_hbm, mult_hbm, misfit_hbm, land_ref,
    inc_ref, traj_ref, mult_ref, misfit_ref, up_ref, dn_ref, edge_ref, inner_ref, damp_ref, h_s, sems,
):
    subs, fields, width, levels, latitude = inc_ref.shape[0], inc_ref.shape[1], land_ref.shape[0], up_ref.shape[1], land_ref.shape[1]
    level = lax.broadcasted_iota(jnp.int32, (LB, latitude), 0)

    def copies(b):
        rows = native(b, width)
        first = [
            pltpu.make_async_copy(inc_hbm.at[:, :, rows], inc_ref.at[:, :, rows], sems.at[0, b]),
            pltpu.make_async_copy(traj_hbm.at[:, :, :, rows], traj_ref.at[:, :, :, rows], sems.at[1, b]),
        ]
        second = [
            pltpu.make_async_copy(mult_hbm.at[0, :, rows], mult_ref.at[:, rows], sems.at[2, b]),
            pltpu.make_async_copy(misfit_hbm.at[0, :, rows], misfit_ref.at[:, rows], sems.at[3, b]),
        ]
        return first, second

    for part in range(2):
        for b in range(levels // LB):
            for c in copies(b)[part]:
                c.start()

    def ahead(b):
        for c in copies(b)[0]:
            c.wait()
        for k in range(subs):
            for j in range(2):
                for s in range(2):
                    h_s[2 * j + s] = traj_ref[k, j, s, native(b, width), :].astype(F32)
            for out, near, far in ((up_ref, width - 1, width - 2), (dn_ref, 0, 1)):
                base = AHEAD * k
                for col, planes, q in ((near, NEAR, QN), (far, FAR, QF)):
                    vals = {f: rows_of(inc_ref, (k, f), b, col, width) for f in planes}
                    for f, p in planes.items():
                        out[base + p, at(b), :] = vals[f].astype(BF16)
                    kt, ks = dens(rows_of(h_s, (0,), 0, col, width), rows_of(h_s, (1,), 0, col, width))
                    out[base + q, at(b), :] = (vals[PR] + gravity * (kt * vals[TE] + ks * vals[SA])).astype(BF16)
                out[base + H0, at(b), :] = rows_of(h_s, (2,), 0, near, width).astype(BF16)
                out[base + H1, at(b), :] = rows_of(h_s, (3,), 0, near, width).astype(BF16)
        for out, near in ((up_ref, width - 1), (dn_ref, 0)):
            mask = land_ref[near : near + 1, :].astype(F32)
            out[AHEAD * subs, at(b), :] = jnp.broadcast_to(mask, (LB, mask.shape[1])).astype(BF16)

    def partial(b):
        for f in range(fields):
            damp = jnp.zeros((LB, latitude), F32)
            for i in range(LB):
                damp = jnp.where(level == i, error_ref[f, b * LB + i], damp)
            damp_ref[f, at(b), :] = damp
        for c in copies(b)[1]:
            c.wait()
        for f in range(fields):
            damp = damp_ref[f, at(b), :]
            for c in range(width):
                mult = rows_of(mult_ref, (f,), b, c, width)
                resid = rows_of(misfit_ref, (f,), b, c, width) - damp * mult - rows_of(inc_ref, (0, f), b, c, width)
                value = (mult + relaxation * resid).astype(BF16)
                if 2 <= c < width - 2:
                    inner_ref[f, c - 2, at(b), :] = value
                else:
                    edge_ref[f, c if c < 2 else c - width + 4, at(b), :] = value

    blocks_of(levels, ahead)
    blocks_of(levels, partial)


def prepare_kernel(traj_ref, mult_hbm, misfit_hbm, dens_ref, mult_ref, misfit_ref, h_s, sems):
    subs, width, levels = dens_ref.shape[0], dens_ref.shape[3], dens_ref.shape[4]
    copies = [
        pltpu.make_async_copy(mult_hbm.at[1], mult_ref, sems.at[0]),
        pltpu.make_async_copy(misfit_hbm.at[1], misfit_ref, sems.at[1]),
    ]
    for c in copies:
        c.start()

    def body(b):
        for k in range(subs):
            for j in range(2):
                for s in range(2):
                    h_s[s] = traj_ref[k, j, s, native(b, width), :].astype(F32)
                for c in range(width):
                    kt, ks = dens(rows_of(h_s, (0,), 0, c, width), rows_of(h_s, (1,), 0, c, width))
                    dens_ref[k, j, 0, c, at(b), :] = kt
                    dens_ref[k, j, 1, c, at(b), :] = ks

    blocks_of(levels, body)
    for c in copies:
        c.wait()


def sensor_kernel(inc_ref, cell_ref, mult_ref, innov_ref, err_ref, obs_ref, spread_ref, sum_ref, hot_s, acc_s, *, width, columns):
    subs, rows, latitude = inc_ref.shape[0], 2 * inc_ref.shape[2], inc_ref.shape[3]
    nobs = cell_ref.shape[1]
    peers, share = obs_ref.shape[0], obs_ref.shape[1]
    tiles = subs * nobs // (128 * share)
    blk = 512
    small = 32
    lat_bits = latitude.bit_length() - 1
    col_bits = columns.bit_length() - 1
    offset = lax.axis_index("space") * width
    total = jnp.zeros((1, blk), F32)
    for k in range(subs):
        flat_t = jnp.concatenate([inc_ref[k, 0], inc_ref[k, 1]], axis=0).T
        hi = flat_t.astype(BF16)
        lo = (flat_t - hi.astype(F32)).astype(BF16)
        left = jnp.concatenate([hi, lo], axis=0)
        for b in range(nobs // blk):
            span = slice(b * blk, (b + 1) * blk)
            cell = cell_ref[k : k + 1, span]
            lat = cell & (latitude - 1)
            column = (lax.shift_right_logical(cell, lat_bits) & (columns - 1)) - offset
            owned = (column >= 0) & (column < width)
            row = jnp.where(owned, lax.shift_right_logical(cell, lat_bits + col_bits) * width + column, -1)
            fine = jnp.where(lax.broadcasted_iota(jnp.int32, (small, blk), 0) == (row & (small - 1)), 1.0, 0.0).astype(BF16)
            group = lax.shift_right_arithmetic(row, small.bit_length() - 1)
            for i in range(rows // small):
                coarse = jnp.broadcast_to(jnp.where(group == i, 1.0, 0.0), (small, blk)).astype(BF16)
                hot_s[i * small : (i + 1) * small, :] = coarse * fine
            hot = hot_s[...]
            here = lax.broadcasted_iota(jnp.int32, (latitude, blk), 0) == lat
            both = jnp.dot(left, hot, preferred_element_type=F32)
            seen = jnp.sum(jnp.where(here, both[:latitude] + both[latitude:], 0.0), axis=0, keepdims=True)
            mult = mult_ref[k : k + 1, span]
            resid = innov_ref[k : k + 1, span] - err_ref[k : k + 1, span] * mult - seen
            nxt = mult + relaxation * resid
            total = total + jnp.where(owned, resid * resid, 0.0)
            nhi = nxt.astype(BF16).astype(F32)
            nlo = nxt - nhi
            right = jnp.concatenate([jnp.where(here, nhi, 0.0), jnp.where(here, nlo, 0.0)], axis=0).astype(BF16)
            add = lax.dot_general(hot, right, (((1,), (1,)), ((), ())), preferred_element_type=F32)
            if b == 0:
                acc_s[...] = add
            else:
                acc_s[...] += add
            for i in range(blk // 128):
                g = (k * nobs + b * blk) // 128 + i
                for t in range(peers // tiles):
                    obs_ref[t * tiles + g // share, g % share : g % share + 1, :] = seen[:, i * 128 : (i + 1) * 128]
        spread_ref[k] = acc_s[:, :latitude] + acc_s[:, latitude:]
    sum_ref[...] = total


def keeper(axis):
    return jnp.where(lax.axis_index(axis) < lax.axis_size(axis) - 1, 1.0, 0.0).astype(F32)


def forward_kernel(
    inc_ref, dens_ref, land_ref, left_ref, right_ref, mult_ref, misfit_ref, damp_ref, edge_ref, sensor_ref,
    fwd_ref, send_ref, mult_out, up_ref, dn_ref, sum_ref, x_s, y_s, q_s,
):
    subs, fields, width, latitude = inc_ref.shape[0], inc_ref.shape[1], land_ref.shape[0], land_ref.shape[1]
    levels = fwd_ref.shape[2]
    lanes = Rows(latitude)
    keep = keeper("tm")
    centre = 1.0 - 4.0 * mixing
    sum_ref[...] = jnp.zeros_like(sum_ref)
    sum_ref[0:1, :] = jnp.full((1, latitude), jnp.sum(sensor_ref[...]) / latitude, F32)

    def body(b):
        def mask_at(c):
            if c < 0:
                return left_ref[AHEAD * subs, at(b), :].astype(F32)
            if c >= width:
                return right_ref[AHEAD * subs, at(b), :].astype(F32)
            return jnp.broadcast_to(land_ref[c : c + 1, :].astype(F32), (LB, latitude))

        total = jnp.zeros((LB, latitude), F32)
        for k in reversed(range(subs)):
            base = AHEAD * k
            for c in range(width):
                for f in range(fields):
                    x_s[f, c + 2] = rows_of(inc_ref, (k, f), b, c, width)
                kt, ks = dens_ref[k, 0, 0, c, at(b), :], dens_ref[k, 0, 1, c, at(b), :]
                q_s[c + 2] = x_s[PR, c + 2] + gravity * (kt * x_s[TE, c + 2] + ks * x_s[SA, c + 2])
            for ref, near, far in ((left_ref, 1, 0), (right_ref, width + 2, width + 3)):
                for f, p in NEAR.items():
                    x_s[f, near] = ref[base + p, at(b), :].astype(F32)
                for f, p in FAR.items():
                    x_s[f, far] = ref[base + p, at(b), :].astype(F32)
                q_s[near] = ref[base + QN, at(b), :].astype(F32)
                q_s[far] = ref[base + QF, at(b), :].astype(F32)

            def substep(src, q, i, mask, with_v):
                te, sa, u, v, pr = (src[f, i] for f in range(5))
                stay, swap = centre * mask, mixing * mask
                thrust = half * mask
                heat = stay * te + swap * (src[TE, i + 1] + src[TE, i - 1] + lanes.both(te))
                salt = stay * sa + swap * (src[SA, i + 1] + src[SA, i - 1] + lanes.both(sa))
                east = mask * (u + lanes.rot * v) - thrust * (q[i + 1] - q[i - 1])
                north = mask * (v - lanes.rot * u) - thrust * lanes.diff(q[i]) if with_v else None
                if mixing == half:
                    around_p = lanes.up(pr - v) + lanes.down(pr + v)
                    around_p = around_p + (src[PR, i + 1] + src[PR, i - 1]) - (src[U, i + 1] - src[U, i - 1])
                    surf = stay * pr + swap * around_p
                else:
                    surf = stay * pr + swap * (src[PR, i + 1] + src[PR, i - 1] + lanes.both(pr))
                    surf = surf - thrust * (src[U, i + 1] - src[U, i - 1] + lanes.diff(v))
                return heat, salt, east, north, surf

            for c in range(-1, width + 1):
                inside = 0 <= c < width
                new = substep(x_s, q_s, c + 2, mask_at(c), inside)
                for f in range(5):
                    if new[f] is not None:
                        y_s[f, c + 2] = new[f]
                if inside:
                    kt, ks = dens_ref[k, 1, 0, c, at(b), :], dens_ref[k, 1, 1, c, at(b), :]
                else:
                    ref = left_ref if c < 0 else right_ref
                    kt, ks = dens(ref[base + H0, at(b), :].astype(F32), ref[base + H1, at(b), :].astype(F32))
                y_s[5, c + 2] = new[PR] + gravity * (kt * new[TE] + ks * new[SA])
            for c in range(width):
                mask = mask_at(c)
                new = substep(y_s, y_s.at[5], c + 2, mask, True)
                for f in range(fields):
                    if k == subs - 1:
                        fwd_ref[f, c, at(b), :] = new[f]
                        send_ref[f, c, at(b), :] = new[f].astype(BF16)
                        if c < 2 or c >= width - 2:
                            got = edge_ref[f, c if c < 2 else c - width + 4, at(b), :].astype(F32)
                            after = mask * (keep * (got + relaxation * new[f]))
                    else:
                        mult = rows_of(mult_ref, (f,), b, c, width)
                        resid = (
                            rows_of(misfit_ref, (f,), b, c, width)
                            - damp_ref[f, at(b), :] * mult
                            - (rows_of(inc_ref, (k + 1, f), b, c, width) - new[f])
                        )
                        total = total + resid * resid
                        after = mult + relaxation * resid
                        mult_out[f, c, at(b), :] = after
                        after = mask * after
                    where = BACK * k
                    if c == width - 1:
                        up_ref[where + NEAR[f], at(b), :] = after.astype(BF16)
                    if c == width - 2 and f != V:
                        up_ref[where + FAR[f], at(b), :] = after.astype(BF16)
                    if c == 0:
                        dn_ref[where + NEAR[f], at(b), :] = after.astype(BF16)
                    if c == 1 and f != V:
                        dn_ref[where + FAR[f], at(b), :] = after.astype(BF16)
        sum_ref[...] += total

    blocks_of(levels, body)


def adjoint_kernel(
    inc_ref, dens_ref, land_ref, left_ref, right_ref, backl_ref, backr_ref, mult_ref, misfit_ref, damp_ref,
    fwd_ref, mnext_ref, edge_ref, inner_ref, prev_ref, spread_ref, sum_ref, seen_ref,
    mult_out, grad_ref, fin_ref, x_s, y_s, acc_s,
):
    subs, fields, width, latitude = dens_ref.shape[0], mult_ref.shape[0], land_ref.shape[0], land_ref.shape[1]
    levels = fwd_ref.shape[2]
    lanes = Rows(latitude)
    keep = keeper("tm")
    centre = 1.0 - 4.0 * mixing
    b = pl.program_id(0)

    @pl.when(b == 0)
    def _():
        acc_s[...] = jnp.zeros_like(acc_s)

    def body():
        def mask_at(c):
            if c < 0:
                return left_ref[AHEAD * subs, at(b), :].astype(F32)
            if c >= width:
                return right_ref[AHEAD * subs, at(b), :].astype(F32)
            return jnp.broadcast_to(land_ref[c : c + 1, :].astype(F32), (LB, latitude))

        misfit_total = jnp.zeros((LB, latitude), F32)
        grad_total = jnp.zeros((LB, latitude), F32)
        for k in range(subs):
            for c in range(width):
                mask = mask_at(c)
                for f in range(fields):
                    if k == subs - 1:
                        if 2 <= c < width - 2:
                            got = inner_ref[f, c - 2, at(b), :]
                        else:
                            got = edge_ref[f, c if c < 2 else c - width + 4, at(b), :]
                        value = keep * (got.astype(F32) + relaxation * fwd_ref[f, c, at(b), :])
                    else:
                        value = mnext_ref[f, c, at(b), :]
                    x_s[f, c + 2] = mask * value
            for ref, near, far in ((backl_ref, 1, 0), (backr_ref, width + 2, width + 3)):
                for f, p in NEAR.items():
                    x_s[f, near] = ref[BACK * k + p, at(b), :].astype(F32)
                for f, p in FAR.items():
                    x_s[f, far] = ref[BACK * k + p, at(b), :].astype(F32)

            def back(src, i, kt, ks, with_v):
                te, sa, u, v, pr = (src[f, i] for f in range(5))
                mix = lambda f, x: centre * x + mixing * (src[f, i + 1] + src[f, i - 1] + lanes.both(x))
                q = half * (src[U, i + 1] - src[U, i - 1] + lanes.diff(v))
                gq = gravity * q if gravity != 1.0 else q
                heat = mix(TE, te) + kt * gq
                salt = mix(SA, sa) + ks * gq
                east = u - lanes.rot * v + half * (src[PR, i + 1] - src[PR, i - 1])
                north = v + lanes.rot * u + half * lanes.diff(pr) if with_v else None
                surf = mix(PR, pr) + q
                return heat, salt, east, north, surf

            for c in range(-1, width + 1):
                inside = 0 <= c < width
                if inside:
                    kt, ks = dens_ref[k, 1, 0, c, at(b), :], dens_ref[k, 1, 1, c, at(b), :]
                else:
                    ref = left_ref if c < 0 else right_ref
                    kt, ks = dens(
                        ref[AHEAD * k + H0, at(b), :].astype(F32), ref[AHEAD * k + H1, at(b), :].astype(F32)
                    )
                mask = mask_at(c)
                new = back(x_s, c + 2, kt, ks, inside)
                for f in range(5):
                    if new[f] is not None:
                        y_s[f, c + 2] = mask * new[f]
            for c in range(width):
                new = back(y_s, c + 2, dens_ref[k, 0, 0, c, at(b), :], dens_ref[k, 0, 1, c, at(b), :], True)
                for f in range(fields):
                    if k == 0:
                        mult = rows_of(mult_ref, (f,), b, c, width)
                        resid = (
                            rows_of(misfit_ref, (f,), b, c, width)
                            - damp_ref[f, at(b), :] * mult
                            - (rows_of(inc_ref, (0, f), b, c, width) - prev_ref[f, c, at(b), :].astype(F32))
                        )
                        misfit_total = misfit_total + resid * resid
                        value = mult + relaxation * resid
                    else:
                        value = mnext_ref[f, c, at(b), :]
                    spot = pl.ds(b * (LB * width) + c, LB, stride=width)
                    mult_out[k, f, pl.ds(c, LB, stride=width), :] = value
                    grad = value - new[f]
                    if f < 2:
                        grad = grad + rows_of(spread_ref, (k, f), b, c, width)
                    grad_total = grad_total + grad * grad
                    grad_ref[k, f, spot, :] = grad
        acc_s[0] += misfit_total
        acc_s[1] += grad_total

    body()

    @pl.when(b == pl.num_programs(0) - 1)
    def _():
        misfit_sum = jnp.sum(acc_s[0] + sum_ref[...])
        grad_sum = jnp.sum(acc_s[1])
        lane = lax.broadcasted_iota(jnp.int32, (1, 128), 1)
        scalars = jnp.where(lane == 0, misfit_sum, jnp.where(lane == 1, grad_sum, 0.0))
        tiles = lax.axis_size("space")
        mine = seen_ref[pl.ds(lax.axis_index("tm") * tiles, tiles)]
        pieces = jnp.sum(mine, axis=0)
        peers = fin_ref.shape[0]
        for i in range(peers):
            fin_ref[i, 0:1, :] = scalars
            fin_ref[i, 1:, :] = pieces


def step_kernel(recv_ref, inc_ref, grad_ref, mult_ref, innov_ref, err_ref, out_ref, next_ref, *, steps):
    parts = recv_ref[:, 0, :]
    sums = jnp.sum(parts, axis=0, keepdims=True)
    lane = lax.broadcasted_iota(jnp.int32, sums.shape, 1)
    misfit_square = jnp.sum(jnp.where(lane == 0, sums, 0.0), axis=1, keepdims=True)
    gradient_square = jnp.sum(jnp.where(lane == 1, sums, 0.0), axis=1, keepdims=True)
    stride = misfit_square / (gradient_square + epsilon)
    size = out_ref.shape[2]
    b = pl.program_id(0)
    spot = pl.ds(pl.multiple_of(b * size, size), size)
    for k in range(inc_ref.shape[0]):
        for f in range(inc_ref.shape[1]):
            out_ref[k, f] = inc_ref[k, f, spot, :] - stride * grad_ref[k, f, spot, :]

    @pl.when(b == 0)
    def _():
        subs, nobs = mult_ref.shape
        share = recv_ref.shape[1] - 1
        first = lax.axis_index("tm") * lax.axis_size("space")
        for k in range(subs):
            for i in range(nobs // 128):
                g = k * (nobs // 128) + i
                span = slice(i * 128, (i + 1) * 128)
                seen = recv_ref[first + g // share, 1 + g % share : 2 + g % share, :]
                mult = mult_ref[k : k + 1, span]
                resid = innov_ref[k : k + 1, span] - err_ref[k : k + 1, span] * mult - seen
                next_ref[k : k + 1, span] = mult + relaxation * resid


def shifted(shard, axis, by):
    peers = lax.axis_size(axis)
    pairs = [(i, i + by) for i in range(peers) if 0 <= i + by < peers]
    return lax.ppermute(shard, axis, pairs)


def around(shard, axis, by):
    peers = lax.axis_size(axis)
    return lax.ppermute(shard, axis, [(i, (i + by) % peers) for i in range(peers)])


def on_device(
    increment, multiplier, sensor_multiplier, misfit, innovation,
    model_error, sensor_error, trajectory, land_sea, sensor_cells,
):
    subs, fields, levels, width, latitude = increment.shape
    nobs = sensor_cells.shape[1]
    teams, tiles = lax.axis_size("tm"), lax.axis_size("space")
    peers = teams * tiles
    share = subs * nobs // (128 * tiles)
    assert fields == 5 and trajectory.shape[1] == 2 and subs == 2 and levels % LB == 0 and width >= 4
    assert latitude == 128 and (width * tiles) & (width * tiles - 1) == 0 and nobs % 512 == 0
    assert share * 128 * tiles == subs * nobs and (2 * levels * width) % 32 == 0
    rows = levels * width
    fast = lambda x: pltpu.with_memory_space_constraint(x, pltpu.VMEM)
    slow = lambda x: pltpu.with_memory_space_constraint(x, pltpu.HBM)
    native_shape = (subs, fields, rows, latitude)
    inc = slow(increment.reshape(native_shape))
    traj = slow(trajectory.reshape(subs, 2, 2, rows, latitude))
    mult = slow(multiplier.reshape(native_shape))
    mis = slow(misfit.reshape(native_shape))
    land = fast(land_sea)
    cells, sen_m, sen_i, sen_e = (fast(x) for x in (sensor_cells, sensor_multiplier, innovation, sensor_error))
    vmem = pl.BlockSpec(memory_space=pltpu.VMEM)
    smem = pl.BlockSpec(memory_space=pltpu.SMEM)
    hbm = pl.BlockSpec(memory_space=pltpu.HBM)
    scr = lambda *s: pltpu.VMEM(s, F32)
    limit = pltpu.CompilerParams(vmem_limit_bytes=VMEM_LIMIT)

    def call(kernel, name, outs, scratch, *args, specs=None):
        return pl.pallas_call(
            kernel,
            name=name,
            in_specs=specs or [vmem] * len(args),
            out_specs=[vmem] * len(outs),
            out_shape=[pltpu.VMEM(s, d) for s, d in outs],
            scratch_shapes=scratch,
            compiler_params=limit,
        )(*args)

    ahead = (subs * AHEAD + 1, levels, latitude)
    one = native_shape[1:]
    inc, traj, mult0, mis0, up, dn, edge, inner, damp = call(
        load_kernel, "load",
        [
            (native_shape, F32), (traj.shape, BF16), (one, F32), (one, F32), (ahead, BF16), (ahead, BF16),
            ((fields, 4, levels, latitude), BF16),
            ((fields, width - 4, levels, latitude), BF16),
            ((fields, levels, latitude), F32),
        ],
        [scr(4, LB * width, latitude), pltpu.SemaphoreType.DMA((4, levels // LB))],
        model_error, inc, traj, mult, mis, land,
        specs=[smem] + [hbm] * 4 + [vmem],
    )
    left = fast(around(up, "space", 1))
    right = fast(around(dn, "space", -1))
    edge_in = fast(shifted(edge, "tm", -1))
    inner_in = fast(shifted(inner, "tm", -1))

    density, mult1, mis1 = call(
        prepare_kernel, "prepare",
        [((subs, 2, 2, width, levels, latitude), F32), (one, F32), (one, F32)],
        [scr(2, LB * width, latitude), pltpu.SemaphoreType.DMA((2,))],
        traj, mult, mis,
        specs=[vmem, hbm, hbm],
    )

    seen, spread, sensor_sum = call(
        lambda *refs: sensor_kernel(*refs, width=width, columns=width * tiles), "sensor",
        [((peers, share, 128), F32), ((subs, 2 * rows, latitude), F32), ((1, 512), F32)],
        [pltpu.VMEM((2 * rows, 512), BF16), scr(2 * rows, 2 * latitude)],
        inc, cells, sen_m, sen_i, sen_e,
    )
    spread = spread.reshape(subs, 2, rows, latitude)
    seen_in = fast(lax.all_to_all(seen, ("tm", "space"), 0, 0))

    column = (fields, width, levels, latitude)
    behind = (subs * BACK, levels, latitude)
    fwd, send, mnext, back_up, back_dn, sums = call(
        forward_kernel, "forward",
        [(column, F32), (column, BF16), (column, F32), (behind, BF16), (behind, BF16), ((LB, latitude), F32)],
        [scr(5, width + 4, LB, latitude), scr(6, width + 4, LB, latitude), scr(width + 4, LB, latitude)],
        inc, density, land, left, right, mult1, mis1, damp, edge_in, sensor_sum,
    )
    back_left = fast(around(back_up, "space", 1))
    back_right = fast(around(back_dn, "space", -1))
    prev = fast(shifted(send, "tm", 1))

    block = pl.BlockSpec((subs, fields, LB * width, latitude), lambda i: (0, 0, i, 0))
    mult_next, gradient, final = pl.pallas_call(
        adjoint_kernel,
        name="adjoint",
        grid=(levels // LB,),
        in_specs=[vmem] * 18,
        out_specs=[block, vmem, vmem],
        out_shape=[
            jax.ShapeDtypeStruct(native_shape, F32),
            pltpu.VMEM(native_shape, F32),
            pltpu.VMEM((peers, 1 + share, 128), F32),
        ],
        scratch_shapes=[scr(5, width + 4, LB, latitude), scr(5, width + 4, LB, latitude), scr(2, LB, latitude)],
        compiler_params=limit,
    )(
        inc, density, land, left, right, back_left, back_right, mult0, mis0, damp,
        fwd, mnext, edge_in, inner_in, prev, spread, sums, seen_in,
    )
    final = fast(lax.all_to_all(final, ("tm", "space"), 0, 0))

    steps = 4 if rows % 32 == 0 else 1
    size = rows // steps
    increment_next, sensor_next = pl.pallas_call(
        lambda *refs: step_kernel(*refs, steps=steps),
        name="step",
        grid=(steps,),
        in_specs=[vmem] * 6,
        out_specs=[
            pl.BlockSpec((subs, fields, size, latitude), lambda i: (0, 0, i, 0)),
            pl.BlockSpec((subs, nobs), lambda i: (0, 0)),
        ],
        out_shape=[
            jax.ShapeDtypeStruct(native_shape, F32),
            jax.ShapeDtypeStruct((subs, nobs), F32),
        ],
        compiler_params=limit,
    )(final, inc, gradient, sen_m, sen_i, sen_e)
    return (increment_next.reshape(increment.shape), mult_next.reshape(multiplier.shape), sensor_next)


def solution(mesh):
    state = P("tm", None, None, "space", None)
    placed = (
        state,
        state,
        P("tm", None),
        state,
        P("tm", None),
        P(),
        P("tm", None),
        P("tm", None, None, None, "space", None),
        P("space", None),
        P("tm", None),
    )
    return jax.shard_map(
        on_device,
        mesh=mesh,
        in_specs=placed,
        out_specs=(state, state, P("tm", None)),
        check_vma=False,
    )
```

time: 275 us -> 57.6 us (0.21)
  blocking collectives: 97.1 us -> 19.2 us
  other arithmetic: 60 us -> 0 us
  local copies, waits for them, and re-layouts: 52.4 us -> 1.4 us
  starting transfers between devices: 39.7 us -> 16.4 us
  waiting for transfers between devices: 20.6 us -> 0.86 us
  Pallas kernels: 0 us -> 18.7 us
  between operations: 4.83 us -> 0.79 us
    psum x2 -> x0, blocking collectives: 97.1 us -> none  [the longest x1 58.2 us: on_device(): observed = lax.psum(local_values, 'space')]
    gather x3 -> x0, local copies, waits for them, and re-layouts: 34.9 us -> none  [on_device(): jnp.take_along_axis(flattened, local_index, axis=1)]
    unnamed x20 -> x0, other arithmetic: 31.9 us -> none
    ppermute x18 -> x4, starting transfers between devices: 34.5 us -> 10.1 us  [around(): lax.ppermute(shard, axis, [(i, (i + by) % peers) for i in range(peers)])]
    all_to_all x0 -> x2, blocking collectives: none -> 19.2 us  [the longest x1 10.1 us: on_device(): seen_in = fast(lax.all_to_all(seen, ('tm', 'space'), 0, 0))]
    pallas_call x0 -> x6, Pallas kernels: none -> 18.7 us  [the longest x4 12.2 us: call(): pl.pallas_call(kernel, name=name, in_specs=specs or [vmem] * len(args), o...]
    ppermute x2 -> x3, waiting for transfers between devices: 11.4 us -> 0.85 us  [shifted(): return lax.ppermute(shard, axis, pairs)]
    ppermute x18 -> x4, waiting for transfers between devices: 9.24 us -> 0.01 us  [around(): lax.ppermute(shard, axis, [(i, (i + by) % peers) for i in range(peers)])]
  transfers between devices with their start and end apart: 20 -> 7, of which waited for: 7 -> 1; matrix products, arithmetic and copies ran while one was open for 28% -> 0% of each run, Pallas kernels for 0% -> 10%
where the time goes in v2:
time: 57.6 us; the launch traced here: 57.3 us
  blocking collectives  19.2 us (33%)
  Pallas kernels  18.7 us (32%)
  starting transfers between devices  16.4 us (28%)
  local copies, waits for them, and re-layouts  1.4 us (2%)
  waiting for transfers between devices  0.86 us (1%)
  between operations  0.79 us (1%)
    pallas_call x4, Pallas kernels, call(): pl.pallas_call(kernel, name=name, in_specs=specs or [vmem] * len(args), o...  12.2 us
    ppermute x4, starting transfers between devices, around(): lax.ppermute(shard, axis, [(i, (i + by) % peers) for i in range(peers)])  10.1 us
    all_to_all x1, blocking collectives, on_device(): seen_in = fast(lax.all_to_all(seen, ('tm', 'space'), 0, 0))  10.1 us
    all_to_all x1, blocking collectives, on_device(): final = fast(lax.all_to_all(final, ('tm', 'space'), 0, 0))  9.09 us
    ppermute x3, starting transfers between devices, shifted(): return lax.ppermute(shard, axis, pairs)  6.34 us
    pallas_call x1, Pallas kernels, on_device(): pl.pallas_call(adjoint_kernel, name='adjoint', grid=(levels // LB,), in_s...  4.39 us
    pallas_call x1, Pallas kernels, on_device(): pl.pallas_call(lambda *refs: step_kernel(*refs, steps=steps), name='step'...  2.05 us
    unnamed x14, local copies, waits for them, and re-layouts  1.4 us
  transfers between devices with their start and end apart: 7, of which 1 were waited for; matrix products, arithmetic and copies ran while one was open for 0% of the time, Pallas kernels for 10%

profile of v2, /device:TPU:0, one launch (start us, length us, event | category | flops | bytes accessed | tf_op | source)
XLA Modules:
  0.0 57.3 jit_solution(91022348032439462)
XLA Ops:
  0.6 0.0 copy-start.3
  0.6 0.7 %copy-done.3 = s32[8,128]{1,0:T(8,128)S(1)} copy-done((s32[8,128]{1,0:T(8,128)S(1)}, s32[8,128]{1,0:T(8,128)}, u32[]{:S(2)}) %copy-start.3) | copy-done | bytes 4120
  1.3 0.7 %copy-done.6 = f32[5,48]{1,0:T(8,128)S(1)} copy-done((f32[5,48]{1,0:T(8,128)S(1)}, f32[5,48]{1,0:T(8,128)}, u32[]{:S(2)}) %copy-start.6) | copy-done | bytes 984
  2.0 3.4 %load.1 = (f32[2,5,384,128]{3,2,1,0:T(8,128)S(1)}, bf16[2,2,2,384,128]{4,3,2,1,0:T(8,128)(2,1)S(1)}, f32[5,384,128]{2,1,0:T(8,128)S(1)}, f32[5,384,128]{2,1,0:T(...) custom-call(f32[5,48]{1,0:T(8,128)S(1)} %copy-done.6, ...), custom_call_target="tpu_custom_call" | custom-call | tf_op jit(solution)/shard_map/load/pallas_call | solution.py:511
  5.4 0.5 collective-permute-start
  5.9 5.0 %collective-permute-start.1 = (bf16[27,48,128]{2,1,0:T(8,128)(2,1)S(1)}, bf16[27,48,128]{2,1,0:T(8,128)(2,1)S(1)}, u32[]{:S(2)}, u32[]{:S(2)}) collective-permute-start(bf16[27,48,128]{2,1,0:T(8,128)(2,1)S(1)} %get-tuple-element.33), channel_id=1, source_target_pairs={{0,15},{1,0},{2,1},{3,2},{4,3},{5,4},{6,5},{7,6},{8,7},{9,8},{10,9... | collective-permute-start | bytes 995336 | tf_op jit(solution)/shard_map/ppermute | solution.py:479
  11.0 1.3 %collective-permute-start.2 = (bf16[5,4,48,128]{3,2,1,0:T(8,128)(2,1)S(1)}, bf16[5,4,48,128]{3,2,1,0:T(8,128)(2,1)S(1)}, u32[]{:S(2)}, u32[]{:S(2)}) collective-permute-start(bf16[5,4,48,128]{3,2,1,0:T(8,128)(2,1)S(1)} %get-tuple-element.37), channel_id=1, source_target_pairs={{16,0},{17,1},{18,2},{19,3},{20,4},{21,5},{22,6},{23,7},{24,8},{25... | collective-permute-start | bytes 737288 | tf_op jit(solution)/shard_map/ppermute | solution.py:474
  12.3 0.0 copy-start
  12.3 0.0 copy-start.1
  12.3 0.0 copy-start.2
  12.3 0.0 copy-start.5
  12.3 1.5 %prepare.1 = (f32[2,2,2,8,48,128]{5,4,3,2,1,0:T(8,128)S(1)}, f32[5,384,128]{2,1,0:T(8,128)S(1)}, f32[5,384,128]{2,1,0:T(8,128)S(1)}) custom-call(bf16[2,2,2,384,128]{4,3,2,1,0:T(8,128)(2,1)S(1)} %get-tuple-element.30.traj_ref, f32[2,5,384,128]{3,2,1,0:T(8,128)} %bitcast.9, f32[2,5,384,128]{3,2,1,0:T(8,128)} %bitcast.11), custom_call_target="tpu_custom_call" | custom-call | tf_op jit(solution)/shard_map/prepare/pallas_call | solution.py:511
  13.9 0.0 copy-start.4
  13.9 0.0 copy-done
  13.9 0.0 copy-done.1
  13.9 4.3 %sensor.1 = (f32[32,2,128]{2,1,0:T(2,128)S(1)}, f32[2,768,128]{2,1,0:T(8,128)S(1)}, f32[1,512]{1,0:T(1,128)S(1)}) custom-call(f32[2,5,384,128]{3,2,1,0:T(8,128)S(1)} %get-tuple-element.29.refs_0_.inc_ref.refs_1_, s32[2,2048]{1,0:T(2,128)S(1)} %copy-done.5, f32[2,2048]{1,0:T(2,128)S(1)} %copy-done, f32[2,2048]{1,0:T(2,128)S(1)} %copy-done.1, ...), custom_call_target="tpu_custom_call" | custom-call | tf_op jit(solution)/shard_map/sensor/pallas_call | solution.py:511
  18.2 0.8 %collective-permute-done.2.edge_ref = bf16[5,4,48,128]{3,2,1,0:T(8,128)(2,1)S(1)} collective-permute-done((bf16[5,4,48,128]{3,2,1,0:T(8,128)(2,1)S(1)}, bf16[5,4,48,128]{3,2,1,0:T(8,128)(2,1)S(1)}, u32[]{:S(2)}, u32[]{:S(2)}) %collective-permute-start.2) | collective-permute-done | bytes 245792 | tf_op jit(solution)/shard_map/ppermute | solution.py:474
  19.1 0.0 collective-permute-done.left_ref
  19.1 0.0 collective-permute-done.1.right_ref
  19.1 3.0 %forward.1 = (f32[5,8,48,128]{3,2,1,0:T(8,128)S(1)}, bf16[5,8,48,128]{3,2,1,0:T(8,128)(2,1)S(1)}, f32[5,8,48,128]{3,2,1,0:T(8,128)S(1)}, bf16[18,48,128]{2,1,0:T...) custom-call(f32[2,5,384,128]{3,2,1,0:T(8,128)S(1)} %get-tuple-element.29.refs_0_.inc_ref.refs_1_, ...), custom_call_target="tpu_custom_call" | custom-call | tf_op jit(solution)/shard_map/forward/pallas_call | solution.py:511
  22.1 3.8 %collective-permute-start.6 = (bf16[5,8,48,128]{3,2,1,0:T(8,128)(2,1)S(1)}, bf16[5,8,48,128]{3,2,1,0:T(8,128)(2,1)S(1)}, u32[]{:S(2)}, u32[]{:S(2)}) collective-permute-start(bf16[5,8,48,128]{3,2,1,0:T(8,128)(2,1)S(1)} %get-tuple-element.46), channel_id=1, source_target_pairs={{0,16},{1,17},{2,18},{3,19},{4,20},{5,21},{6,22},{7,23},{8,24},{9,... | collective-permute-start | bytes 1474568 | tf_op jit(solution)/shard_map/ppermute | solution.py:474
  25.9 1.3 %collective-permute-start.5 = (bf16[5,4,48,128]{3,2,1,0:T(8,128)(2,1)S(1)}, bf16[5,4,48,128]{3,2,1,0:T(8,128)(2,1)S(1)}, u32[]{:S(2)}, u32[]{:S(2)}) collective-permute-start(bf16[5,4,48,128]{3,2,1,0:T(8,128)(2,1)S(1)} %get-tuple-element.45), channel_id=1, source_target_pairs={{16,0},{17,1},{18,2},{19,3},{20,4},{21,5},{22,6},{23,7},{24,8},{25... | collective-permute-start | bytes 737288 | tf_op jit(solution)/shard_map/ppermute | solution.py:474
  27.2 0.1 collective-permute-start.3
  27.2 4.4 %collective-permute-start.4 = (bf16[18,48,128]{2,1,0:T(8,128)(2,1)S(1)}, bf16[18,48,128]{2,1,0:T(8,128)(2,1)S(1)}, u32[]{:S(2)}, u32[]{:S(2)}) collective-permute-start(bf16[18,48,128]{2,1,0:T(8,128)(2,1)S(1)} %get-tuple-element.40), channel_id=1, source_target_pairs={{0,15},{1,0},{2,1},{3,2},{4,3},{5,4},{6,5},{7,6},{8,7},{9,8},{10,9... | collective-permute-start | bytes 663560 | tf_op jit(solution)/shard_map/ppermute | solution.py:479
  31.7 10.1 %all_to_all.10.seen_ref = f32[32,2,128]{2,1,0:T(2,128)S(1)} all-to-all(f32[32,2,128]{2,1,0:T(2,128)S(1)} %get-tuple-element.49), channel_id=1, replica_groups=mesh['tm'=2,'space'=16] {'tm','space'}, dimensions={0} | all-to-all | bytes 65536 | tf_op jit(solution)/shard_map/all_to_all | solution.py:555
  41.7 0.0 collective-permute-done.5.inner_ref
  41.7 0.0 collective-permute-done.3.backl_ref
  41.8 0.0 collective-permute-done.4.backr_ref
  41.8 0.0 collective-permute-done.6.prev_ref
  41.8 4.4 %adjoint.1 = (f32[2,5,384,128]{3,2,1,0:T(8,128)}, f32[2,5,384,128]{3,2,1,0:T(8,128)S(1)}, f32[32,3,128]{2,1,0:T(4,128)S(1)}) custom-call(f32[2,5,384,128]{3,2,1,0:T(8,128)S(1)} %get-tuple-element.29.refs_0_.inc_ref.refs_1_, f32[2,2,2,8,48,128]{5,4,3,2,1,0:T(8,128)S(1)} %get-tuple-element.31.dens_ref, s32[8,128]{1,0:T(8,128)S(1)} %copy-done.4, ...), custom_call_target="tpu_custom_call" | custom-call | tf_op jit(solution)/shard_map/adjoint/pallas_call | solution.py:570
  46.2 9.1 %all_to_all.11.refs_0_ = f32[32,3,128]{2,1,0:T(4,128)S(1)} all-to-all(f32[32,3,128]{2,1,0:T(4,128)S(1)} %get-tuple-element.50), channel_id=1, replica_groups=mesh['tm'=2,'space'=16] {'tm','space'}, dimensions={0} | all-to-all | bytes 98304 | tf_op jit(solution)/shard_map/all_to_all | solution.py:587
  55.2 2.1 %step.1 = (f32[2,5,384,128]{3,2,1,0:T(8,128)}, f32[2,2048]{1,0:T(2,128)}) custom-call(f32[32,3,128]{2,1,0:T(4,128)S(1)} %all_to_all.11.refs_0_, f32[2,5,384,128]{3,2,1,0:T(8,128)S(1)} %get-tuple-element.29.refs_0_.inc_ref.refs_1_, f32[2,5,384,128]{3,2,1,0:T(8,128)S(1)} %get-tuple-element.51.refs_2_, f32[2,2048]{1,0:T(2,128)S(1)} %copy-done, ...), custom_call_target="tpu_custom_call" | custom-call | tf_op jit(solution)/shard_map/step/pallas_call | solution.py:591
  (4 shorter events, 0.0 us)
Async XLA Ops:
  0.6 0.7 %copy-start.3 = (s32[8,128]{1,0:T(8,128)S(1)}, s32[8,128]{1,0:T(8,128)}, u32[]{:S(2)}) copy-start(s32[8,128]{1,0:T(8,128)} %land_ref.5) | copy-start | bytes 12292
  1.3 0.7 %copy-start.6 = (f32[5,48]{1,0:T(8,128)S(1)}, f32[5,48]{1,0:T(8,128)}, u32[]{:S(2)}) copy-start(f32[5,48]{1,0:T(8,128)} %error_ref.1) | copy-start | bytes 2884
  5.4 13.7 %collective-permute-start = (bf16[27,48,128]{2,1,0:T(8,128)(2,1)S(1)}, bf16[27,48,128]{2,1,0:T(8,128)(2,1)S(1)}, u32[]{:S(2)}, u32[]{:S(2)}) collective-permute-start(bf16[27,48,128]{2,1,0:T(8,128)(2,1)S(1)} %get-tuple-element.32), channel_id=1, source_target_pairs={{0,1},{1,2},{2,3},{3,4},{4,5},{5,6},{6,7},{7,8},{8,9},{9,10},{10,1... | collective-permute-start | bytes 995336 | tf_op jit(solution)/shard_map/ppermute | solution.py:479
  5.9 13.1 %collective-permute-start.1 = (bf16[27,48,128]{2,1,0:T(8,128)(2,1)S(1)}, bf16[27,48,128]{2,1,0:T(8,128)(2,1)S(1)}, u32[]{:S(2)}, u32[]{:S(2)}) collective-permute-start(bf16[27,48,128]{2,1,0:T(8,128)(2,1)S(1)} %get-tuple-element.33), channel_id=1, source_target_pairs={{0,15},{1,0},{2,1},{3,2},{4,3},{5,4},{6,5},{7,6},{8,7},{9,8},{10,9... | collective-permute-start | bytes 995336 | tf_op jit(solution)/shard_map/ppermute | solution.py:479
  11.0 8.1 %collective-permute-start.2 = (bf16[5,4,48,128]{3,2,1,0:T(8,128)(2,1)S(1)}, bf16[5,4,48,128]{3,2,1,0:T(8,128)(2,1)S(1)}, u32[]{:S(2)}, u32[]{:S(2)}) collective-permute-start(bf16[5,4,48,128]{3,2,1,0:T(8,128)(2,1)S(1)} %get-tuple-element.37), channel_id=1, source_target_pairs={{16,0},{17,1},{18,2},{19,3},{20,4},{21,5},{22,6},{23,7},{24,8},{25... | collective-permute-start | bytes 737288 | tf_op jit(solution)/shard_map/ppermute | solution.py:474
  12.3 1.6 %copy-start = (f32[2,2048]{1,0:T(2,128)S(1)}, f32[2,2048]{1,0:T(2,128)}, u32[]{:S(2)}) copy-start(f32[2,2048]{1,0:T(2,128)} %refs_3_.3) | copy-start | bytes 49156
  12.3 1.6 %copy-start.1 = (f32[2,2048]{1,0:T(2,128)S(1)}, f32[2,2048]{1,0:T(2,128)}, u32[]{:S(2)}) copy-start(f32[2,2048]{1,0:T(2,128)} %refs_4_.3) | copy-start | bytes 49156
  12.3 1.6 %copy-start.2 = (f32[2,2048]{1,0:T(2,128)S(1)}, f32[2,2048]{1,0:T(2,128)}, u32[]{:S(2)}) copy-start(f32[2,2048]{1,0:T(2,128)} %refs_5_.1) | copy-start | bytes 49156
  12.3 1.6 %copy-start.5 = (s32[2,2048]{1,0:T(2,128)S(1)}, s32[2,2048]{1,0:T(2,128)}, u32[]{:S(2)}) copy-start(s32[2,2048]{1,0:T(2,128)} %refs_1_.1) | copy-start | bytes 49156
  13.9 5.2 %copy-start.4 = (s32[8,128]{1,0:T(8,128)S(1)}, s32[8,128]{1,0:T(8,128)}, u32[]{:S(2)}) copy-start(s32[8,128]{1,0:T(8,128)} %land_ref.5) | copy-start | bytes 12292
  22.1 19.7 %collective-permute-start.6 = (bf16[5,8,48,128]{3,2,1,0:T(8,128)(2,1)S(1)}, bf16[5,8,48,128]{3,2,1,0:T(8,128)(2,1)S(1)}, u32[]{:S(2)}, u32[]{:S(2)}) collective-permute-start(bf16[5,8,48,128]{3,2,1,0:T(8,128)(2,1)S(1)} %get-tuple-element.46), channel_id=1, source_target_pairs={{0,16},{1,17},{2,18},{3,19},{4,20},{5,21},{6,22},{7,23},{8,24},{9,... | collective-permute-start | bytes 1474568 | tf_op jit(solution)/shard_map/ppermute | solution.py:474
  25.9 15.9 %collective-permute-start.5 = (bf16[5,4,48,128]{3,2,1,0:T(8,128)(2,1)S(1)}, bf16[5,4,48,128]{3,2,1,0:T(8,128)(2,1)S(1)}, u32[]{:S(2)}, u32[]{:S(2)}) collective-permute-start(bf16[5,4,48,128]{3,2,1,0:T(8,128)(2,1)S(1)} %get-tuple-element.45), channel_id=1, source_target_pairs={{16,0},{17,1},{18,2},{19,3},{20,4},{21,5},{22,6},{23,7},{24,8},{25... | collective-permute-start | bytes 737288 | tf_op jit(solution)/shard_map/ppermute | solution.py:474
  27.2 14.6 %collective-permute-start.3 = (bf16[18,48,128]{2,1,0:T(8,128)(2,1)S(1)}, bf16[18,48,128]{2,1,0:T(8,128)(2,1)S(1)}, u32[]{:S(2)}, u32[]{:S(2)}) collective-permute-start(bf16[18,48,128]{2,1,0:T(8,128)(2,1)S(1)} %get-tuple-element.39), channel_id=1, source_target_pairs={{0,1},{1,2},{2,3},{3,4},{4,5},{5,6},{6,7},{7,8},{8,9},{9,10},{10,1... | collective-permute-start | bytes 663560 | tf_op jit(solution)/shard_map/ppermute | solution.py:479
  27.2 14.5 %collective-permute-start.4 = (bf16[18,48,128]{2,1,0:T(8,128)(2,1)S(1)}, bf16[18,48,128]{2,1,0:T(8,128)(2,1)S(1)}, u32[]{:S(2)}, u32[]{:S(2)}) collective-permute-start(bf16[18,48,128]{2,1,0:T(8,128)(2,1)S(1)} %get-tuple-element.40), channel_id=1, source_target_pairs={{0,15},{1,0},{2,1},{3,2},{4,3},{5,4},{6,5},{7,6},{8,7},{9,8},{10,9... | collective-permute-start | bytes 663560 | tf_op jit(solution)/shard_map/ppermute | solution.py:479

commit v3 on v2

--- a/solution.py
+++ b/solution.py
@@ -4,6 +4,7 @@
 from jax.experimental import pallas as pl
 from jax.experimental.pallas import tpu as pltpu
 from jax.sharding import PartitionSpec as P
+
 
 thermal_lin = 0.2
 thermal_quad = 0.02
@@ -79,11 +80,30 @@
     return pl.ds(pl.multiple_of(block * size, size), size)
 
 
+def even_tile():
+    return lax.axis_index("space") % 2 == 0
+
+
+def edges(width):
+    even = even_tile()
+    pair = (jnp.where(even, width - 1, 0), jnp.where(even, width - 2, 1))
+    link = (jnp.where(even, 0, width - 1), jnp.where(even, 1, width - 2))
+    return pair, link
+
+
+def halos(width):
+    even = even_tile()
+    pair = (jnp.where(even, width + 2, 1), jnp.where(even, width + 3, 0))
+    link = (jnp.where(even, 1, width + 2), jnp.where(even, 0, width + 3))
+    return pair, link
+
+
 def load_kernel(
-    error_ref, inc_hbm, traj_hbm, mult_hbm, misfit_hbm, land_ref,
-    inc_ref, traj_ref, mult_ref, misfit_ref, up_ref, dn_ref, edge_ref, inner_ref, damp_ref, h_s, sems,
+    error_hbm, inc_hbm, traj_hbm, mult_hbm, misfit_hbm, land_hbm,
+    inc_ref, traj_ref, mult_ref, misfit_ref, land_ref, pair_ref, link_ref, edge_ref, inner_ref, damp_ref,
+    error_ref, h_s, sems, small_sems,
 ):
-    subs, fields, width, levels, latitude = inc_ref.shape[0], inc_ref.shape[1], land_ref.shape[0], up_ref.shape[1], land_ref.shape[1]
+    subs, fields, width, levels, latitude = inc_ref.shape[0], inc_ref.shape[1], land_ref.shape[0], pair_ref.shape[1], land_ref.shape[1]
     level = lax.broadcasted_iota(jnp.int32, (LB, latitude), 0)
 
     def copies(b):
@@ -98,10 +118,18 @@
         ]
         return first, second
 
-    for part in range(2):
-        for b in range(levels // LB):
-            for c in copies(b)[part]:
-                c.start()
+    land_copy = pltpu.make_async_copy(land_hbm, land_ref, small_sems.at[0])
+    error_copy = pltpu.make_async_copy(error_hbm, error_ref, small_sems.at[1])
+    for b in range(levels // LB):
+        for c in copies(b)[0]:
+            c.start()
+    land_copy.start()
+    error_copy.start()
+    for b in range(levels // LB):
+        for c in copies(b)[1]:
+            c.start()
+    land_copy.wait()
+    pair_edge, link_edge = edges(width)
 
     def ahead(b):
         for c in copies(b)[0]:
@@ -110,7 +138,7 @@
             for j in range(2):
                 for s in range(2):
                     h_s[2 * j + s] = traj_ref[k, j, s, native(b, width), :].astype(F32)
-            for out, near, far in ((up_ref, width - 1, width - 2), (dn_ref, 0, 1)):
+            for out, (near, far) in ((pair_ref, pair_edge), (link_ref, link_edge)):
                 base = AHEAD * k
                 for col, planes, q in ((near, NEAR, QN), (far, FAR, QF)):
                     vals = {f: rows_of(inc_ref, (k, f), b, col, width) for f in planes}
@@ -120,8 +148,8 @@
                     out[base + q, at(b), :] = (vals[PR] + gravity * (kt * vals[TE] + ks * vals[SA])).astype(BF16)
                 out[base + H0, at(b), :] = rows_of(h_s, (2,), 0, near, width).astype(BF16)
                 out[base + H1, at(b), :] = rows_of(h_s, (3,), 0, near, width).astype(BF16)
-        for out, near in ((up_ref, width - 1), (dn_ref, 0)):
-            mask = land_ref[near : near + 1, :].astype(F32)
+        for out, (near, _) in ((pair_ref, pair_edge), (link_ref, link_edge)):
+            mask = land_ref[pl.ds(near, 1), :].astype(F32)
             out[AHEAD * subs, at(b), :] = jnp.broadcast_to(mask, (LB, mask.shape[1])).astype(BF16)
 
     def partial(b):
@@ -144,20 +172,24 @@
                     edge_ref[f, c if c < 2 else c - width + 4, at(b), :] = value
 
     blocks_of(levels, ahead)
+    error_copy.wait()
     blocks_of(levels, partial)
 
 
-def prepare_kernel(traj_ref, mult_hbm, misfit_hbm, dens_ref, mult_ref, misfit_ref, h_s, sems):
-    subs, width, levels = dens_ref.shape[0], dens_ref.shape[3], dens_ref.shape[4]
+def sensor_kernel(
+    inc_ref, cell_ref, mult_ref, innov_ref, err_ref, traj_ref, mult_hbm, misfit_hbm,
+    obs_ref, spread_ref, sum_ref, dens_ref, mult1_ref, misfit1_ref, hot_s, acc_s, h_s, sems, *, columns,
+):
+    width, levels = dens_ref.shape[3], dens_ref.shape[4]
     copies = [
-        pltpu.make_async_copy(mult_hbm.at[1], mult_ref, sems.at[0]),
-        pltpu.make_async_copy(misfit_hbm.at[1], misfit_ref, sems.at[1]),
+        pltpu.make_async_copy(mult_hbm.at[1], mult1_ref, sems.at[0]),
+        pltpu.make_async_copy(misfit_hbm.at[1], misfit1_ref, sems.at[1]),
     ]
     for c in copies:
         c.start()
 
-    def body(b):
-        for k in range(subs):
+    def density(b):
+        for k in range(inc_ref.shape[0]):
             for j in range(2):
                 for s in range(2):
                     h_s[s] = traj_ref[k, j, s, native(b, width), :].astype(F32)
@@ -166,16 +198,10 @@
                     dens_ref[k, j, 0, c, at(b), :] = kt
                     dens_ref[k, j, 1, c, at(b), :] = ks
 
-    blocks_of(levels, body)
-    for c in copies:
-        c.wait()
-
-
-def sensor_kernel(inc_ref, cell_ref, mult_ref, innov_ref, err_ref, obs_ref, spread_ref, sum_ref, hot_s, acc_s, *, width, columns):
+    blocks_of(levels, density)
     subs, rows, latitude = inc_ref.shape[0], 2 * inc_ref.shape[2], inc_ref.shape[3]
     nobs = cell_ref.shape[1]
-    peers, share = obs_ref.shape[0], obs_ref.shape[1]
-    tiles = subs * nobs // (128 * share)
+    share = obs_ref.shape[1]
     blk = 512
     small = 32
     lat_bits = latitude.bit_length() - 1
@@ -217,34 +243,41 @@
                 acc_s[...] += add
             for i in range(blk // 128):
                 g = (k * nobs + b * blk) // 128 + i
-                for t in range(peers // tiles):
-                    obs_ref[t * tiles + g // share, g % share : g % share + 1, :] = seen[:, i * 128 : (i + 1) * 128]
+                obs_ref[g // share, g % share : g % share + 1, :] = seen[:, i * 128 : (i + 1) * 128]
         spread_ref[k] = acc_s[:, :latitude] + acc_s[:, latitude:]
     sum_ref[...] = total
-
-
-def keeper(axis):
-    return jnp.where(lax.axis_index(axis) < lax.axis_size(axis) - 1, 1.0, 0.0).astype(F32)
+    for c in copies:
+        c.wait()
+
+
+def team_flags():
+    team = lax.axis_index("tm")
+    follows = jnp.where(team < lax.axis_size("tm") - 1, 1.0, 0.0).astype(F32)
+    return follows, jnp.where(team > 0, 1.0, 0.0).astype(F32)
 
 
 def forward_kernel(
-    inc_ref, dens_ref, land_ref, left_ref, right_ref, mult_ref, misfit_ref, damp_ref, edge_ref, sensor_ref,
-    fwd_ref, send_ref, mult_out, up_ref, dn_ref, sum_ref, x_s, y_s, q_s,
+    inc_ref, dens_ref, land_ref, pair_ref, link_ref, mult_ref, misfit_ref, damp_ref, edge_ref, sensor_ref,
+    fwd_ref, send_ref, mult_out, back_pair_ref, back_link_ref, sum_ref, x_s, y_s, q_s, side_s,
 ):
     subs, fields, width, latitude = inc_ref.shape[0], inc_ref.shape[1], land_ref.shape[0], land_ref.shape[1]
     levels = fwd_ref.shape[2]
     lanes = Rows(latitude)
-    keep = keeper("tm")
+    keep, _ = team_flags()
     centre = 1.0 - 4.0 * mixing
+    even = even_tile()
+    pair_halo, link_halo = halos(width)
     sum_ref[...] = jnp.zeros_like(sum_ref)
     sum_ref[0:1, :] = jnp.full((1, latitude), jnp.sum(sensor_ref[...]) / latitude, F32)
 
     def body(b):
+        def beyond(c, plane):
+            pair, link = pair_ref[plane, at(b), :].astype(F32), link_ref[plane, at(b), :].astype(F32)
+            return jnp.where(even, link, pair) if c < 0 else jnp.where(even, pair, link)
+
         def mask_at(c):
-            if c < 0:
-                return left_ref[AHEAD * subs, at(b), :].astype(F32)
-            if c >= width:
-                return right_ref[AHEAD * subs, at(b), :].astype(F32)
+            if c < 0 or c >= width:
+                return beyond(c, AHEAD * subs)
             return jnp.broadcast_to(land_ref[c : c + 1, :].astype(F32), (LB, latitude))
 
         total = jnp.zeros((LB, latitude), F32)
@@ -255,7 +288,7 @@
                     x_s[f, c + 2] = rows_of(inc_ref, (k, f), b, c, width)
                 kt, ks = dens_ref[k, 0, 0, c, at(b), :], dens_ref[k, 0, 1, c, at(b), :]
                 q_s[c + 2] = x_s[PR, c + 2] + gravity * (kt * x_s[TE, c + 2] + ks * x_s[SA, c + 2])
-            for ref, near, far in ((left_ref, 1, 0), (right_ref, width + 2, width + 3)):
+            for ref, (near, far) in ((pair_ref, pair_halo), (link_ref, link_halo)):
                 for f, p in NEAR.items():
                     x_s[f, near] = ref[base + p, at(b), :].astype(F32)
                 for f, p in FAR.items():
@@ -289,8 +322,7 @@
                 if inside:
                     kt, ks = dens_ref[k, 1, 0, c, at(b), :], dens_ref[k, 1, 1, c, at(b), :]
                 else:
-                    ref = left_ref if c < 0 else right_ref
-                    kt, ks = dens(ref[base + H0, at(b), :].astype(F32), ref[base + H1, at(b), :].astype(F32))
+                    kt, ks = dens(beyond(c, base + H0), beyond(c, base + H1))
                 y_s[5, c + 2] = new[PR] + gravity * (kt * new[TE] + ks * new[SA])
             for c in range(width):
                 mask = mask_at(c)
@@ -315,28 +347,33 @@
                         after = mask * after
                     where = BACK * k
                     if c == width - 1:
-                        up_ref[where + NEAR[f], at(b), :] = after.astype(BF16)
+                        side_s[1, where + NEAR[f]] = after
                     if c == width - 2 and f != V:
-                        up_ref[where + FAR[f], at(b), :] = after.astype(BF16)
+                        side_s[1, where + FAR[f]] = after
                     if c == 0:
-                        dn_ref[where + NEAR[f], at(b), :] = after.astype(BF16)
+                        side_s[0, where + NEAR[f]] = after
                     if c == 1 and f != V:
-                        dn_ref[where + FAR[f], at(b), :] = after.astype(BF16)
+                        side_s[0, where + FAR[f]] = after
+        up = jnp.where(even, 1, 0)
+        for p in range(BACK * subs):
+            back_pair_ref[p, at(b), :] = side_s[up, p].astype(BF16)
+            back_link_ref[p, at(b), :] = side_s[1 - up, p].astype(BF16)
         sum_ref[...] += total
 
     blocks_of(levels, body)
 
 
 def adjoint_kernel(
-    inc_ref, dens_ref, land_ref, left_ref, right_ref, backl_ref, backr_ref, mult_ref, misfit_ref, damp_ref,
+    inc_ref, dens_ref, land_ref, pair_ref, link_ref, back_pair_ref, back_link_ref, mult_ref, misfit_ref, damp_ref,
     fwd_ref, mnext_ref, edge_ref, inner_ref, prev_ref, spread_ref, sum_ref, seen_ref,
     mult_out, grad_ref, fin_ref, x_s, y_s, acc_s,
 ):
     subs, fields, width, latitude = dens_ref.shape[0], mult_ref.shape[0], land_ref.shape[0], land_ref.shape[1]
-    levels = fwd_ref.shape[2]
     lanes = Rows(latitude)
-    keep = keeper("tm")
+    keep, precede = team_flags()
     centre = 1.0 - 4.0 * mixing
+    even = even_tile()
+    pair_halo, link_halo = halos(width)
     b = pl.program_id(0)
 
     @pl.when(b == 0)
@@ -344,11 +381,13 @@
         acc_s[...] = jnp.zeros_like(acc_s)
 
     def body():
+        def beyond(c, plane):
+            pair, link = pair_ref[plane, at(b), :].astype(F32), link_ref[plane, at(b), :].astype(F32)
+            return jnp.where(even, link, pair) if c < 0 else jnp.where(even, pair, link)
+
         def mask_at(c):
-            if c < 0:
-                return left_ref[AHEAD * subs, at(b), :].astype(F32)
-            if c >= width:
-                return right_ref[AHEAD * subs, at(b), :].astype(F32)
+            if c < 0 or c >= width:
+                return beyond(c, AHEAD * subs)
             return jnp.broadcast_to(land_ref[c : c + 1, :].astype(F32), (LB, latitude))
 
         misfit_total = jnp.zeros((LB, latitude), F32)
@@ -366,7 +405,7 @@
                     else:
                         value = mnext_ref[f, c, at(b), :]
                     x_s[f, c + 2] = mask * value
-            for ref, near, far in ((backl_ref, 1, 0), (backr_ref, width + 2, width + 3)):
+            for ref, (near, far) in ((back_pair_ref, pair_halo), (back_link_ref, link_halo)):
                 for f, p in NEAR.items():
                     x_s[f, near] = ref[BACK * k + p, at(b), :].astype(F32)
                 for f, p in FAR.items():
@@ -389,10 +428,7 @@
                 if inside:
                     kt, ks = dens_ref[k, 1, 0, c, at(b), :], dens_ref[k, 1, 1, c, at(b), :]
                 else:
-                    ref = left_ref if c < 0 else right_ref
-                    kt, ks = dens(
-                        ref[AHEAD * k + H0, at(b), :].astype(F32), ref[AHEAD * k + H1, at(b), :].astype(F32)
-                    )
+                    kt, ks = dens(beyond(c, AHEAD * k + H0), beyond(c, AHEAD * k + H1))
                 mask = mask_at(c)
                 new = back(x_s, c + 2, kt, ks, inside)
                 for f in range(5):
@@ -406,7 +442,7 @@
                         resid = (
                             rows_of(misfit_ref, (f,), b, c, width)
                             - damp_ref[f, at(b), :] * mult
-                            - (rows_of(inc_ref, (0, f), b, c, width) - prev_ref[f, c, at(b), :].astype(F32))
+                            - (rows_of(inc_ref, (0, f), b, c, width) - precede * prev_ref[f, c, at(b), :].astype(F32))
                         )
                         misfit_total = misfit_total + resid * resid
                         value = mult + relaxation * resid
@@ -430,16 +466,14 @@
         grad_sum = jnp.sum(acc_s[1])
         lane = lax.broadcasted_iota(jnp.int32, (1, 128), 1)
         scalars = jnp.where(lane == 0, misfit_sum, jnp.where(lane == 1, grad_sum, 0.0))
-        tiles = lax.axis_size("space")
-        mine = seen_ref[pl.ds(lax.axis_index("tm") * tiles, tiles)]
-        pieces = jnp.sum(mine, axis=0)
+        pieces = jnp.sum(seen_ref[...], axis=0)
         peers = fin_ref.shape[0]
         for i in range(peers):
             fin_ref[i, 0:1, :] = scalars
             fin_ref[i, 1:, :] = pieces
 
 
-def step_kernel(recv_ref, inc_ref, grad_ref, mult_ref, innov_ref, err_ref, out_ref, next_ref, *, steps):
+def step_kernel(recv_ref, inc_ref, grad_ref, mult_ref, innov_ref, err_ref, out_ref, next_ref):
     parts = recv_ref[:, 0, :]
     sums = jnp.sum(parts, axis=0, keepdims=True)
     lane = lax.broadcasted_iota(jnp.int32, sums.shape, 1)
@@ -470,16 +504,16 @@
 
 def shifted(shard, axis, by):
     peers = lax.axis_size(axis)
-    pairs = [(i, i + by) for i in range(peers) if 0 <= i + by < peers]
-    return lax.ppermute(shard, axis, pairs)
-
-
-def around(shard, axis, by):
+    return lax.ppermute(shard, axis, [(i, (i + by) % peers) for i in range(peers)])
+
+
+def swapped(shard, axis, pair):
     peers = lax.axis_size(axis)
-    return lax.ppermute(shard, axis, [(i, (i + by) % peers) for i in range(peers)])
-
-
-def on_device(
+    ahead = 0 if pair else 1
+    return lax.ppermute(shard, axis, [(i, (i + (1 if i % 2 == ahead else -1)) % peers) for i in range(peers)])
+
+
+def within(
     increment, multiplier, sensor_multiplier, misfit, innovation,
     model_error, sensor_error, trajectory, land_sea, sensor_cells,
 ):
@@ -488,7 +522,7 @@
     teams, tiles = lax.axis_size("tm"), lax.axis_size("space")
     peers = teams * tiles
     share = subs * nobs // (128 * tiles)
-    assert fields == 5 and trajectory.shape[1] == 2 and subs == 2 and levels % LB == 0 and width >= 4
+    assert tiles % 2 == 0 and fields == 5 and trajectory.shape[1] == 2 and subs == 2 and levels % LB == 0 and width >= 4
     assert latitude == 128 and (width * tiles) & (width * tiles - 1) == 0 and nobs % 512 == 0
     assert share * 128 * tiles == subs * nobs and (2 * levels * width) % 32 == 0
     rows = levels * width
@@ -499,18 +533,15 @@
     traj = slow(trajectory.reshape(subs, 2, 2, rows, latitude))
     mult = slow(multiplier.reshape(native_shape))
     mis = slow(misfit.reshape(native_shape))
-    land = fast(land_sea)
     cells, sen_m, sen_i, sen_e = (fast(x) for x in (sensor_cells, sensor_multiplier, innovation, sensor_error))
     vmem = pl.BlockSpec(memory_space=pltpu.VMEM)
-    smem = pl.BlockSpec(memory_space=pltpu.SMEM)
     hbm = pl.BlockSpec(memory_space=pltpu.HBM)
     scr = lambda *s: pltpu.VMEM(s, F32)
     limit = pltpu.CompilerParams(vmem_limit_bytes=VMEM_LIMIT)
 
-    def call(kernel, name, outs, scratch, *args, specs=None):
+    def call(kernel, outs, scratch, *args, specs=None):
         return pl.pallas_call(
             kernel,
-            name=name,
             in_specs=specs or [vmem] * len(args),
             out_specs=[vmem] * len(outs),
             out_shape=[pltpu.VMEM(s, d) for s, d in outs],
@@ -520,50 +551,56 @@
 
     ahead = (subs * AHEAD + 1, levels, latitude)
     one = native_shape[1:]
-    inc, traj, mult0, mis0, up, dn, edge, inner, damp = call(
-        load_kernel, "load",
+    inc, traj, mult0, mis0, land, pair, link, edge, inner, damp = call(
+        load_kernel,
         [
-            (native_shape, F32), (traj.shape, BF16), (one, F32), (one, F32), (ahead, BF16), (ahead, BF16),
+            (native_shape, F32), (traj.shape, BF16), (one, F32), (one, F32), (land_sea.shape, jnp.int32),
+            (ahead, BF16), (ahead, BF16),
             ((fields, 4, levels, latitude), BF16),
             ((fields, width - 4, levels, latitude), BF16),
             ((fields, levels, latitude), F32),
         ],
-        [scr(4, LB * width, latitude), pltpu.SemaphoreType.DMA((4, levels // LB))],
-        model_error, inc, traj, mult, mis, land,
-        specs=[smem] + [hbm] * 4 + [vmem],
+        [
+            pltpu.SMEM(model_error.shape, F32), scr(4, LB * width, latitude),
+            pltpu.SemaphoreType.DMA((4, levels // LB)), pltpu.SemaphoreType.DMA((2,)),
+        ],
+        slow(model_error), inc, traj, mult, mis, slow(land_sea),
+        specs=[hbm] * 6,
     )
-    left = fast(around(up, "space", 1))
-    right = fast(around(dn, "space", -1))
+    link_in = fast(swapped(link, "space", False))
+    pair_in = fast(swapped(pair, "space", True))
     edge_in = fast(shifted(edge, "tm", -1))
     inner_in = fast(shifted(inner, "tm", -1))
 
-    density, mult1, mis1 = call(
-        prepare_kernel, "prepare",
-        [((subs, 2, 2, width, levels, latitude), F32), (one, F32), (one, F32)],
-        [scr(2, LB * width, latitude), pltpu.SemaphoreType.DMA((2,))],
-        traj, mult, mis,
-        specs=[vmem, hbm, hbm],
-    )
-
-    seen, spread, sensor_sum = call(
-        lambda *refs: sensor_kernel(*refs, width=width, columns=width * tiles), "sensor",
-        [((peers, share, 128), F32), ((subs, 2 * rows, latitude), F32), ((1, 512), F32)],
-        [pltpu.VMEM((2 * rows, 512), BF16), scr(2 * rows, 2 * latitude)],
-        inc, cells, sen_m, sen_i, sen_e,
+    seen, spread, sensor_sum, density, mult1, mis1 = call(
+        lambda *refs: sensor_kernel(*refs, columns=width * tiles),
+        [
+            ((tiles, share, 128), F32), ((subs, 2 * rows, latitude), F32), ((1, 512), F32),
+            ((subs, 2, 2, width, levels, latitude), F32), (one, F32), (one, F32),
+        ],
+        [
+            pltpu.VMEM((2 * rows, 512), BF16), scr(2 * rows, 2 * latitude), scr(2, LB * width, latitude),
+            pltpu.SemaphoreType.DMA((2,)),
+        ],
+        inc, cells, sen_m, sen_i, sen_e, traj, mult, mis,
+        specs=[vmem] * 6 + [hbm] * 2,
     )
     spread = spread.reshape(subs, 2, rows, latitude)
-    seen_in = fast(lax.all_to_all(seen, ("tm", "space"), 0, 0))
+    seen_in = fast(lax.all_to_all(seen, "space", 0, 0))
 
     column = (fields, width, levels, latitude)
     behind = (subs * BACK, levels, latitude)
-    fwd, send, mnext, back_up, back_dn, sums = call(
-        forward_kernel, "forward",
+    fwd, send, mnext, back_pair, back_link, sums = call(
+        forward_kernel,
         [(column, F32), (column, BF16), (column, F32), (behind, BF16), (behind, BF16), ((LB, latitude), F32)],
-        [scr(5, width + 4, LB, latitude), scr(6, width + 4, LB, latitude), scr(width + 4, LB, latitude)],
-        inc, density, land, left, right, mult1, mis1, damp, edge_in, sensor_sum,
+        [
+            scr(5, width + 4, LB, latitude), scr(6, width + 4, LB, latitude), scr(width + 4, LB, latitude),
+            scr(2, subs * BACK, LB, latitude),
+        ],
+        inc, density, land, pair_in, link_in, mult1, mis1, damp, edge_in, sensor_sum,
     )
-    back_left = fast(around(back_up, "space", 1))
-    back_right = fast(around(back_dn, "space", -1))
+    back_link_in = fast(swapped(back_link, "space", False))
+    back_pair_in = fast(swapped(back_pair, "space", True))
     prev = fast(shifted(send, "tm", 1))
 
     block = pl.BlockSpec((subs, fields, LB * width, latitude), lambda i: (0, 0, i, 0))
@@ -581,7 +618,7 @@
         scratch_shapes=[scr(5, width + 4, LB, latitude), scr(5, width + 4, LB, latitude), scr(2, LB, latitude)],
         compiler_params=limit,
     )(
-        inc, density, land, left, right, back_left, back_right, mult0, mis0, damp,
+        inc, density, land, pair_in, link_in, back_pair_in, back_link_in, mult0, mis0, damp,
         fwd, mnext, edge_in, inner_in, prev, spread, sums, seen_in,
     )
     final = fast(lax.all_to_all(final, ("tm", "space"), 0, 0))
@@ -589,7 +626,7 @@
     steps = 4 if rows % 32 == 0 else 1
     size = rows // steps
     increment_next, sensor_next = pl.pallas_call(
-        lambda *refs: step_kernel(*refs, steps=steps),
+        lambda *refs: step_kernel(*refs),
         name="step",
         grid=(steps,),
         in_specs=[vmem] * 6,
@@ -621,7 +658,7 @@
         P("tm", None),
     )
     return jax.shard_map(
-        on_device,
+        within,
         mesh=mesh,
         in_specs=placed,
         out_specs=(state, state, P("tm", None)),

time: 57.6 us -> 57.3 us (level)
  starting transfers between devices: 16.4 us -> 13.5 us
  waiting for transfers between devices: 0.86 us -> 3.12 us
  blocking collectives: 19.2 us -> 21.3 us
  local copies, waits for them, and re-layouts: 1.4 us -> 0.02 us
    ppermute x7, starting transfers between devices: 16.4 us -> 13.5 us  [the longest x4 9.93 us: swapped(): lax.ppermute(shard, axis, [(i, (i + (1 if i % 2 == ahead else -1)) % peer...]
    ppermute x7, waiting for transfers between devices: 0.86 us -> 3.12 us  [the longest x3 3.11 us: shifted(): lax.ppermute(shard, axis, [(i, (i + by) % peers) for i in range(peers)])]
    all_to_all x2, blocking collectives: 19.2 us -> 21.3 us  [the longest x1 12.3 us: within(): final = fast(lax.all_to_all(final, ('tm', 'space'), 0, 0))]
    unnamed x14 -> x8, local copies, waits for them, and re-layouts: 1.4 us -> 0.02 us
    pallas_call x6 -> x5, Pallas kernels: 18.7 us -> 18.4 us  [the longest x3 11.7 us: call(): pl.pallas_call(kernel, in_specs=specs or [vmem] * len(args), out_specs=[v...]
  transfers between devices with their start and end apart: 7 -> 7, of which waited for: 1 -> 1; matrix products, arithmetic and copies ran while one was open for 0% -> 0% of each run, Pallas kernels for 10% -> 9%
where the time goes in v3:
time: 57.3 us; the launch traced here: 57.1 us
  blocking collectives  21.3 us (37%)
  Pallas kernels  18.4 us (32%)
  starting transfers between devices  13.5 us (24%)
  waiting for transfers between devices  3.12 us (5%)
  between operations  0.72 us (1%)
    all_to_all x1, blocking collectives, within(): final = fast(lax.all_to_all(final, ('tm', 'space'), 0, 0))  12.3 us
    pallas_call x3, Pallas kernels, call(): pl.pallas_call(kernel, in_specs=specs or [vmem] * len(args), out_specs=[v...  11.7 us
    ppermute x4, starting transfers between devices, swapped(): lax.ppermute(shard, axis, [(i, (i + (1 if i % 2 == ahead else -1)) % peer...  9.93 us
    all_to_all x1, blocking collectives, within(): seen_in = fast(lax.all_to_all(seen, 'space', 0, 0))  9.06 us
    pallas_call x1, Pallas kernels, within(): pl.pallas_call(adjoint_kernel, name='adjoint', grid=(levels // LB,), in_s...  4.63 us
    ppermute x3, starting transfers between devices, shifted(): lax.ppermute(shard, axis, [(i, (i + by) % peers) for i in range(peers)])  3.58 us
    ppermute x3, waiting for transfers between devices, shifted(): lax.ppermute(shard, axis, [(i, (i + by) % peers) for i in range(peers)])  3.11 us
    pallas_call x1, Pallas kernels, within(): pl.pallas_call(lambda *refs: step_kernel(*refs), name='step', grid=(steps...  2.05 us
  transfers between devices with their start and end apart: 7, of which 1 were waited for; matrix products, arithmetic and copies ran while one was open for 0% of the time, Pallas kernels for 9%

profile of v3, /device:TPU:0, one launch (start us, length us, event | category | flops | bytes accessed | tf_op | source)
XLA Modules:
  0.0 57.1 jit_solution(11824782176877469331)
XLA Ops:
  0.6 0.0 copy-start
  0.6 0.0 copy-start.1
  0.7 0.0 copy-start.2
  0.7 0.0 copy-start.3
  0.7 3.4 %shard_map.121 = (f32[2,5,384,128]{3,2,1,0:T(8,128)S(1)}, bf16[2,2,2,384,128]{4,3,2,1,0:T(8,128)(2,1)S(1)}, f32[5,384,128]{2,1,0:T(8,128)S(1)}, f32[5,384,128]{2...) custom-call(f32[5,48]{1,0:T(8,128)} %error_hbm.1, ...), custom_call_target="tpu_custom_call" | custom-call | tf_op jit(solution)/shard_map/pallas_call | solution.py:543
  4.1 0.6 collective-permute-start
  4.6 5.7 %collective-permute-start.1 = (bf16[27,48,128]{2,1,0:T(8,128)(2,1)S(1)}, bf16[27,48,128]{2,1,0:T(8,128)(2,1)S(1)}, u32[]{:S(2)}, u32[]{:S(2)}) collective-permute-start(bf16[27,48,128]{2,1,0:T(8,128)(2,1)S(1)} %get-tuple-element.35), channel_id=1, source_target_pairs={{0,15},{1,2},{2,1},{3,4},{4,3},{5,6},{6,5},{7,8},{8,7},{9,10},{10,... | collective-permute-start | bytes 995336 | tf_op jit(solution)/shard_map/ppermute | solution.py:513
  10.3 1.5 %collective-permute-start.2 = (bf16[5,4,48,128]{3,2,1,0:T(8,128)(2,1)S(1)}, bf16[5,4,48,128]{3,2,1,0:T(8,128)(2,1)S(1)}, u32[]{:S(2)}, u32[]{:S(2)}) collective-permute-start(bf16[5,4,48,128]{3,2,1,0:T(8,128)(2,1)S(1)} %get-tuple-element.39), channel_id=1, source_target_pairs={{0,16},{16,0},{1,17},{17,1},{2,18},{18,2},{3,19},{19,3},{4,20},{20... | collective-permute-start | bytes 737288 | tf_op jit(solution)/shard_map/ppermute | solution.py:507
  11.8 0.0 copy-done
  11.8 0.0 copy-done.1
  11.8 0.0 copy-done.2
  11.8 0.0 copy-done.3
  11.8 4.9 %shard_map.122 = (f32[16,2,128]{2,1,0:T(2,128)S(1)}, f32[2,768,128]{2,1,0:T(8,128)S(1)}, f32[1,512]{1,0:T(1,128)S(1)}, f32[2,2,2,8,48,128]{5,4,3,2,1,0:T(8,128)S...) custom-call(f32[2,5,384,128]{3,2,1,0:T(8,128)S(1)} %get-tuple-element.30.refs_0_.inc_ref.refs_1_, ...), custom_call_target="tpu_custom_call" | custom-call | tf_op jit(solution)/shard_map/pallas_call | solution.py:543
  16.7 0.0 collective-permute-done.2.edge_ref
  16.7 0.0 collective-permute-done.pair_ref
  16.7 0.0 collective-permute-done.1.link_ref
  16.8 3.4 %shard_map.123 = (f32[5,8,48,128]{3,2,1,0:T(8,128)S(1)}, bf16[5,8,48,128]{3,2,1,0:T(8,128)(2,1)S(1)}, f32[5,8,48,128]{3,2,1,0:T(8,128)S(1)}, bf16[18,48,128]{2,1...) custom-call(f32[2,5,384,128]{3,2,1,0:T(8,128)S(1)} %get-tuple-element.30.refs_0_.inc_ref.refs_1_, ...), custom_call_target="tpu_custom_call" | custom-call | tf_op jit(solution)/shard_map/pallas_call | solution.py:543
  20.1 1.3 %collective-permute-start.6 = (bf16[5,8,48,128]{3,2,1,0:T(8,128)(2,1)S(1)}, bf16[5,8,48,128]{3,2,1,0:T(8,128)(2,1)S(1)}, u32[]{:S(2)}, u32[]{:S(2)}) collective-permute-start(bf16[5,8,48,128]{3,2,1,0:T(8,128)(2,1)S(1)} %get-tuple-element.48), channel_id=1, source_target_pairs={{0,16},{16,0},{1,17},{17,1},{2,18},{18,2},{3,19},{19,3},{4,20},{20... | collective-permute-start | bytes 1474568 | tf_op jit(solution)/shard_map/ppermute | solution.py:507
  21.4 0.8 %collective-permute-start.5 = (bf16[5,4,48,128]{3,2,1,0:T(8,128)(2,1)S(1)}, bf16[5,4,48,128]{3,2,1,0:T(8,128)(2,1)S(1)}, u32[]{:S(2)}, u32[]{:S(2)}) collective-permute-start(bf16[5,4,48,128]{3,2,1,0:T(8,128)(2,1)S(1)} %get-tuple-element.47), channel_id=1, source_target_pairs={{0,16},{16,0},{1,17},{17,1},{2,18},{18,2},{3,19},{19,3},{4,20},{20... | collective-permute-start | bytes 737288 | tf_op jit(solution)/shard_map/ppermute | solution.py:507
  22.2 0.0 collective-permute-start.3
  22.2 3.7 %collective-permute-start.4 = (bf16[18,48,128]{2,1,0:T(8,128)(2,1)S(1)}, bf16[18,48,128]{2,1,0:T(8,128)(2,1)S(1)}, u32[]{:S(2)}, u32[]{:S(2)}) collective-permute-start(bf16[18,48,128]{2,1,0:T(8,128)(2,1)S(1)} %get-tuple-element.42), channel_id=1, source_target_pairs={{0,15},{1,2},{2,1},{3,4},{4,3},{5,6},{6,5},{7,8},{8,7},{9,10},{10,... | collective-permute-start | bytes 663560 | tf_op jit(solution)/shard_map/ppermute | solution.py:513
  25.9 9.1 %all_to_all.10.seen_ref = f32[16,2,128]{2,1,0:T(2,128)S(1)} all-to-all(f32[16,2,128]{2,1,0:T(2,128)S(1)} %get-tuple-element.51), channel_id=1, replica_groups=mesh['tm'=2,'space'=16] {'space'}, dimensions={0} | all-to-all | bytes 32768 | tf_op jit(solution)/shard_map/all_to_all | solution.py:589
  35.0 3.1 %collective-permute-done.5.inner_ref = bf16[5,4,48,128]{3,2,1,0:T(8,128)(2,1)S(1)} collective-permute-done((bf16[5,4,48,128]{3,2,1,0:T(8,128)(2,1)S(1)}, bf16[5,4,48,128]{3,2,1,0:T(8,128)(2,1)S(1)}, u32[]{:S(2)}, u32[]{:S(2)}) %collective-permute-start.5) | collective-permute-done | bytes 245792 | tf_op jit(solution)/shard_map/ppermute | solution.py:507
  38.1 0.0 collective-permute-done.3.back_pair_ref
  38.1 0.0 collective-permute-done.4.back_link_ref
  38.1 0.0 collective-permute-done.6.prev_ref
  38.1 4.6 %adjoint.1 = (f32[2,5,384,128]{3,2,1,0:T(8,128)}, f32[2,5,384,128]{3,2,1,0:T(8,128)S(1)}, f32[32,3,128]{2,1,0:T(4,128)S(1)}) custom-call(f32[2,5,384,128]{3,2,1,0:T(8,128)S(1)} %get-tuple-element.30.refs_0_.inc_ref.refs_1_, f32[2,2,2,8,48,128]{5,4,3,2,1,0:T(8,128)S(1)} %get-tuple-element.32.dens_ref, s32[8,128]{1,0:T(8,128)S(1)} %get-tuple-element.33.land_ref, ...), custom_call_target="tpu_custom_call" | custom-call | tf_op jit(solution)/shard_map/adjoint/pallas_call | solution.py:607
  42.7 12.3 %all_to_all.11.refs_0_ = f32[32,3,128]{2,1,0:T(4,128)S(1)} all-to-all(f32[32,3,128]{2,1,0:T(4,128)S(1)} %get-tuple-element.52), channel_id=1, replica_groups=mesh['tm'=2,'space'=16] {'tm','space'}, dimensions={0} | all-to-all | bytes 98304 | tf_op jit(solution)/shard_map/all_to_all | solution.py:624
  55.0 2.1 %step.1 = (f32[2,5,384,128]{3,2,1,0:T(8,128)}, f32[2,2048]{1,0:T(2,128)}) custom-call(f32[32,3,128]{2,1,0:T(4,128)S(1)} %all_to_all.11.refs_0_, f32[2,5,384,128]{3,2,1,0:T(8,128)S(1)} %get-tuple-element.30.refs_0_.inc_ref.refs_1_, f32[2,5,384,128]{3,2,1,0:T(8,128)S(1)} %get-tuple-element.53.refs_2_, f32[2,2048]{1,0:T(2,128)S(1)} %copy-done, ...), custom_call_target="tpu_custom_call" | custom-call | tf_op jit(solution)/shard_map/step/pallas_call | solution.py:628
Async XLA Ops:
  0.6 11.2 %copy-start = (f32[2,2048]{1,0:T(2,128)S(1)}, f32[2,2048]{1,0:T(2,128)}, u32[]{:S(2)}) copy-start(f32[2,2048]{1,0:T(2,128)} %refs_3_.3) | copy-start | bytes 49156
  0.6 11.2 %copy-start.1 = (f32[2,2048]{1,0:T(2,128)S(1)}, f32[2,2048]{1,0:T(2,128)}, u32[]{:S(2)}) copy-start(f32[2,2048]{1,0:T(2,128)} %refs_4_.3) | copy-start | bytes 49156
  0.7 11.2 %copy-start.2 = (f32[2,2048]{1,0:T(2,128)S(1)}, f32[2,2048]{1,0:T(2,128)}, u32[]{:S(2)}) copy-start(f32[2,2048]{1,0:T(2,128)} %refs_5_.1) | copy-start | bytes 49156
  0.7 11.1 %copy-start.3 = (s32[2,2048]{1,0:T(2,128)S(1)}, s32[2,2048]{1,0:T(2,128)}, u32[]{:S(2)}) copy-start(s32[2,2048]{1,0:T(2,128)} %refs_1_.1) | copy-start | bytes 49156
  4.1 12.6 %collective-permute-start = (bf16[27,48,128]{2,1,0:T(8,128)(2,1)S(1)}, bf16[27,48,128]{2,1,0:T(8,128)(2,1)S(1)}, u32[]{:S(2)}, u32[]{:S(2)}) collective-permute-start(bf16[27,48,128]{2,1,0:T(8,128)(2,1)S(1)} %get-tuple-element.34), channel_id=1, source_target_pairs={{0,1},{1,0},{2,3},{3,2},{4,5},{5,4},{6,7},{7,6},{8,9},{9,8},{10,11... | collective-permute-start | bytes 995336 | tf_op jit(solution)/shard_map/ppermute | solution.py:513
  4.6 12.1 %collective-permute-start.1 = (bf16[27,48,128]{2,1,0:T(8,128)(2,1)S(1)}, bf16[27,48,128]{2,1,0:T(8,128)(2,1)S(1)}, u32[]{:S(2)}, u32[]{:S(2)}) collective-permute-start(bf16[27,48,128]{2,1,0:T(8,128)(2,1)S(1)} %get-tuple-element.35), channel_id=1, source_target_pairs={{0,15},{1,2},{2,1},{3,4},{4,3},{5,6},{6,5},{7,8},{8,7},{9,10},{10,... | collective-permute-start | bytes 995336 | tf_op jit(solution)/shard_map/ppermute | solution.py:513
  10.3 6.4 %collective-permute-start.2 = (bf16[5,4,48,128]{3,2,1,0:T(8,128)(2,1)S(1)}, bf16[5,4,48,128]{3,2,1,0:T(8,128)(2,1)S(1)}, u32[]{:S(2)}, u32[]{:S(2)}) collective-permute-start(bf16[5,4,48,128]{3,2,1,0:T(8,128)(2,1)S(1)} %get-tuple-element.39), channel_id=1, source_target_pairs={{0,16},{16,0},{1,17},{17,1},{2,18},{18,2},{3,19},{19,3},{4,20},{20... | collective-permute-start | bytes 737288 | tf_op jit(solution)/shard_map/ppermute | solution.py:507
  20.1 18.0 %collective-permute-start.6 = (bf16[5,8,48,128]{3,2,1,0:T(8,128)(2,1)S(1)}, bf16[5,8,48,128]{3,2,1,0:T(8,128)(2,1)S(1)}, u32[]{:S(2)}, u32[]{:S(2)}) collective-permute-start(bf16[5,8,48,128]{3,2,1,0:T(8,128)(2,1)S(1)} %get-tuple-element.48), channel_id=1, source_target_pairs={{0,16},{16,0},{1,17},{17,1},{2,18},{18,2},{3,19},{19,3},{4,20},{20... | collective-permute-start | bytes 1474568 | tf_op jit(solution)/shard_map/ppermute | solution.py:507
  21.4 16.7 %collective-permute-start.5 = (bf16[5,4,48,128]{3,2,1,0:T(8,128)(2,1)S(1)}, bf16[5,4,48,128]{3,2,1,0:T(8,128)(2,1)S(1)}, u32[]{:S(2)}, u32[]{:S(2)}) collective-permute-start(bf16[5,4,48,128]{3,2,1,0:T(8,128)(2,1)S(1)} %get-tuple-element.47), channel_id=1, source_target_pairs={{0,16},{16,0},{1,17},{17,1},{2,18},{18,2},{3,19},{19,3},{4,20},{20... | collective-permute-start | bytes 737288 | tf_op jit(solution)/shard_map/ppermute | solution.py:507
  22.2 15.9 %collective-permute-start.3 = (bf16[18,48,128]{2,1,0:T(8,128)(2,1)S(1)}, bf16[18,48,128]{2,1,0:T(8,128)(2,1)S(1)}, u32[]{:S(2)}, u32[]{:S(2)}) collective-permute-start(bf16[18,48,128]{2,1,0:T(8,128)(2,1)S(1)} %get-tuple-element.41), channel_id=1, source_target_pairs={{0,1},{1,0},{2,3},{3,2},{4,5},{5,4},{6,7},{7,6},{8,9},{9,8},{10,11... | collective-permute-start | bytes 663560 | tf_op jit(solution)/shard_map/ppermute | solution.py:513
  22.2 15.9 %collective-permute-start.4 = (bf16[18,48,128]{2,1,0:T(8,128)(2,1)S(1)}, bf16[18,48,128]{2,1,0:T(8,128)(2,1)S(1)}, u32[]{:S(2)}, u32[]{:S(2)}) collective-permute-start(bf16[18,48,128]{2,1,0:T(8,128)(2,1)S(1)} %get-tuple-element.42), channel_id=1, source_target_pairs={{0,15},{1,2},{2,1},{3,4},{4,3},{5,6},{6,5},{7,8},{8,7},{9,10},{10,... | collective-permute-start | bytes 663560 | tf_op jit(solution)/shard_map/ppermute | solution.py:513

commit v4 on v3

--- a/solution.py
+++ b/solution.py
@@ -25,7 +25,8 @@
 half = 0.5 * time_stride
 
 LB = 16
-VMEM_LIMIT = 16 * 1024 * 1024
+VMEM_LIMIT = 24 * 1024 * 1024
+SCATTER_ROWS = 256
 TE, SA, U, V, PR = range(5)
 F32 = jnp.float32
 BF16 = jnp.bfloat16
@@ -178,7 +179,7 @@
 
 def sensor_kernel(
     inc_ref, cell_ref, mult_ref, innov_ref, err_ref, traj_ref, mult_hbm, misfit_hbm,
-    obs_ref, spread_ref, sum_ref, dens_ref, mult1_ref, misfit1_ref, hot_s, acc_s, h_s, sems, *, columns,
+    obs_ref, spread_ref, sum_ref, dens_ref, mult1_ref, misfit1_ref, hot_s, right_s, h_s, sems, *, columns,
 ):
     width, levels = dens_ref.shape[3], dens_ref.shape[4]
     copies = [
@@ -224,8 +225,8 @@
             group = lax.shift_right_arithmetic(row, small.bit_length() - 1)
             for i in range(rows // small):
                 coarse = jnp.broadcast_to(jnp.where(group == i, 1.0, 0.0), (small, blk)).astype(BF16)
-                hot_s[i * small : (i + 1) * small, :] = coarse * fine
-            hot = hot_s[...]
+                hot_s[i * small : (i + 1) * small, span] = coarse * fine
+            hot = hot_s[:, span]
             here = lax.broadcasted_iota(jnp.int32, (latitude, blk), 0) == lat
             both = jnp.dot(left, hot, preferred_element_type=F32)
             seen = jnp.sum(jnp.where(here, both[:latitude] + both[latitude:], 0.0), axis=0, keepdims=True)
@@ -235,16 +236,16 @@
             total = total + jnp.where(owned, resid * resid, 0.0)
             nhi = nxt.astype(BF16).astype(F32)
             nlo = nxt - nhi
-            right = jnp.concatenate([jnp.where(here, nhi, 0.0), jnp.where(here, nlo, 0.0)], axis=0).astype(BF16)
-            add = lax.dot_general(hot, right, (((1,), (1,)), ((), ())), preferred_element_type=F32)
-            if b == 0:
-                acc_s[...] = add
-            else:
-                acc_s[...] += add
+            right_s[:latitude, span] = jnp.where(here, nhi, 0.0).astype(BF16)
+            right_s[latitude:, span] = jnp.where(here, nlo, 0.0).astype(BF16)
             for i in range(blk // 128):
                 g = (k * nobs + b * blk) // 128 + i
                 obs_ref[g // share, g % share : g % share + 1, :] = seen[:, i * 128 : (i + 1) * 128]
-        spread_ref[k] = acc_s[:, :latitude] + acc_s[:, latitude:]
+        part = SCATTER_ROWS if rows % SCATTER_ROWS == 0 else rows
+        for r in range(rows // part):
+            here = slice(r * part, (r + 1) * part)
+            both = lax.dot_general(hot_s[here, :], right_s[...], (((1,), (1,)), ((), ())), preferred_element_type=F32)
+            spread_ref[k, here, :] = both[:, :latitude] + both[:, latitude:]
     sum_ref[...] = total
     for c in copies:
         c.wait()
@@ -256,19 +257,93 @@
     return follows, jnp.where(team > 0, 1.0, 0.0).astype(F32)
 
 
-def forward_kernel(
-    inc_ref, dens_ref, land_ref, pair_ref, link_ref, mult_ref, misfit_ref, damp_ref, edge_ref, sensor_ref,
+def tangent(lanes, src, q, i, mask, with_v):
+    te, sa, u, v, pr = (src[f, i] for f in range(5))
+    stay, swap, thrust = (1.0 - 4.0 * mixing) * mask, mixing * mask, half * mask
+    heat = stay * te + swap * (src[TE, i + 1] + src[TE, i - 1] + lanes.both(te))
+    salt = stay * sa + swap * (src[SA, i + 1] + src[SA, i - 1] + lanes.both(sa))
+    east = mask * (u + lanes.rot * v) - thrust * (q[i + 1] - q[i - 1])
+    north = mask * (v - lanes.rot * u) - thrust * lanes.diff(q[i]) if with_v else None
+    if mixing == half:
+        around_p = lanes.up(pr - v) + lanes.down(pr + v)
+        around_p = around_p + (src[PR, i + 1] + src[PR, i - 1]) - (src[U, i + 1] - src[U, i - 1])
+        surf = stay * pr + swap * around_p
+    else:
+        surf = stay * pr + swap * (src[PR, i + 1] + src[PR, i - 1] + lanes.both(pr))
+        surf = surf - thrust * (src[U, i + 1] - src[U, i - 1] + lanes.diff(v))
+    return heat, salt, east, north, surf
+
+
+def fill(inc_ref, dens_ref, x_s, q_s, k, b, c, width):
+    for f in range(5):
+        x_s[f, c + 2] = rows_of(inc_ref, (k, f), b, c, width)
+    kt, ks = dens_ref[k, 0, 0, c, at(b), :], dens_ref[k, 0, 1, c, at(b), :]
+    q_s[c + 2] = x_s[PR, c + 2] + gravity * (kt * x_s[TE, c + 2] + ks * x_s[SA, c + 2])
+
+
+def renew(inc_ref, mult_ref, misfit_ref, damp_ref, new, f, b, c, width):
+    mult = rows_of(mult_ref, (f,), b, c, width)
+    resid = (
+        rows_of(misfit_ref, (f,), b, c, width)
+        - damp_ref[f, at(b), :] * mult
+        - (rows_of(inc_ref, (1, f), b, c, width) - new)
+    )
+    return mult + relaxation * resid, resid
+
+
+def interior_kernel(
+    inc_ref, dens_ref, land_ref, mult_ref, misfit_ref, damp_ref, sensor_ref,
+    mid_ref, fwd_ref, send_ref, mult_out, sum_ref, x_s, y_s, q_s,
+):
+    subs, fields, width, latitude = inc_ref.shape[0], inc_ref.shape[1], land_ref.shape[0], land_ref.shape[1]
+    levels = fwd_ref.shape[2]
+    lanes = Rows(latitude)
+    sum_ref[...] = jnp.zeros_like(sum_ref)
+    sum_ref[0:1, :] = jnp.full((1, latitude), jnp.sum(sensor_ref[...]) / latitude, F32)
+
+    def body(b):
+        mask_at = lambda c: jnp.broadcast_to(land_ref[c : c + 1, :].astype(F32), (LB, latitude))
+        total = jnp.zeros((LB, latitude), F32)
+        for k in reversed(range(subs)):
+            for c in range(width):
+                fill(inc_ref, dens_ref, x_s, q_s, k, b, c, width)
+            for c in range(1, width - 1):
+                new = tangent(lanes, x_s, q_s, c + 2, mask_at(c), True)
+                kt, ks = dens_ref[k, 1, 0, c, at(b), :], dens_ref[k, 1, 1, c, at(b), :]
+                new = new + (new[PR] + gravity * (kt * new[TE] + ks * new[SA]),)
+                for f in range(6):
+                    y_s[f, c + 2] = new[f]
+                    if c in (1, 2):
+                        mid_ref[k, f, c - 1, at(b), :] = new[f]
+                    if c in (width - 3, width - 2):
+                        mid_ref[k, f, c - width + 5, at(b), :] = new[f]
+            for c in range(2, width - 2):
+                new = tangent(lanes, y_s, y_s.at[5], c + 2, mask_at(c), True)
+                for f in range(fields):
+                    if k == 1:
+                        fwd_ref[f, c - 2, at(b), :] = new[f]
+                        send_ref[f, c - 2, at(b), :] = new[f].astype(BF16)
+                    else:
+                        value, resid = renew(inc_ref, mult_ref, misfit_ref, damp_ref, new[f], f, b, c, width)
+                        total = total + resid * resid
+                        mult_out[f, c - 2, at(b), :] = value
+        sum_ref[...] += total
+
+    blocks_of(levels, body)
+
+
+def edge_kernel(
+    inc_ref, dens_ref, land_ref, pair_ref, link_ref, mult_ref, misfit_ref, damp_ref, edge_ref, mid_ref, part_ref,
     fwd_ref, send_ref, mult_out, back_pair_ref, back_link_ref, sum_ref, x_s, y_s, q_s, side_s,
 ):
     subs, fields, width, latitude = inc_ref.shape[0], inc_ref.shape[1], land_ref.shape[0], land_ref.shape[1]
     levels = fwd_ref.shape[2]
     lanes = Rows(latitude)
     keep, _ = team_flags()
-    centre = 1.0 - 4.0 * mixing
     even = even_tile()
     pair_halo, link_halo = halos(width)
-    sum_ref[...] = jnp.zeros_like(sum_ref)
-    sum_ref[0:1, :] = jnp.full((1, latitude), jnp.sum(sensor_ref[...]) / latitude, F32)
+    outer = (0, 1, width - 2, width - 1)
+    sum_ref[...] = part_ref[...]
 
     def body(b):
         def beyond(c, plane):
@@ -283,11 +358,8 @@
         total = jnp.zeros((LB, latitude), F32)
         for k in reversed(range(subs)):
             base = AHEAD * k
-            for c in range(width):
-                for f in range(fields):
-                    x_s[f, c + 2] = rows_of(inc_ref, (k, f), b, c, width)
-                kt, ks = dens_ref[k, 0, 0, c, at(b), :], dens_ref[k, 0, 1, c, at(b), :]
-                q_s[c + 2] = x_s[PR, c + 2] + gravity * (kt * x_s[TE, c + 2] + ks * x_s[SA, c + 2])
+            for c in outer:
+                fill(inc_ref, dens_ref, x_s, q_s, k, b, c, width)
             for ref, (near, far) in ((pair_ref, pair_halo), (link_ref, link_halo)):
                 for f, p in NEAR.items():
                     x_s[f, near] = ref[base + p, at(b), :].astype(F32)
@@ -295,27 +367,12 @@
                     x_s[f, far] = ref[base + p, at(b), :].astype(F32)
                 q_s[near] = ref[base + QN, at(b), :].astype(F32)
                 q_s[far] = ref[base + QF, at(b), :].astype(F32)
-
-            def substep(src, q, i, mask, with_v):
-                te, sa, u, v, pr = (src[f, i] for f in range(5))
-                stay, swap = centre * mask, mixing * mask
-                thrust = half * mask
-                heat = stay * te + swap * (src[TE, i + 1] + src[TE, i - 1] + lanes.both(te))
-                salt = stay * sa + swap * (src[SA, i + 1] + src[SA, i - 1] + lanes.both(sa))
-                east = mask * (u + lanes.rot * v) - thrust * (q[i + 1] - q[i - 1])
-                north = mask * (v - lanes.rot * u) - thrust * lanes.diff(q[i]) if with_v else None
-                if mixing == half:
-                    around_p = lanes.up(pr - v) + lanes.down(pr + v)
-                    around_p = around_p + (src[PR, i + 1] + src[PR, i - 1]) - (src[U, i + 1] - src[U, i - 1])
-                    surf = stay * pr + swap * around_p
-                else:
-                    surf = stay * pr + swap * (src[PR, i + 1] + src[PR, i - 1] + lanes.both(pr))
-                    surf = surf - thrust * (src[U, i + 1] - src[U, i - 1] + lanes.diff(v))
-                return heat, salt, east, north, surf
-
-            for c in range(-1, width + 1):
+            for i, c in enumerate((1, 2, width - 3, width - 2)):
+                for f in range(6):
+                    y_s[f, c + 2] = mid_ref[k, f, i, at(b), :]
+            for c in (-1, 0, width - 1, width):
                 inside = 0 <= c < width
-                new = substep(x_s, q_s, c + 2, mask_at(c), inside)
+                new = tangent(lanes, x_s, q_s, c + 2, mask_at(c), inside)
                 for f in range(5):
                     if new[f] is not None:
                         y_s[f, c + 2] = new[f]
@@ -324,36 +381,23 @@
                 else:
                     kt, ks = dens(beyond(c, base + H0), beyond(c, base + H1))
                 y_s[5, c + 2] = new[PR] + gravity * (kt * new[TE] + ks * new[SA])
-            for c in range(width):
+            for i, c in enumerate(outer):
                 mask = mask_at(c)
-                new = substep(y_s, y_s.at[5], c + 2, mask, True)
+                new = tangent(lanes, y_s, y_s.at[5], c + 2, mask, True)
                 for f in range(fields):
-                    if k == subs - 1:
-                        fwd_ref[f, c, at(b), :] = new[f]
-                        send_ref[f, c, at(b), :] = new[f].astype(BF16)
-                        if c < 2 or c >= width - 2:
-                            got = edge_ref[f, c if c < 2 else c - width + 4, at(b), :].astype(F32)
-                            after = mask * (keep * (got + relaxation * new[f]))
+                    if k == 1:
+                        fwd_ref[f, i, at(b), :] = new[f]
+                        send_ref[f, i, at(b), :] = new[f].astype(BF16)
+                        got = edge_ref[f, i, at(b), :].astype(F32)
+                        after = mask * (keep * (got + relaxation * new[f]))
                     else:
-                        mult = rows_of(mult_ref, (f,), b, c, width)
-                        resid = (
-                            rows_of(misfit_ref, (f,), b, c, width)
-                            - damp_ref[f, at(b), :] * mult
-                            - (rows_of(inc_ref, (k + 1, f), b, c, width) - new[f])
-                        )
+                        value, resid = renew(inc_ref, mult_ref, misfit_ref, damp_ref, new[f], f, b, c, width)
                         total = total + resid * resid
-                        after = mult + relaxation * resid
-                        mult_out[f, c, at(b), :] = after
-                        after = mask * after
-                    where = BACK * k
-                    if c == width - 1:
-                        side_s[1, where + NEAR[f]] = after
-                    if c == width - 2 and f != V:
-                        side_s[1, where + FAR[f]] = after
-                    if c == 0:
-                        side_s[0, where + NEAR[f]] = after
-                    if c == 1 and f != V:
-                        side_s[0, where + FAR[f]] = after
+                        mult_out[f, i, at(b), :] = value
+                        after = mask * value
+                    plane = NEAR[f] if i in (0, 3) else FAR.get(f)
+                    if plane is not None:
+                        side_s[i // 2, BACK * k + plane] = after
         up = jnp.where(even, 1, 0)
         for p in range(BACK * subs):
             back_pair_ref[p, at(b), :] = side_s[up, p].astype(BF16)
@@ -363,9 +407,15 @@
     blocks_of(levels, body)
 
 
+def column_of(inner_ref, outer_ref, f, b, c, width):
+    if 2 <= c < width - 2:
+        return inner_ref[f, c - 2, at(b), :]
+    return outer_ref[f, c if c < 2 else c - width + 4, at(b), :]
+
+
 def adjoint_kernel(
     inc_ref, dens_ref, land_ref, pair_ref, link_ref, back_pair_ref, back_link_ref, mult_ref, misfit_ref, damp_ref,
-    fwd_ref, mnext_ref, edge_ref, inner_ref, prev_ref, spread_ref, sum_ref, seen_ref,
+    fwd_in, fwd_out, mnext_in, mnext_out, edge_ref, inner_ref, prev_in, prev_out, spread_ref, sum_ref, seen_ref,
     mult_out, grad_ref, fin_ref, x_s, y_s, acc_s,
 ):
     subs, fields, width, latitude = dens_ref.shape[0], mult_ref.shape[0], land_ref.shape[0], land_ref.shape[1]
@@ -397,13 +447,10 @@
                 mask = mask_at(c)
                 for f in range(fields):
                     if k == subs - 1:
-                        if 2 <= c < width - 2:
-                            got = inner_ref[f, c - 2, at(b), :]
-                        else:
-                            got = edge_ref[f, c if c < 2 else c - width + 4, at(b), :]
-                        value = keep * (got.astype(F32) + relaxation * fwd_ref[f, c, at(b), :])
+                        got = column_of(inner_ref, edge_ref, f, b, c, width).astype(F32)
+                        value = keep * (got + relaxation * column_of(fwd_in, fwd_out, f, b, c, width))
                     else:
-                        value = mnext_ref[f, c, at(b), :]
+                        value = column_of(mnext_in, mnext_out, f, b, c, width)
                     x_s[f, c + 2] = mask * value
             for ref, (near, far) in ((back_pair_ref, pair_halo), (back_link_ref, link_halo)):
                 for f, p in NEAR.items():
@@ -442,12 +489,12 @@
                         resid = (
                             rows_of(misfit_ref, (f,), b, c, width)
                             - damp_ref[f, at(b), :] * mult
-                            - (rows_of(inc_ref, (0, f), b, c, width) - precede * prev_ref[f, c, at(b), :].astype(F32))
+                            - (rows_of(inc_ref, (0, f), b, c, width) - precede * column_of(prev_in, prev_out, f, b, c, width).astype(F32))
                         )
                         misfit_total = misfit_total + resid * resid
                         value = mult + relaxation * resid
                     else:
-                        value = mnext_ref[f, c, at(b), :]
+                        value = column_of(mnext_in, mnext_out, f, b, c, width)
                     spot = pl.ds(b * (LB * width) + c, LB, stride=width)
                     mult_out[k, f, pl.ds(c, LB, stride=width), :] = value
                     grad = value - new[f]
@@ -522,7 +569,7 @@
     teams, tiles = lax.axis_size("tm"), lax.axis_size("space")
     peers = teams * tiles
     share = subs * nobs // (128 * tiles)
-    assert tiles % 2 == 0 and fields == 5 and trajectory.shape[1] == 2 and subs == 2 and levels % LB == 0 and width >= 4
+    assert tiles % 2 == 0 and fields == 5 and trajectory.shape[1] == 2 and subs == 2 and levels % LB == 0 and width >= 6
     assert latitude == 128 and (width * tiles) & (width * tiles - 1) == 0 and nobs % 512 == 0
     assert share * 128 * tiles == subs * nobs and (2 * levels * width) % 32 == 0
     rows = levels * width
@@ -579,7 +626,7 @@
             ((subs, 2, 2, width, levels, latitude), F32), (one, F32), (one, F32),
         ],
         [
-            pltpu.VMEM((2 * rows, 512), BF16), scr(2 * rows, 2 * latitude), scr(2, LB * width, latitude),
+            pltpu.VMEM((2 * rows, nobs), BF16), pltpu.VMEM((2 * latitude, nobs), BF16), scr(2, LB * width, latitude),
             pltpu.SemaphoreType.DMA((2,)),
         ],
         inc, cells, sen_m, sen_i, sen_e, traj, mult, mis,
@@ -588,27 +635,32 @@
     spread = spread.reshape(subs, 2, rows, latitude)
     seen_in = fast(lax.all_to_all(seen, "space", 0, 0))
 
-    column = (fields, width, levels, latitude)
+    outside, within_it = (fields, 4, levels, latitude), (fields, width - 4, levels, latitude)
     behind = (subs * BACK, levels, latitude)
-    fwd, send, mnext, back_pair, back_link, sums = call(
-        forward_kernel,
-        [(column, F32), (column, BF16), (column, F32), (behind, BF16), (behind, BF16), ((LB, latitude), F32)],
-        [
-            scr(5, width + 4, LB, latitude), scr(6, width + 4, LB, latitude), scr(width + 4, LB, latitude),
-            scr(2, subs * BACK, LB, latitude),
-        ],
-        inc, density, land, pair_in, link_in, mult1, mis1, damp, edge_in, sensor_sum,
+    strip = lambda n: scr(n, width + 4, LB, latitude)
+    mid, fwd_in, send_in, mnext_in, sums = call(
+        interior_kernel,
+        [((subs, 6, 4, levels, latitude), F32), (within_it, F32), (within_it, BF16), (within_it, F32), ((LB, latitude), F32)],
+        [strip(5), strip(6), scr(width + 4, LB, latitude)],
+        inc, density, land, mult1, mis1, damp, sensor_sum,
+    )
+    prev_in = fast(shifted(send_in, "tm", 1))
+    fwd_out, send_out, mnext_out, back_pair, back_link, sums = call(
+        edge_kernel,
+        [(outside, F32), (outside, BF16), (outside, F32), (behind, BF16), (behind, BF16), ((LB, latitude), F32)],
+        [strip(5), strip(6), scr(width + 4, LB, latitude), scr(2, subs * BACK, LB, latitude)],
+        inc, density, land, pair_in, link_in, mult1, mis1, damp, edge_in, mid, sums,
     )
     back_link_in = fast(swapped(back_link, "space", False))
     back_pair_in = fast(swapped(back_pair, "space", True))
-    prev = fast(shifted(send, "tm", 1))
+    prev_out = fast(shifted(send_out, "tm", 1))
 
     block = pl.BlockSpec((subs, fields, LB * width, latitude), lambda i: (0, 0, i, 0))
     mult_next, gradient, final = pl.pallas_call(
         adjoint_kernel,
         name="adjoint",
         grid=(levels // LB,),
-        in_specs=[vmem] * 18,
+        in_specs=[vmem] * 21,
         out_specs=[block, vmem, vmem],
         out_shape=[
             jax.ShapeDtypeStruct(native_shape, F32),
@@ -619,7 +671,7 @@
         compiler_params=limit,
     )(
         inc, density, land, pair_in, link_in, back_pair_in, back_link_in, mult0, mis0, damp,
-        fwd, mnext, edge_in, inner_in, prev, spread, sums, seen_in,
+        fwd_in, fwd_out, mnext_in, mnext_out, edge_in, inner_in, prev_in, prev_out, spread, sums, seen_in,
     )
     final = fast(lax.all_to_all(final, ("tm", "space"), 0, 0))
 

time: 57.3 us -> 50.7 us (0.88)
  waiting for transfers between devices: 3.12 us -> 0.02 us
  starting transfers between devices: 13.5 us -> 11.6 us
  blocking collectives: 21.3 us -> 20 us
    all_to_all x1, blocking collectives: 12.3 us -> 9.09 us  [within(): final = fast(lax.all_to_all(final, ('tm', 'space'), 0, 0))]
    ppermute x3 -> x4, waiting for transfers between devices: 3.11 us -> 0.01 us  [shifted(): lax.ppermute(shard, axis, [(i, (i + by) % peers) for i in range(peers)])]
    ppermute x4, starting transfers between devices: 9.93 us -> 7.45 us  [swapped(): lax.ppermute(shard, axis, [(i, (i + (1 if i % 2 == ahead else -1)) % peer...]
    all_to_all x1, blocking collectives: 9.06 us -> 10.9 us  [within(): seen_in = fast(lax.all_to_all(seen, 'space', 0, 0))]
    ppermute x3 -> x4, starting transfers between devices: 3.58 us -> 4.18 us  [shifted(): lax.ppermute(shard, axis, [(i, (i + by) % peers) for i in range(peers)])]
    pallas_call x3 -> x4, Pallas kernels: 11.7 us -> 11.4 us  [call(): pl.pallas_call(kernel, in_specs=specs or [vmem] * len(args), out_specs=[v...]
  transfers between devices with their start and end apart: 7 -> 8, of which waited for: 1 -> 0; matrix products, arithmetic and copies ran while one was open for 0% -> 0% of each run, Pallas kernels for 9% -> 16%
where the time goes in v4:
time: 50.7 us; the launch traced here: 50.5 us
  blocking collectives  20 us (39%)
  Pallas kernels  18.1 us (36%)
  starting transfers between devices  11.6 us (23%)
  between operations  0.73 us (1%)
    pallas_call x4, Pallas kernels, call(): pl.pallas_call(kernel, in_specs=specs or [vmem] * len(args), out_specs=[v...  11.4 us
    all_to_all x1, blocking collectives, within(): seen_in = fast(lax.all_to_all(seen, 'space', 0, 0))  10.9 us
    all_to_all x1, blocking collectives, within(): final = fast(lax.all_to_all(final, ('tm', 'space'), 0, 0))  9.09 us
    ppermute x4, starting transfers between devices, swapped(): lax.ppermute(shard, axis, [(i, (i + (1 if i % 2 == ahead else -1)) % peer...  7.45 us
    pallas_call x1, Pallas kernels, within(): pl.pallas_call(adjoint_kernel, name='adjoint', grid=(levels // LB,), in_s...  4.67 us
    ppermute x4, starting transfers between devices, shifted(): lax.ppermute(shard, axis, [(i, (i + by) % peers) for i in range(peers)])  4.18 us
    pallas_call x1, Pallas kernels, within(): pl.pallas_call(lambda *refs: step_kernel(*refs), name='step', grid=(steps...  2.05 us
  transfers between devices with their start and end apart: 8, of which 0 were waited for; matrix products, arithmetic and copies ran while one was open for 0% of the time, Pallas kernels for 16%

profile of v4, /device:TPU:0, one launch (start us, length us, event | category | flops | bytes accessed | tf_op | source)
XLA Modules:
  0.0 50.5 jit_solution(3833817398439384692)
XLA Ops:
  0.6 0.0 copy-start
  0.6 0.0 copy-start.1
  0.7 0.0 copy-start.2
  0.7 0.0 copy-start.3
  0.7 3.4 %shard_map.121 = (f32[2,5,384,128]{3,2,1,0:T(8,128)S(1)}, bf16[2,2,2,384,128]{4,3,2,1,0:T(8,128)(2,1)S(1)}, f32[5,384,128]{2,1,0:T(8,128)S(1)}, f32[5,384,128]{2...) custom-call(f32[5,48]{1,0:T(8,128)} %error_hbm.1, ...), custom_call_target="tpu_custom_call" | custom-call | tf_op jit(solution)/shard_map/pallas_call | solution.py:590
  4.1 0.6 %collective-permute-start = (bf16[27,48,128]{2,1,0:T(8,128)(2,1)S(1)}, bf16[27,48,128]{2,1,0:T(8,128)(2,1)S(1)}, u32[]{:S(2)}, u32[]{:S(2)}) collective-permute-start(bf16[27,48,128]{2,1,0:T(8,128)(2,1)S(1)} %get-tuple-element.39), channel_id=1, source_target_pairs={{0,1},{1,0},{2,3},{3,2},{4,5},{5,4},{6,7},{7,6},{8,9},{9,8},{10,11... | collective-permute-start | bytes 995336 | tf_op jit(solution)/shard_map/ppermute | solution.py:560
  4.6 5.7 %collective-permute-start.1 = (bf16[27,48,128]{2,1,0:T(8,128)(2,1)S(1)}, bf16[27,48,128]{2,1,0:T(8,128)(2,1)S(1)}, u32[]{:S(2)}, u32[]{:S(2)}) collective-permute-start(bf16[27,48,128]{2,1,0:T(8,128)(2,1)S(1)} %get-tuple-element.40), channel_id=1, source_target_pairs={{0,15},{1,2},{2,1},{3,4},{4,3},{5,6},{6,5},{7,8},{8,7},{9,10},{10,... | collective-permute-start | bytes 995336 | tf_op jit(solution)/shard_map/ppermute | solution.py:560
  10.3 1.5 %collective-permute-start.2 = (bf16[5,4,48,128]{3,2,1,0:T(8,128)(2,1)S(1)}, bf16[5,4,48,128]{3,2,1,0:T(8,128)(2,1)S(1)}, u32[]{:S(2)}, u32[]{:S(2)}) collective-permute-start(bf16[5,4,48,128]{3,2,1,0:T(8,128)(2,1)S(1)} %get-tuple-element.44), channel_id=1, source_target_pairs={{0,16},{16,0},{1,17},{17,1},{2,18},{18,2},{3,19},{19,3},{4,20},{20... | collective-permute-start | bytes 737288 | tf_op jit(solution)/shard_map/ppermute | solution.py:554
  11.8 0.5 %collective-permute-start.5 = (bf16[5,4,48,128]{3,2,1,0:T(8,128)(2,1)S(1)}, bf16[5,4,48,128]{3,2,1,0:T(8,128)(2,1)S(1)}, u32[]{:S(2)}, u32[]{:S(2)}) collective-permute-start(bf16[5,4,48,128]{3,2,1,0:T(8,128)(2,1)S(1)} %get-tuple-element.56), channel_id=1, source_target_pairs={{0,16},{16,0},{1,17},{17,1},{2,18},{18,2},{3,19},{19,3},{4,20},{20... | collective-permute-start | bytes 737288 | tf_op jit(solution)/shard_map/ppermute | solution.py:554
  12.3 0.0 copy-done
  12.3 0.0 copy-done.1
  12.3 0.0 copy-done.2
  12.3 0.0 copy-done.3
  12.3 4.5 %shard_map.122 = (f32[16,2,128]{2,1,0:T(2,128)S(1)}, f32[2,768,128]{2,1,0:T(8,128)S(1)}, f32[1,512]{1,0:T(1,128)S(1)}, f32[2,2,2,8,48,128]{5,4,3,2,1,0:T(8,128)S...) custom-call(f32[2,5,384,128]{3,2,1,0:T(8,128)S(1)} %get-tuple-element.35.refs_0_.inc_ref.refs_1_, ...), custom_call_target="tpu_custom_call" | custom-call | tf_op jit(solution)/shard_map/pallas_call | solution.py:590
  16.9 1.7 %shard_map.123 = (f32[2,6,4,48,128]{4,3,2,1,0:T(8,128)S(1)}, f32[5,4,48,128]{3,2,1,0:T(8,128)S(1)}, bf16[5,4,48,128]{3,2,1,0:T(8,128)(2,1)S(1)}, f32[5,4,48,128]{3,2,1,0:T(8,128)S(1)}, f32[16,128]{1,0:T(8,128)S(1)}) custom-call(f32[2,5,384,128]{3,2,1,0:T(8,128)S(1)} %get-tuple-element.35.refs_0_.inc_ref.refs_1_, ...), custom_call_target="tpu_custom_call" | custom-call | tf_op jit(solution)/shard_map/pallas_call | solution.py:590
  18.6 1.6 %collective-permute-start.6 = (bf16[5,4,48,128]{3,2,1,0:T(8,128)(2,1)S(1)}, bf16[5,4,48,128]{3,2,1,0:T(8,128)(2,1)S(1)}, u32[]{:S(2)}, u32[]{:S(2)}) collective-permute-start(bf16[5,4,48,128]{3,2,1,0:T(8,128)(2,1)S(1)} %get-tuple-element.57), channel_id=1, source_target_pairs={{0,16},{16,0},{1,17},{17,1},{2,18},{18,2},{3,19},{19,3},{4,20},{20... | collective-permute-start | bytes 737288 | tf_op jit(solution)/shard_map/ppermute | solution.py:554
  20.2 0.0 collective-permute-done.2.edge_ref
  20.2 0.0 collective-permute-done.pair_ref
  20.2 0.0 collective-permute-done.1.link_ref
  20.2 1.7 %shard_map.124 = (f32[5,4,48,128]{3,2,1,0:T(8,128)S(1)}, bf16[5,4,48,128]{3,2,1,0:T(8,128)(2,1)S(1)}, f32[5,4,48,128]{3,2,1,0:T(8,128)S(1)}, bf16[18,48,128]{2,1...) custom-call(f32[2,5,384,128]{3,2,1,0:T(8,128)S(1)} %get-tuple-element.35.refs_0_.inc_ref.refs_1_, ...), custom_call_target="tpu_custom_call" | custom-call | tf_op jit(solution)/shard_map/pallas_call | solution.py:590
  21.9 0.6 %collective-permute-start.7 = (bf16[5,4,48,128]{3,2,1,0:T(8,128)(2,1)S(1)}, bf16[5,4,48,128]{3,2,1,0:T(8,128)(2,1)S(1)}, u32[]{:S(2)}, u32[]{:S(2)}) collective-permute-start(bf16[5,4,48,128]{3,2,1,0:T(8,128)(2,1)S(1)} %get-tuple-element.58), channel_id=1, source_target_pairs={{0,16},{16,0},{1,17},{17,1},{2,18},{18,2},{3,19},{19,3},{4,20},{20... | collective-permute-start | bytes 737288 | tf_op jit(solution)/shard_map/ppermute | solution.py:554
  22.5 0.0 collective-permute-start.3
  22.5 1.2 %collective-permute-start.4 = (bf16[18,48,128]{2,1,0:T(8,128)(2,1)S(1)}, bf16[18,48,128]{2,1,0:T(8,128)(2,1)S(1)}, u32[]{:S(2)}, u32[]{:S(2)}) collective-permute-start(bf16[18,48,128]{2,1,0:T(8,128)(2,1)S(1)} %get-tuple-element.49), channel_id=1, source_target_pairs={{0,15},{1,2},{2,1},{3,4},{4,3},{5,6},{6,5},{7,8},{8,7},{9,10},{10,... | collective-permute-start | bytes 663560 | tf_op jit(solution)/shard_map/ppermute | solution.py:560
  23.8 10.9 %all_to_all.10.seen_ref = f32[16,2,128]{2,1,0:T(2,128)S(1)} all-to-all(f32[16,2,128]{2,1,0:T(2,128)S(1)} %get-tuple-element.61), channel_id=1, replica_groups=mesh['tm'=2,'space'=16] {'space'}, dimensions={0} | all-to-all | bytes 32768 | tf_op jit(solution)/shard_map/all_to_all | solution.py:636
  34.7 0.0 collective-permute-done.5.inner_ref
  34.7 0.0 collective-permute-done.6.prev_in
  34.7 0.0 collective-permute-done.3.back_pair_ref
  34.7 0.0 collective-permute-done.4.back_link_ref
  34.7 0.0 collective-permute-done.7.prev_out
  34.7 4.7 %adjoint.1 = (f32[2,5,384,128]{3,2,1,0:T(8,128)}, f32[2,5,384,128]{3,2,1,0:T(8,128)S(1)}, f32[32,3,128]{2,1,0:T(4,128)S(1)}) custom-call(f32[2,5,384,128]{3,2,1,0:T(8,128)S(1)} %get-tuple-element.35.refs_0_.inc_ref.refs_1_, f32[2,2,2,8,48,128]{5,4,3,2,1,0:T(8,128)S(1)} %get-tuple-element.37.dens_ref, s32[8,128]{1,0:T(8,128)S(1)} %get-tuple-element.38.land_ref, ...), custom_call_target="tpu_custom_call" | custom-call | tf_op jit(solution)/shard_map/adjoint/pallas_call | solution.py:659
  39.4 9.1 %all_to_all.11.refs_0_ = f32[32,3,128]{2,1,0:T(4,128)S(1)} all-to-all(f32[32,3,128]{2,1,0:T(4,128)S(1)} %get-tuple-element.62), channel_id=1, replica_groups=mesh['tm'=2,'space'=16] {'tm','space'}, dimensions={0} | all-to-all | bytes 98304 | tf_op jit(solution)/shard_map/all_to_all | solution.py:676
  48.5 2.1 %step.1 = (f32[2,5,384,128]{3,2,1,0:T(8,128)}, f32[2,2048]{1,0:T(2,128)}) custom-call(f32[32,3,128]{2,1,0:T(4,128)S(1)} %all_to_all.11.refs_0_, f32[2,5,384,128]{3,2,1,0:T(8,128)S(1)} %get-tuple-element.35.refs_0_.inc_ref.refs_1_, f32[2,5,384,128]{3,2,1,0:T(8,128)S(1)} %get-tuple-element.63.refs_2_, f32[2,2048]{1,0:T(2,128)S(1)} %copy-done, ...), custom_call_target="tpu_custom_call" | custom-call | tf_op jit(solution)/shard_map/step/pallas_call | solution.py:680
Async XLA Ops:
  0.6 11.7 %copy-start = (f32[2,2048]{1,0:T(2,128)S(1)}, f32[2,2048]{1,0:T(2,128)}, u32[]{:S(2)}) copy-start(f32[2,2048]{1,0:T(2,128)} %refs_3_.3) | copy-start | bytes 49156
  0.6 11.7 %copy-start.1 = (f32[2,2048]{1,0:T(2,128)S(1)}, f32[2,2048]{1,0:T(2,128)}, u32[]{:S(2)}) copy-start(f32[2,2048]{1,0:T(2,128)} %refs_4_.3) | copy-start | bytes 49156
  0.7 11.7 %copy-start.2 = (f32[2,2048]{1,0:T(2,128)S(1)}, f32[2,2048]{1,0:T(2,128)}, u32[]{:S(2)}) copy-start(f32[2,2048]{1,0:T(2,128)} %refs_5_.1) | copy-start | bytes 49156
  0.7 11.7 %copy-start.3 = (s32[2,2048]{1,0:T(2,128)S(1)}, s32[2,2048]{1,0:T(2,128)}, u32[]{:S(2)}) copy-start(s32[2,2048]{1,0:T(2,128)} %refs_1_.1) | copy-start | bytes 49156
  4.1 16.1 %collective-permute-start = (bf16[27,48,128]{2,1,0:T(8,128)(2,1)S(1)}, bf16[27,48,128]{2,1,0:T(8,128)(2,1)S(1)}, u32[]{:S(2)}, u32[]{:S(2)}) collective-permute-start(bf16[27,48,128]{2,1,0:T(8,128)(2,1)S(1)} %get-tuple-element.39), channel_id=1, source_target_pairs={{0,1},{1,0},{2,3},{3,2},{4,5},{5,4},{6,7},{7,6},{8,9},{9,8},{10,11... | collective-permute-start | bytes 995336 | tf_op jit(solution)/shard_map/ppermute | solution.py:560
  4.6 15.5 %collective-permute-start.1 = (bf16[27,48,128]{2,1,0:T(8,128)(2,1)S(1)}, bf16[27,48,128]{2,1,0:T(8,128)(2,1)S(1)}, u32[]{:S(2)}, u32[]{:S(2)}) collective-permute-start(bf16[27,48,128]{2,1,0:T(8,128)(2,1)S(1)} %get-tuple-element.40), channel_id=1, source_target_pairs={{0,15},{1,2},{2,1},{3,4},{4,3},{5,6},{6,5},{7,8},{8,7},{9,10},{10,... | collective-permute-start | bytes 995336 | tf_op jit(solution)/shard_map/ppermute | solution.py:560
  10.3 9.9 %collective-permute-start.2 = (bf16[5,4,48,128]{3,2,1,0:T(8,128)(2,1)S(1)}, bf16[5,4,48,128]{3,2,1,0:T(8,128)(2,1)S(1)}, u32[]{:S(2)}, u32[]{:S(2)}) collective-permute-start(bf16[5,4,48,128]{3,2,1,0:T(8,128)(2,1)S(1)} %get-tuple-element.44), channel_id=1, source_target_pairs={{0,16},{16,0},{1,17},{17,1},{2,18},{18,2},{3,19},{19,3},{4,20},{20... | collective-permute-start | bytes 737288 | tf_op jit(solution)/shard_map/ppermute | solution.py:554
  11.8 22.9 %collective-permute-start.5 = (bf16[5,4,48,128]{3,2,1,0:T(8,128)(2,1)S(1)}, bf16[5,4,48,128]{3,2,1,0:T(8,128)(2,1)S(1)}, u32[]{:S(2)}, u32[]{:S(2)}) collective-permute-start(bf16[5,4,48,128]{3,2,1,0:T(8,128)(2,1)S(1)} %get-tuple-element.56), channel_id=1, source_target_pairs={{0,16},{16,0},{1,17},{17,1},{2,18},{18,2},{3,19},{19,3},{4,20},{20... | collective-permute-start | bytes 737288 | tf_op jit(solution)/shard_map/ppermute | solution.py:554
  18.6 16.0 %collective-permute-start.6 = (bf16[5,4,48,128]{3,2,1,0:T(8,128)(2,1)S(1)}, bf16[5,4,48,128]{3,2,1,0:T(8,128)(2,1)S(1)}, u32[]{:S(2)}, u32[]{:S(2)}) collective-permute-start(bf16[5,4,48,128]{3,2,1,0:T(8,128)(2,1)S(1)} %get-tuple-element.57), channel_id=1, source_target_pairs={{0,16},{16,0},{1,17},{17,1},{2,18},{18,2},{3,19},{19,3},{4,20},{20... | collective-permute-start | bytes 737288 | tf_op jit(solution)/shard_map/ppermute | solution.py:554
  21.9 12.7 %collective-permute-start.7 = (bf16[5,4,48,128]{3,2,1,0:T(8,128)(2,1)S(1)}, bf16[5,4,48,128]{3,2,1,0:T(8,128)(2,1)S(1)}, u32[]{:S(2)}, u32[]{:S(2)}) collective-permute-start(bf16[5,4,48,128]{3,2,1,0:T(8,128)(2,1)S(1)} %get-tuple-element.58), channel_id=1, source_target_pairs={{0,16},{16,0},{1,17},{17,1},{2,18},{18,2},{3,19},{19,3},{4,20},{20... | collective-permute-start | bytes 737288 | tf_op jit(solution)/shard_map/ppermute | solution.py:554
  22.5 12.1 %collective-permute-start.3 = (bf16[18,48,128]{2,1,0:T(8,128)(2,1)S(1)}, bf16[18,48,128]{2,1,0:T(8,128)(2,1)S(1)}, u32[]{:S(2)}, u32[]{:S(2)}) collective-permute-start(bf16[18,48,128]{2,1,0:T(8,128)(2,1)S(1)} %get-tuple-element.48), channel_id=1, source_target_pairs={{0,1},{1,0},{2,3},{3,2},{4,5},{5,4},{6,7},{7,6},{8,9},{9,8},{10,11... | collective-permute-start | bytes 663560 | tf_op jit(solution)/shard_map/ppermute | solution.py:560
  22.5 12.1 %collective-permute-start.4 = (bf16[18,48,128]{2,1,0:T(8,128)(2,1)S(1)}, bf16[18,48,128]{2,1,0:T(8,128)(2,1)S(1)}, u32[]{:S(2)}, u32[]{:S(2)}) collective-permute-start(bf16[18,48,128]{2,1,0:T(8,128)(2,1)S(1)} %get-tuple-element.49), channel_id=1, source_target_pairs={{0,15},{1,2},{2,1},{3,4},{4,3},{5,6},{6,5},{7,8},{8,7},{9,10},{10,... | collective-permute-start | bytes 663560 | tf_op jit(solution)/shard_map/ppermute | solution.py:560
